TPU v7x, 256 devices: a whole 4x4x8 slice. The times are simulated.
256 devices in a mesh: grp: 32 (over x, z_hi, y), ep: 8 (over z_lo, core).
Axes of the slice: x: 4, y: 4, z: 8 (z_hi: 2, z_lo: 4; z = z_hi * 4 + z_lo), core: 2. Of those that a mesh axis runs over, the one named last changes fastest.
Arguments:
- queries: bfloat16 [1024, 2304], P('grp'), may hold values from -36 to 36, as said below
- residual: bfloat16 [1024, 2304], P(('grp', 'ep')), may hold values from -20 to 20
- gain: bfloat16 [2304], replicated, may hold values from 0.5 to 1.5
- key_pages: bfloat16 [2048, 128, 2304], P(('grp', 'ep')), may hold values from -6 to 6
- value_pages: bfloat16 [2048, 128, 2304], P(('grp', 'ep')), may hold values from -6 to 6
- page_table: int32 [1024, 32], P('grp'), may hold values from -1 to 63, as said below
- lengths: int32 [1024], P('grp'), may hold values from 1 to 4096, as said below
- split_flag: int32 [1024], P('grp'), may hold values from 0 to 1, as said below
- routes: int32 [1024, 2], P(('grp', 'ep')), may hold values from 0 to 7, all different within a row; in each aligned block of 4 rows (0 to 3, 4 to 7, ...) at most 2 rows name the same one
- gates: bfloat16 [1024, 2], P(('grp', 'ep')), may hold values from 0.19921875 to 1
- w_gate: bfloat16 [8, 2304, 5760], P('ep', None, 'grp'), may hold values from -0.125 to 0.125
- w_up: bfloat16 [8, 2304, 5760], P('ep', None, 'grp'), may hold values from -0.125 to 0.125
- w_down: bfloat16 [8, 5760, 2304], P('ep', 'grp'), may hold values from -0.078125 to 0.078125
Outputs:
- update: bfloat16 [1024, 2304], P(('grp', 'ep'))
Inputs may be any that keep to these rules, and one draw needn't show every extreme that they name: `page_table`: entries j with j * 128 < lengths[r] are pages of the row's group; no page is named twice within a group; the other entries are -1. `lengths`: A split request's first half, in the even group of its pair, is always 32 * 128 tokens; other rows are no longer. `split_flag`: in every group exactly one row is 1, at the same slot in both groups of each pair 2i, 2i + 1. `routes`: within the rows of one device no expert is named more than 2 times. `queries`: the two rows of a split request hold the same query.
All inputs are finite; a program needn't handle non-finite values.
Results may differ from a plain program's by a relative error of at most 0.015.
Values may be sent and summed in bfloat16 or wider, within the bound.
No kernel may reach another device: no remote copies, remote signals or barrier semaphores. Data moves between devices by JAX's collectives and lax.ppermute only.
A program may use at most 192 MiB of HBM per device.

v0:
```python
import jax
import jax.numpy as jnp
from jax import lax
from jax.sharding import PartitionSpec as P

HEAD_DIM = 64
PAGE = 128


NEG_FILL = -1e30
NORM_EPS = 1e-06


def joined_2(array, axis, combine):
    everything = jax.tree.map(lambda part: lax.all_gather(part, axis), array)
    leading = jax.tree.map(lambda part: part[0], everything)

    def turn(k, so_far):
        return combine(so_far, jax.tree.map(lambda part: part[k], everything))

    return lax.fori_loop(1, lax.axis_size(axis), turn, leading)


def from_partner(array, axis, bit):
    return lax.ppermute(array, axis, [(i, i ^ 1 << bit) for i in range(lax.axis_size(axis))])


def merge_parts(first_part, second_part):
    maxima_a, totals_a, weighted_a = first_part
    maxima_b, totals_b, weighted_b = second_part
    highest = jnp.maximum(maxima_a, maxima_b)
    factor_a = jnp.exp(maxima_a - highest)
    factor_b = jnp.exp(maxima_b - highest)
    head_count = maxima_a.shape[-1]
    shaped = weighted_a.shape
    wide = shaped[:-1] + (head_count, shaped[-1] // head_count)
    weighted = (
        weighted_a.reshape(wide) * factor_a[..., None]
        + weighted_b.reshape(wide) * factor_b[..., None]
    )
    return (highest, totals_a * factor_a + totals_b * factor_b, weighted.reshape(shaped))


def page_partials(group_q, page_rows, row_lengths, key_rows, value_rows, first_page):
    page_count = key_rows.shape[0]
    slot_count = group_q.shape[0]
    head_count = group_q.shape[1] // HEAD_DIM
    page_ids = first_page + jnp.arange(page_count, dtype=jnp.int32)
    table_steps = jnp.arange(page_rows.shape[1], dtype=jnp.int32)
    live_step = (table_steps * PAGE)[None, :] < row_lengths[:, None]
    matches = (page_rows[:, :, None] == page_ids[None, None, :]) & live_step[:, :, None]
    owned_page = jnp.any(matches, axis=1)
    where_at = jnp.sum(jnp.where(matches, table_steps[None, :, None], 0), axis=1)
    offsets = jnp.arange(PAGE, dtype=jnp.int32)
    token_pos = where_at[:, :, None] * PAGE + offsets[None, None, :]
    visible = (owned_page[:, :, None] & (token_pos < row_lengths[:, None, None])).reshape(
        slot_count, page_count * PAGE
    )
    query_heads = group_q.reshape(slot_count, head_count, HEAD_DIM)
    key_heads = key_rows.reshape(page_count * PAGE, head_count, HEAD_DIM)
    value_heads = value_rows.reshape(page_count * PAGE, head_count, HEAD_DIM)
    scores = jnp.einsum(
        "shd,khd->hsk", query_heads, key_heads, preferred_element_type=jnp.float32
    ) * HEAD_DIM ** (-0.5)
    scores = jnp.where(visible[None], scores, NEG_FILL)
    maxima = jnp.max(scores, axis=2)
    exp_terms = jnp.where(visible[None], jnp.exp(scores - maxima[..., None]), 0.0)
    totals = jnp.sum(exp_terms, axis=2)
    weights = exp_terms.astype(jnp.bfloat16)
    weighted = jnp.einsum("hsk,khd->shd", weights, value_heads, preferred_element_type=jnp.float32)
    return (maxima.T, totals.T, weighted.reshape(slot_count, head_count * HEAD_DIM))


def on_device(
    queries,
    residual,
    gain,
    key_pages,
    value_pages,
    page_table,
    lengths,
    split_flag,
    routes,
    gates,
    w_gate,
    w_up,
    w_down,
):
    req_dev = residual.shape[0]
    ep_size = lax.axis_size("ep")
    my_ep = lax.axis_index("ep")
    first_page = my_ep * key_pages.shape[0]
    maxima, totals, weighted = page_partials(
        queries, page_table, lengths, key_pages, value_pages, first_page
    )
    row_start = my_ep * req_dev
    merged = joined_2((maxima, totals, weighted), "ep", merge_parts)
    maxima = lax.dynamic_slice_in_dim(merged[0], row_start, req_dev, 0)
    totals = lax.dynamic_slice_in_dim(merged[1], row_start, req_dev, 0)
    weighted = lax.dynamic_slice_in_dim(merged[2], row_start, req_dev, 0)
    own_split = (lax.dynamic_slice_in_dim(split_flag, row_start, req_dev, 0) == 1)[:, None]
    partner = from_partner((maxima, totals, weighted), "grp", 0)
    joined = merge_parts((maxima, totals, weighted), partner)
    totals = jnp.where(own_split, joined[1], totals)
    weighted = jnp.where(own_split, joined[2], weighted)
    head_count = totals.shape[1]
    attn = (
        (weighted.reshape(req_dev, head_count, -1) / totals[..., None])
        .reshape(req_dev, -1)
        .astype(jnp.bfloat16)
    )
    stream = residual.astype(jnp.float32) + attn.astype(jnp.float32)
    normed = (
        stream
        * lax.rsqrt(jnp.mean(stream * stream, axis=-1, keepdims=True) + NORM_EPS)
        * gain.astype(jnp.float32)
    ).astype(jnp.bfloat16)
    capacity = max(2, (2 * req_dev + ep_size - 1) // ep_size)
    slot_count = ep_size * capacity
    chosen = routes.reshape(-1)
    one_hot = (chosen[:, None] == jnp.arange(ep_size, dtype=jnp.int32)[None, :]).astype(jnp.int32)
    ranking = jnp.sum((jnp.cumsum(one_hot, axis=0) - one_hot) * one_hot, axis=1)
    slot_of = chosen * capacity + ranking
    slot_ids = jnp.arange(slot_count, dtype=jnp.int32)
    placing = (slot_ids[:, None] == slot_of[None, :]).astype(jnp.bfloat16)
    doubled = jnp.repeat(normed, 2, axis=0)
    outgoing = (
        jnp.dot(placing, doubled, preferred_element_type=jnp.float32)
        .astype(jnp.bfloat16)
        .reshape(ep_size, capacity, -1)
    )
    arrived = lax.all_to_all(outgoing, "ep", split_axis=0, concat_axis=0, tiled=True).reshape(
        slot_count, -1
    )
    gate_matrix = w_gate[0]
    up_matrix = w_up[0]
    down_matrix = w_down[0]
    block_rows = lax.all_gather(arrived, "grp", axis=0, tiled=True)
    gate_part = jnp.dot(block_rows, gate_matrix, preferred_element_type=jnp.float32)
    up_part = jnp.dot(block_rows, up_matrix, preferred_element_type=jnp.float32)
    inner = (jax.nn.silu(gate_part) * up_part).astype(jnp.bfloat16)
    block_rows = inner
    summed = lax.psum_scatter(
        jnp.dot(block_rows, down_matrix, preferred_element_type=jnp.float32).astype(jnp.bfloat16),
        "grp",
        scatter_dimension=0,
        tiled=True,
    )
    results = summed.reshape(ep_size, capacity, -1)
    returned = lax.all_to_all(results, "ep", split_axis=0, concat_axis=0, tiled=True)
    picking = (slot_of[:, None] == slot_ids[None, :]).astype(jnp.float32) * gates.reshape(-1)[
        :, None
    ].astype(jnp.float32)
    blending = picking.reshape(req_dev, 2, slot_count).sum(axis=1).astype(jnp.bfloat16)
    mixture = jnp.dot(
        blending, returned.reshape(slot_count, -1), preferred_element_type=jnp.float32
    )
    return (attn.astype(jnp.float32) + mixture).astype(jnp.bfloat16)


def solution(mesh):
    in_specs = (
        P("grp", None),
        P(("grp", "ep"), None),
        P(),
        P(("grp", "ep"), None, None),
        P(("grp", "ep"), None, None),
        P("grp", None),
        P("grp"),
        P("grp"),
        P(("grp", "ep"), None),
        P(("grp", "ep"), None),
        P("ep", None, "grp"),
        P("ep", None, "grp"),
        P("ep", "grp", None),
    )
    out_specs = P(("grp", "ep"), None)
    return jax.shard_map(
        on_device, mesh=mesh, in_specs=in_specs, out_specs=out_specs, check_vma=False
    )
```

profile of v0, /device:TPU:16, one launch (start us, length us, event | category | flops | bytes accessed | tf_op | source)
XLA Modules:
  0.0 493.2 jit_solution(9139386518411092309)
XLA Ops:
  7.4 1.4 select_reduce_fusion
  8.8 1.4 fusion.33
  10.2 7.1 %copy.64 = bf16[8,128,2304]{1,0,2:T(8,128)(2,1)} copy(bf16[8,128,2304]{2,1,0:T(8,128)(2,1)} %param.18) | data formatting | bytes 9437184 | tf_op args[3]
  17.3 8.2 %reshape.186 = bf16[1024,36,64]{0,2,1:T(8,128)(2,1)} reshape(bf16[8,128,2304]{1,0,2:T(8,128)(2,1)} %copy.64) | data formatting | bytes 9437184 | tf_op jit(solution)/shard_map/reshape | solution.py:60
  25.8 7.0 %copy.68 = bf16[8,128,2304]{1,0,2:T(8,128)(2,1)} copy(bf16[8,128,2304]{2,1,0:T(8,128)(2,1)} %param.19) | data formatting | bytes 9437184 | tf_op args[4]
  32.8 8.2 %reshape.187 = bf16[1024,36,64]{0,2,1:T(8,128)(2,1)} reshape(bf16[8,128,2304]{1,0,2:T(8,128)(2,1)} %copy.68) | data formatting | bytes 9437184 | tf_op jit(solution)/shard_map/reshape | solution.py:61
  41.3 3.6 fusion.3
  45.0 1.4 fusion.14
  48.4 3.7 fusion.6
  52.2 14.9 %all-gather.1 = f32[256,36]{1,0:T(8,128)S(1)} all-gather(f32[32,36]{1,0:T(8,128)S(1)} %copy.67), channel_id=3, replica_groups=mesh['grp'=32,'ep'=8] {'ep'}, dimensions={0}, use_global_device_ids=true | all-gather | bytes 41472 | tf_op jit(solution)/shard_map/all_gather | solution.py:15
  67.2 14.8 %all-gather = f32[256,36]{1,0:T(8,128)S(1)} all-gather(f32[32,36]{1,0:T(8,128)S(1)} %copy.66), channel_id=2, replica_groups=mesh['grp'=32,'ep'=8] {'ep'}, dimensions={0}, use_global_device_ids=true | all-gather | bytes 41472 | tf_op jit(solution)/shard_map/all_gather | solution.py:15
  82.5 8.9 %all-gather.5.cloned.1.call-done = f32[8,32,2304]{2,1,0:T(8,128)} async-done(((f32[1,32,2304]{2,1,0:T(8,128)}), f32[8,32,2304]{2,1,0:T(8,128)}) %all-gather.5.cloned.1.call-update) | async-done | bytes 2359312 | tf_op jit(solution)/shard_map/all_gather | solution.py:15
  91.5 1.0 slice_bitcast_fusion
  92.5 13.8 %while.19 = (s32[]{:T(128)}, f32[32,36]{1,0:T(8,128)S(1)}, f32[32,36]{1,0:T(8,128)S(1)}, f32[32,2304]{1,0:T(8,128)S(1)}, f32[8,32,36]{2,1,0:T(8,128)S(1)}, /*ind...) while((s32[]{:T(128)}, f32[32,36]{1,0:T(8,128)S(1)}, ...), condition=%wide.region_5.6_spmd, body=%wide.region_4.5_spmd.sunk | while | flops 228101 | bytes 3290263 | solution.py:21
  93.3 1.1 fusion.58
  95.3 1.1 fusion.58
  97.3 1.1 fusion.58
  99.3 1.1 fusion.58
  101.3 1.1 fusion.58
  103.2 1.1 fusion.58
  105.2 1.1 fusion.58
  106.3 1.3 collective-permute-start
  108.5 1.3 collective-permute-start.1
  110.0 1.2 collective-permute-done.2
  113.1 8.4 %all_to_all.10 = bf16[8,2,2304]{2,1,0:T(2,128)(2,1)S(1)} all-to-all(bf16[8,2,2304]{2,1,0:T(2,128)(2,1)S(1)} %reshape.189), channel_id=1, replica_groups=mesh['grp'=32,'ep'=8] {'ep'}, dimensions={0} | all-to-all | bytes 147456 | tf_op jit(solution)/shard_map/all_to_all | solution.py:132
  122.2 92.1 %all-gather.7.cloned.1.call-done = bf16[512,2304]{1,0:T(8,128)(2,1)} async-done(((bf16[16,2304]{1,0:T(8,128)(2,1)}), bf16[512,2304]{1,0:T(8,128)(2,1)}) %all-gather.7.cloned.1.call-update) | async-done | bytes 2359312 | tf_op jit(solution)/shard_map/all_gather | solution.py:138
  214.3 2.8 fusion.21
  217.1 4.9 convolution_convert_fusion
  222.2 252.9 %reduce-scatter.2.cloned.1.call-done = bf16[16,2304]{1,0:T(8,128)(2,1)} async-done(((bf16[512,2304]{1,0:T(8,128)(2,1)}), bf16[16,2304]{1,0:T(8,128)(2,1)}) %reduce-scatter.2.cloned.1.call-update) | async-done | bytes 73744 | tf_op jit(solution)/shard_map/reduce_scatter | solution.py:143
  475.1 1.5 reshape.191
  476.6 3.4 all-to-all-start.1
  480.2 5.7 %all-to-all-done.1 = bf16[8,2,2304]{2,1,0:T(2,128)(2,1)S(1)} async-done(((bf16[8,2,2304]{2,1,0:T(2,128)(2,1)}), bf16[8,2,2304]{2,1,0:T(2,128)(2,1)S(1)}, u32[]{:S(2)}, u32[]{:S(2)}) %all-to-all-start.1) | async-done | bytes 73760 | tf_op jit(solution)/shard_map/all_to_all | solution.py:150
  (117 shorter events, 14.7 us)
Async XLA Ops:
  6.5 210.6 %copy-start = (bf16[1,180,2304]{2,1,0:T(8,128)(2,1)S(1)}, bf16[1,180,2304]{2,1,0:T(8,128)(2,1)}, u32[]{:S(2)}) copy-start(bf16[1,180,2304]{2,1,0:T(8,128)(2,1)} %param.27) | copy-start | bytes 2488324
  6.5 84.9 %all-gather.5.cloned.1.call-start = ((), (), s32[]{:S(2)}) async-start(), calls=%async_computation.3 | async-start | bytes 2654208 | tf_op jit(solution)/shard_map/all_gather | solution.py:15
  17.3 8.2 %copy-start.2 = (bf16[32,2304]{1,0:T(8,128)(2,1)S(1)}, bf16[32,2304]{1,0:T(8,128)(2,1)}, u32[]{:S(2)}) copy-start(bf16[32,2304]{1,0:T(8,128)(2,1)} %param.15) | copy-start | bytes 442372
  32.8 8.4 %copy-start.5 = (s32[32]{0:T(128)S(1)}, s32[32]{0:T(128)}, u32[]{:S(2)}) copy-start(s32[32]{0:T(128)} %param.21) | copy-start | bytes 388
  41.2 3.7 slice-start
  41.3 3.6 slice-start.1
  44.9 2.1 copy-start.1
  47.1 34.9 %copy-start.4 = (bf16[2304]{0:T(1024)(128)(2,1)S(1)}, bf16[2304]{0:T(1024)(128)(2,1)}, u32[]{:S(2)}) copy-start(bf16[2304]{0:T(1024)(128)(2,1)} %param.17) | copy-start | bytes 13828
  47.1 34.9 %copy-start.6 = (s32[4,2]{0,1:T(2,128)S(1)}, s32[4,2]{0,1:T(2,128)}, u32[]{:S(2)}) copy-start(s32[4,2]{0,1:T(2,128)} %param.23) | copy-start | bytes 100
  47.1 35.2 %copy-start.8 = (s32[32]{0:T(128)S(1)}, s32[32]{0:T(128)}, u32[]{:S(2)}) copy-start(s32[32]{0:T(128)} %param.22) | copy-start | bytes 388
  48.4 166.0 %all-gather.7.cloned.1.call-start = ((), (), s32[]{:S(2)}) async-start(), calls=%async_computation.4 | async-start | bytes 2433024 | tf_op jit(solution)/shard_map/all_gather | solution.py:138
  92.4 20.1 %copy-start.3 = (bf16[4,2304]{1,0:T(4,128)(2,1)S(1)}, bf16[4,2304]{1,0:T(4,128)(2,1)}, u32[]{:S(2)}) copy-start(bf16[4,2304]{1,0:T(4,128)(2,1)} %param.16) | copy-start | bytes 55300
  106.3 110.8 %copy-start.7 = (bf16[1,2304,180]{1,2,0:T(8,128)(2,1)S(1)}, bf16[1,2304,180]{1,2,0:T(8,128)(2,1)}, u32[]{:S(2)}) copy-start(bf16[1,2304,180]{1,2,0:T(8,128)(2,1)} %param.26) | copy-start | bytes 2488324
  106.3 3.7 collective-permute-start
  107.6 3.6 collective-permute-start.2
  108.5 4.0 collective-permute-start.1
  122.1 353.0 %reduce-scatter.2.cloned.1.call-start = ((), (), s32[]{:S(2)}) async-start(), calls=%async_computation.5 | async-start | bytes 2433024 | tf_op jit(solution)/shard_map/reduce_scatter | solution.py:143
  217.1 263.0 %copy-start.9 = (bf16[4,2]{0,1:T(2,128)(2,1)S(1)}, bf16[4,2]{0,1:T(2,128)(2,1)}, u32[]{:S(2)}) copy-start(bf16[4,2]{0,1:T(2,128)(2,1)} %param.24) | copy-start | bytes 52
  476.6 9.3 %all-to-all-start.1 = ((bf16[8,2,2304]{2,1,0:T(2,128)(2,1)}), bf16[8,2,2304]{2,1,0:T(2,128)(2,1)S(1)}, u32[]{:S(2)}, u32[]{:S(2)}) async-start(bf16[8,2,2304]{2,1,0:T(2,128)(2,1)} %reshape.191), calls=%async_computation.2 | async-start | bytes 147456 | tf_op jit(solution)/shard_map/all_to_all | solution.py:150
Sparse Core Ops, SparseCore 0:
  48.5 42.9 all-gather.4
  122.3 92.0 all-gather.6
  222.2 252.8 reduce-scatter.1
where the time goes:
time: 497 us; the launch traced here: 493 us
  waiting for transfers between devices  362 us (73%)
  local copies, waits for them, and re-layouts  43 us (9%)
  blocking collectives  38.1 us (8%)
  other arithmetic  16 us (3%)
  matrix products  13.6 us (3%)
  between operations  13.4 us (3%)
  starting transfers between devices  6.82 us (1%)
    reduce_scatter x1, waiting for transfers between devices, on_device(): lax.psum_scatter(jnp.dot(block_rows, down_matrix, preferred_element_type=...  253 us
    all_gather x1, waiting for transfers between devices, on_device(): block_rows = lax.all_gather(arrived, 'grp', axis=0, tiled=True)  92.1 us
    all_gather x2, blocking collectives, joined_2(): everything = jax.tree.map(lambda part: lax.all_gather(part, axis), array)  29.7 us
    unnamed x27, local copies, waits for them, and re-layouts  14.9 us
  transfers between devices with their start and end apart: 7, of which 7 were waited for; matrix products, arithmetic and copies ran while one was open for 1% of the time, Pallas kernels for 0%

commit v1 on v0

v1 whole, which is shorter than its diff:
```python
import jax
import jax.numpy as jnp
from jax import lax
from jax.experimental import pallas as pl
from jax.experimental.pallas import tpu as pltpu
from jax.sharding import Mesh, PartitionSpec as P

HEADS = 36
HEAD_DIM = 64
PAGE = 128
D = HEADS * HEAD_DIM
HP = 48
LW = 128
W = D + LW
NEG_FILL = -1e30
NORM_EPS = 1e-06
F32 = jnp.float32
BF16 = jnp.bfloat16


def dot(a, b, ca=1, cb=0):
    return lax.dot_general(a, b, (((ca,), (cb,)), ((), ())), preferred_element_type=F32)


def head_mask(rows, cols):
    row = lax.broadcasted_iota(jnp.int32, (rows, cols), 0)
    col = lax.broadcasted_iota(jnp.int32, (rows, cols), 1)
    return (col >= row * HEAD_DIM) & (col < (row + 1) * HEAD_DIM)


def placed(part, shape, axis):
    head = lax.broadcasted_iota(jnp.int32, shape, axis)
    lane = lax.broadcasted_iota(jnp.int32, shape, 1 - axis)
    return ((lane == head + part * HEADS) & (head < HEADS)).astype(BF16)


def halves(value):
    high = value.astype(BF16)
    return high, (value - high.astype(F32)).astype(BF16)


def attn_kernel(first_ref, q_ref, table_ref, len_ref, k_hbm, v_hbm, out_ref, kbuf, vbuf, obuf, ksem, vsem):
    pages = k_hbm.shape[0]
    rows = q_ref.shape[0]
    for p in range(pages):
        pltpu.make_async_copy(k_hbm.at[p], kbuf.at[p], ksem.at[p]).start()
        pltpu.make_async_copy(v_hbm.at[p], vbuf.at[p], vsem.at[p]).start()
    first = first_ref[0]
    table = table_ref[...]
    length = len_ref[...]
    start = lax.broadcasted_iota(jnp.int32, table.shape, 1) * PAGE
    remain = jnp.clip(length - start, 0, PAGE)
    lane = lax.broadcasted_iota(jnp.int32, (rows, pages), 1)
    owner = jnp.zeros((rows, pages), F32)
    seen = []
    for p in range(pages):
        match = jnp.where(table == first + p, remain, 0).astype(F32)
        per_row = jnp.sum(match, axis=1, keepdims=True)
        seen.append(jnp.sum(per_row, axis=0, keepdims=True).astype(jnp.int32))
        owner = jnp.where((lane == p) & (per_row > 0), 1.0, owner)
    owner_b = owner.astype(BF16)
    q_sel = dot(owner_b, q_ref[...], 0, 0)
    mask = head_mask(HP, D)
    spread = mask.astype(F32).astype(BF16)
    token = lax.broadcasted_iota(jnp.int32, (PAGE, HP), 0)
    tops, sums = [], []
    for p in range(pages):
        q_diag = jnp.where(mask, q_sel[p : p + 1, :], 0.0).astype(BF16)
        pltpu.make_async_copy(k_hbm.at[p], kbuf.at[p], ksem.at[p]).wait()
        scores = dot(kbuf[p], q_diag, 1, 1) * HEAD_DIM**-0.5
        visible = token < seen[p]
        scores = jnp.where(visible, scores, NEG_FILL)
        top = jnp.max(scores, axis=0, keepdims=True)
        terms = jnp.where(visible, jnp.exp(scores - top), 0.0)
        tops.append(top)
        sums.append(jnp.sum(terms, axis=0, keepdims=True))
        pltpu.make_async_copy(v_hbm.at[p], vbuf.at[p], vsem.at[p]).wait()
        mixed = dot(terms.astype(BF16), vbuf[p], 0, 0)
        obuf[p : p + 1, :] = jnp.sum(jnp.where(mask, mixed, 0.0), axis=0, keepdims=True)
    top = jnp.concatenate(tops, axis=0)
    total = jnp.concatenate(sums, axis=0)
    total = jnp.where(total > 0, total, 1.0)
    lse = top + jnp.log(total)
    same = dot(owner_b, owner_b, 0, 0)
    peak = jnp.full(lse.shape, NEG_FILL, F32)
    for p in range(pages):
        peak = jnp.maximum(peak, jnp.where(same[:, p : p + 1] > 0, lse[p : p + 1, :], NEG_FILL))
    share = jnp.exp(lse - peak)
    whole = jnp.zeros(lse.shape, F32)
    for p in range(pages):
        whole = whole + jnp.where(same[:, p : p + 1] > 0, share[p : p + 1, :], 0.0)
    whole = jnp.where(whole > 0, whole, 1.0)
    high, low = halves(share / (whole * total))
    scaled = (dot(high, spread) + dot(low, spread)) * obuf[...]
    high, low = halves(scaled)
    out_ref[:, :D] = (dot(owner_b, high) + dot(owner_b, low)).astype(BF16)
    joint = peak + jnp.log(whole)
    row_lse = jnp.full((rows, HP), NEG_FILL, F32)
    for p in range(pages):
        row_lse = jnp.maximum(row_lse, jnp.where(owner[:, p : p + 1] > 0, joint[p : p + 1, :], NEG_FILL))
    first_part, rest = row_lse.astype(BF16), None
    rest = row_lse - first_part.astype(F32)
    second, third = halves(rest)
    packed = (
        dot(first_part, placed(0, (HP, LW), 0))
        + dot(second, placed(1, (HP, LW), 0))
        + dot(third, placed(2, (HP, LW), 0))
    )
    out_ref[:, D:] = packed.astype(BF16)


def merge_kernel(arr_ref, valid_ref, res_ref, gain_ref, coef_ref, attn_ref, out_ref):
    own = res_ref.shape[0]
    count = arr_ref.shape[0] // own
    folded = placed(0, (LW, HP), 1) + placed(1, (LW, HP), 1) + placed(2, (LW, HP), 1)
    lse = dot(arr_ref[:, D:], folded)
    lse = jnp.where(valid_ref[...] > 0, lse, NEG_FILL)
    parts = [lse[own * s : own * (s + 1), :] for s in range(count)]
    peak = parts[0]
    for part in parts[1:]:
        peak = jnp.maximum(peak, part)
    shares = [jnp.exp(part - peak) for part in parts]
    whole = shares[0]
    for share in shares[1:]:
        whole = whole + share
    scale = 1.0 / whole
    weight = jnp.concatenate([share * scale for share in shares], axis=0)
    spread = head_mask(HP, D).astype(F32).astype(BF16)
    high, low = halves(weight)
    scaled = (dot(high, spread) + dot(low, spread)) * arr_ref[:, :D].astype(F32)
    row = lax.broadcasted_iota(jnp.int32, (own, own * count), 0)
    col = lax.broadcasted_iota(jnp.int32, (own, own * count), 1)
    gather = (lax.rem(col, own) == row).astype(BF16)
    high, low = halves(scaled)
    attn = (dot(gather, high) + dot(gather, low)).astype(BF16)
    attn_ref[...] = attn
    stream = res_ref[...].astype(F32) + attn.astype(F32)
    normed = (
        stream
        * lax.rsqrt(jnp.mean(stream * stream, axis=-1, keepdims=True) + NORM_EPS)
        * gain_ref[...].astype(F32)
    ).astype(BF16)
    for i in range(out_ref.shape[0] // own):
        out_ref[own * i : own * (i + 1), :D] = normed
        out_ref[own * i : own * (i + 1), D:] = coef_ref[...]


def mlp_kernel(count, expert_ref, *refs):
    blocks = refs[:count]
    gate_0, up_0, down_0, gate_1, up_1, down_1 = refs[count : count + 6]
    outs = refs[count + 6 :]
    rows = blocks[0].shape[0]
    each = count // 2
    for half in range(2):
        mine = [ref[...] for ref in blocks[half * each : (half + 1) * each]]
        joined = jnp.concatenate(mine, axis=0)
        x = joined[:, :D]
        coefs = joined[:, D:].astype(F32)
        lane = lax.broadcasted_iota(jnp.int32, coefs.shape, 1)
        result = None
        for k, (gate, up, down) in enumerate(((gate_0, up_0, down_0), (gate_1, up_1, down_1))):
            coef = jnp.sum(jnp.where(lane == expert_ref[k], coefs, 0.0), axis=1, keepdims=True)
            g = dot(x, gate[...])
            u = dot(x, up[...])
            inner = ((g / (1.0 + jnp.exp(-g))) * u * coef).astype(BF16)
            y = dot(inner, down[...])
            result = y if result is None else result + y
        result = result.astype(BF16)
        for i in range(each):
            outs[half * each + i][...] = result[rows * i : rows * (i + 1), :]


VMEM = pltpu.CompilerParams(vmem_limit_bytes=56 * 1024 * 1024)
X = "x"
Y = ("yh", "yp")
Z = ("zh", "zl")


def shifted(array, axis, shift, n=4):
    return lax.ppermute(array, axis, [(i, (i + shift) % n) for i in range(n)])


def gathered(array, axis):
    return [array] + [shifted(array, axis, s) for s in (1, 2, 3)]


def scattered(blocks, axis):
    back = [shifted(block, axis, -s) for s, block in zip((1, 2, 3), blocks[1:])]
    total = blocks[0].astype(F32)
    for block in back:
        total = total + block.astype(F32)
    return total.astype(BF16)


def on_device(
    queries, residual, gain, key_pages, value_pages, page_table, lengths, split_flag, routes, gates,
    w_gate, w_up, w_down,
):
    own = residual.shape[0]
    rows = queries.shape[0]
    pages = key_pages.shape[0]
    my_ep = lax.axis_index(("zl", "c"))
    my_pair = lax.axis_index("yp")
    swap = [(0, 1), (1, 0)]
    mine = (w_gate[0], w_up[0], w_down[0])
    theirs = tuple(lax.ppermute(w, "c", swap) for w in mine)
    experts = jnp.stack([my_ep, my_ep ^ 1]).astype(jnp.int32)

    partial = pl.pallas_call(
        attn_kernel,
        out_shape=jax.ShapeDtypeStruct((rows, W), BF16),
        in_specs=[pl.BlockSpec(memory_space=pltpu.SMEM)]
        + [pl.BlockSpec(memory_space=pltpu.VMEM)] * 3
        + [pl.BlockSpec(memory_space=pl.ANY)] * 2,
        scratch_shapes=[
            pltpu.VMEM((pages, PAGE, D), BF16),
            pltpu.VMEM((pages, PAGE, D), BF16),
            pltpu.VMEM((pages, D), F32),
            pltpu.SemaphoreType.DMA((pages,)),
            pltpu.SemaphoreType.DMA((pages,)),
        ],
        compiler_params=VMEM,
        name="attn",
    )(
        (my_ep * pages).astype(jnp.int32).reshape(1), queries, page_table, lengths.reshape(rows, 1),
        key_pages, value_pages,
    )
    both = jnp.concatenate([partial, partial], axis=0)
    arrived = lax.all_to_all(both, ("yp", "zl", "c"), 0, 0, tiled=True)
    sources = arrived.shape[0] // own
    split_own = lax.dynamic_slice_in_dim(split_flag, my_ep * own, own, 0) == 1
    same_group = (jnp.arange(sources) // (sources // 2)) == my_pair
    valid = (same_group[:, None] | split_own[None, :]).astype(F32).reshape(sources * own, 1)
    lanes = jnp.arange(LW, dtype=jnp.int32)
    coefs = jnp.sum(
        jnp.where(routes[:, :, None] == lanes[None, None, :], gates[:, :, None].astype(F32), 0.0), axis=1
    ).astype(BF16)
    attn, normed = pl.pallas_call(
        merge_kernel,
        out_shape=(
            jax.ShapeDtypeStruct((own, D), BF16),
            jax.ShapeDtypeStruct((8 * own, W), BF16),
        ),
        compiler_params=VMEM,
        name="merge",
    )(arrived, valid, residual, gain.reshape(1, D), coefs)

    stacked = lax.all_to_all(normed, Z, 0, 0, tiled=True)
    half = stacked.shape[0] // 2
    a_x = jnp.concatenate(gathered(stacked[:half], X), axis=0)
    b_y = jnp.concatenate(gathered(stacked[half:], Y), axis=0)
    a_all = gathered(a_x, Y)
    b_all = gathered(b_y, X)
    blocks = a_all + b_all
    results = pl.pallas_call(
        lambda *refs: mlp_kernel(len(blocks), *refs),
        out_shape=[jax.ShapeDtypeStruct((4 * half, D), BF16)] * len(blocks),
        in_specs=[pl.BlockSpec(memory_space=pltpu.SMEM)]
        + [pl.BlockSpec(memory_space=pltpu.VMEM)] * (len(blocks) + 6),
        compiler_params=VMEM,
        name="mlp",
    )(experts, *blocks, *mine, *theirs)
    a_back = scattered(results[:4], Y)
    b_back = scattered(results[4:], X)
    a_fin = scattered([a_back[half * i : half * (i + 1)] for i in range(4)], X)
    b_fin = scattered([b_back[half * i : half * (i + 1)] for i in range(4)], Y)
    outgoing = jnp.concatenate([a_fin, b_fin], axis=0)
    returned = lax.all_to_all(outgoing, Z, 0, 0, tiled=True).reshape(-1, own, D)
    mixture = jnp.sum(returned.astype(F32), axis=0)
    return (attn.astype(F32) + mixture).astype(BF16)


def solution(mesh):
    fine = Mesh(mesh.devices.reshape(4, 2, 2, 2, 4, 2), ("x", "zh", "yh", "yp", "zl", "c"))
    grp = ("x", "zh", "yh", "yp")
    ep = ("zl", "c")
    in_specs = (
        P(grp, None),
        P(grp + ep, None),
        P(),
        P(grp + ep, None, None),
        P(grp + ep, None, None),
        P(grp, None),
        P(grp),
        P(grp),
        P(grp + ep, None),
        P(grp + ep, None),
        P(ep, None, grp),
        P(ep, None, grp),
        P(ep, grp, None),
    )
    return jax.shard_map(
        on_device, mesh=fine, in_specs=in_specs, out_specs=P(grp + ep, None), check_vma=False
    )
```

time: 497 us -> 152 us (0.31)
  waiting for transfers between devices: 362 us -> 48.3 us
  starting transfers between devices: 6.82 us -> 50.3 us
  local copies, waits for them, and re-layouts: 43 us -> 13.6 us
  blocking collectives: 38.1 us -> 11.6 us
  Pallas kernels: 0 us -> 21.1 us
  matrix products: 13.6 us -> 0 us
  between operations: 13.4 us -> 0.28 us
  other arithmetic: 16 us -> 4.46 us
    reduce_scatter x1 -> x0, waiting for transfers between devices: 253 us -> none  [on_device(): lax.psum_scatter(jnp.dot(block_rows, down_matrix, preferred_element_type=...]
    all_gather x2 -> x0, waiting for transfers between devices: 101 us -> none  [the longest x1 92.1 us: on_device(): block_rows = lax.all_gather(arrived, 'grp', axis=0, tiled=True)]
    ppermute x3 -> x27, starting transfers between devices: 3.38 us -> 37.7 us  [the longest x24 37.1 us: shifted(): return lax.ppermute(array, axis, [(i, (i + shift) % n) for i in range(n)])]
    all_gather x2 -> x0, blocking collectives: 29.7 us -> none  [joined_2(): everything = jax.tree.map(lambda part: lax.all_gather(part, axis), array)]
    ppermute x3 -> x27, waiting for transfers between devices: 2.17 us -> 30.5 us  [the longest x24 30.5 us: shifted(): return lax.ppermute(array, axis, [(i, (i + shift) % n) for i in range(n)])]
    pallas_call x0 -> x3, Pallas kernels: none -> 21.1 us  [the longest x1 9.89 us: on_device(): pl.pallas_call(attn_kernel, out_shape=jax.ShapeDtypeStruct((rows, W), BF1...]
    reshape x8 -> x2, local copies, waits for them, and re-layouts: 19 us -> 1.94 us  [the longest x1 1.34 us: on_device(): lengths.reshape(rows, 1)]
    dot_general x6 -> x0, matrix products: 13.6 us -> none  [the longest x1 4.92 us: on_device(): jnp.dot(block_rows, down_matrix, preferred_element_type=jnp.float32)]
  transfers between devices with their start and end apart: 7 -> 29, of which waited for: 7 -> 10; matrix products, arithmetic and copies ran while one was open for 1% -> 8% of each run, Pallas kernels for 0% -> 0%
where the time goes in v1:
time: 152 us; the launch traced here: 150 us
  starting transfers between devices  50.3 us (33%)
  waiting for transfers between devices  48.3 us (32%)
  Pallas kernels  21.1 us (14%)
  local copies, waits for them, and re-layouts  13.6 us (9%)
  blocking collectives  11.6 us (8%)
  other arithmetic  4.46 us (3%)
    ppermute x24, starting transfers between devices, shifted(): return lax.ppermute(array, axis, [(i, (i + shift) % n) for i in range(n)])  37.1 us
    ppermute x24, waiting for transfers between devices, shifted(): return lax.ppermute(array, axis, [(i, (i + shift) % n) for i in range(n)])  30.5 us
    all_to_all x1, blocking collectives, on_device(): returned = lax.all_to_all(outgoing, Z, 0, 0, tiled=True).reshape(-1, own, D)  11.6 us
    pallas_call x1, Pallas kernels, on_device(): pl.pallas_call(attn_kernel, out_shape=jax.ShapeDtypeStruct((rows, W), BF1...  9.89 us
    all_to_all x1, waiting for transfers between devices, on_device(): stacked = lax.all_to_all(normed, Z, 0, 0, tiled=True)  9.03 us
    all_to_all x1, waiting for transfers between devices, on_device(): arrived = lax.all_to_all(both, ('yp', 'zl', 'c'), 0, 0, tiled=True)  8.73 us
    pallas_call x1, Pallas kernels, on_device(): pl.pallas_call(lambda *refs: mlp_kernel(len(blocks), *refs), out_shape=[j...  8.72 us
    all_to_all x1, starting transfers between devices, on_device(): arrived = lax.all_to_all(both, ('yp', 'zl', 'c'), 0, 0, tiled=True)  6.85 us
  transfers between devices with their start and end apart: 29, of which 10 were waited for; matrix products, arithmetic and copies ran while one was open for 8% of the time, Pallas kernels for 0%

profile of v1, /device:TPU:16, one launch (start us, length us, event | category | flops | bytes accessed | tf_op | source)
XLA Modules:
  0.0 149.6 jit_solution(15425192536810791925)
XLA Ops:
  1.3 9.9 %attn.1 = bf16[32,2432]{1,0:T(8,128)(2,1)} custom-call(s32[1]{0:T(128)} %bitcast.first_ref, bf16[32,2304]{1,0:T(8,128)(2,1)} %q_ref.1, s32[32,32]{1,0:T(8,128)} %table_ref.1, s32[32,1]{1,0:T(8,128)} %copy.36.len_ref, bf16[8,128,2304]{2,1,0:T(8,128)(2,1)} %k_hbm.1, bf16[8,128,2304]{2,1,0:T(8,128)(2,1)} %v_hbm.1), custom_call_target="tpu_custom_call" | custom-call | tf_op jit(solution)/shard_map/attn/pallas_call | solution.py:209
  13.1 6.9 %all-to-all-start = ((bf16[16,4,2432]{2,1,0:T(4,128)(2,1)}), bf16[16,4,2432]{2,1,0:T(4,128)(2,1)S(1)}, u32[]{:S(2)}, u32[]{:S(2)}) async-start(bf16[16,4,2432]{2,1,0:T(4,128)(2,1)} %all_to_all.19), calls=%async_computation | async-start | bytes 622592 | tf_op jit(solution)/shard_map/all_to_all | solution.py:229
  22.1 8.7 %all-to-all-done = bf16[16,4,2432]{2,1,0:T(4,128)(2,1)S(1)} async-done(((bf16[16,4,2432]{2,1,0:T(4,128)(2,1)}), bf16[16,4,2432]{2,1,0:T(4,128)(2,1)S(1)}, u32[]{:S(2)}, u32[]{:S(2)}) %all-to-all-start) | async-done | bytes 311328 | tf_op jit(solution)/shard_map/all_to_all | solution.py:229
  31.6 2.5 %merge.1 = (bf16[4,2304]{1,0:T(4,128)(2,1)}, bf16[32,2432]{1,0:T(8,128)(2,1)}) custom-call(bf16[64,2432]{1,0:T(8,128)(2,1)} %all_to_all.21.arr_ref, f32[64,1]{1,0:T(8,128)} %reshape.69.valid_ref, bf16[4,2304]{1,0:T(4,128)(2,1)} %res_ref.1, bf16[1,2304]{1,0:T(2,128)(2,1)} %reshape.67.gain_ref, bf16[4,128]{1,0:T(4,128)(2,1)} %select_reduce_fusion.coef_ref), custom_call_target="tpu_custom_call" | custom-call | tf_op jit(solution)/shard_map/merge/pallas_call | solution.py:238
  34.1 1.6 %all_to_all.22 = bf16[8,4,2432]{2,1,0:T(4,128)(2,1)} reshape(bf16[32,2432]{1,0:T(8,128)(2,1)} %get-tuple-element.16) | data formatting | bytes 311296 | tf_op jit(solution)/shard_map/all_to_all | solution.py:248
  35.7 5.8 %all-to-all-start.1 = ((bf16[8,4,2432]{2,1,0:T(4,128)(2,1)}), bf16[8,4,2432]{2,1,0:T(4,128)(2,1)S(1)}, u32[]{:S(2)}, u32[]{:S(2)}) async-start(bf16[8,4,2432]{2,1,0:T(4,128)(2,1)} %all_to_all.22), calls=%async_computation.1 | async-start | bytes 311296 | tf_op jit(solution)/shard_map/all_to_all | solution.py:248
  42.1 9.0 %all-to-all-done.1 = bf16[8,4,2432]{2,1,0:T(4,128)(2,1)S(1)} async-done(((bf16[8,4,2432]{2,1,0:T(4,128)(2,1)}), bf16[8,4,2432]{2,1,0:T(4,128)(2,1)S(1)}, u32[]{:S(2)}, u32[]{:S(2)}) %all-to-all-start.1) | async-done | bytes 155680 | tf_op jit(solution)/shard_map/all_to_all | solution.py:248
  51.2 2.8 %collective-permute-start.2 = (bf16[16,2432]{1,0:T(8,128)(2,1)S(1)}, bf16[16,2432]{1,0:T(8,128)(2,1)}, u32[]{:S(2)}, u32[]{:S(2)}) collective-permute-start(bf16[16,2432]{1,0:T(8,128)(2,1)S(1)} %slice.37), channel_id=1, source_target_pairs={{0,192},{64,0},{128,64},{192,128},{1,193},{65,1},{129,65},{193,129... | collective-permute-start | bytes 233480 | tf_op jit(solution)/shard_map/ppermute | solution.py:180
  54.1 5.6 %collective-permute-done = bf16[16,2432]{1,0:T(8,128)(2,1)S(1)} collective-permute-done((bf16[16,2432]{1,0:T(8,128)(2,1)S(1)}, bf16[16,2432]{1,0:T(8,128)(2,1)S(1)}, u32[]{:S(2)}, u32[]{:S(2)}) %collective-permute-start) | collective-permute-done | bytes 77856 | tf_op jit(solution)/shard_map/ppermute | solution.py:180
  60.7 4.2 %collective-permute-done.6 = bf16[16,2432]{1,0:T(8,128)(2,1)S(1)} collective-permute-done((bf16[16,2432]{1,0:T(8,128)(2,1)S(1)}, bf16[16,2432]{1,0:T(8,128)(2,1)S(1)}, u32[]{:S(2)}, u32[]{:S(2)}) %collective-permute-start.6) | collective-permute-done | bytes 77856 | tf_op jit(solution)/shard_map/ppermute | solution.py:180
  66.0 4.8 %collective-permute-done.7 = bf16[16,2432]{1,0:T(8,128)(2,1)S(1)} collective-permute-done((bf16[16,2432]{1,0:T(8,128)(2,1)S(1)}, bf16[16,2432]{1,0:T(8,128)(2,1)S(1)}, u32[]{:S(2)}, u32[]{:S(2)}) %collective-permute-start.7) | collective-permute-done | bytes 77856 | tf_op jit(solution)/shard_map/ppermute | solution.py:180
  70.8 4.4 %collective-permute-done.8 = bf16[16,2432]{1,0:T(8,128)(2,1)S(1)} collective-permute-done((bf16[16,2432]{1,0:T(8,128)(2,1)S(1)}, bf16[16,2432]{1,0:T(8,128)(2,1)S(1)}, u32[]{:S(2)}, u32[]{:S(2)}) %collective-permute-start.8) | collective-permute-done | bytes 77856 | tf_op jit(solution)/shard_map/ppermute | solution.py:180
  75.2 6.8 %collective-permute-done.1 = bf16[16,2432]{1,0:T(8,128)(2,1)S(1)} collective-permute-done((bf16[16,2432]{1,0:T(8,128)(2,1)S(1)}, bf16[16,2432]{1,0:T(8,128)(2,1)S(1)}, u32[]{:S(2)}, u32[]{:S(2)}) %collective-permute-start.1) | collective-permute-done | bytes 77856 | tf_op jit(solution)/shard_map/ppermute | solution.py:180
  85.2 4.5 %collective-permute-start.4 = (bf16[64,2432]{1,0:T(8,128)(2,1)S(1)}, bf16[64,2432]{1,0:T(8,128)(2,1)}, u32[]{:S(2)}, u32[]{:S(2)}) collective-permute-start(bf16[64,2432]{1,0:T(8,128)(2,1)S(1)} %constant_dynamic-update-slice_fusion.refs_1_), channel_id=1, source_target_pairs={{0,16},{8,24},{16,0},{24,8},{1,17},{9,25},{17,1},{25,9},{2,18},{10... | collective-permute-start | bytes 933896 | tf_op jit(solution)/shard_map/ppermute | solution.py:180
  89.8 1.7 %collective-permute-start.3 = (bf16[64,2432]{1,0:T(8,128)(2,1)S(1)}, bf16[64,2432]{1,0:T(8,128)(2,1)}, u32[]{:S(2)}, u32[]{:S(2)}) collective-permute-start(bf16[64,2432]{1,0:T(8,128)(2,1)S(1)} %constant_dynamic-update-slice_fusion.refs_1_), channel_id=1, source_target_pairs={{0,8},{8,16},{16,24},{24,0},{1,9},{9,17},{17,25},{25,1},{2,10},{10... | collective-permute-start | bytes 933896 | tf_op jit(solution)/shard_map/ppermute | solution.py:180
  91.5 1.4 copy.38
  92.9 1.4 copy.39
  94.9 1.4 copy.43.refs_13_
  96.3 2.3 %copy.42.refs_12_ = bf16[2304,180]{1,0:T(8,128)(2,1)} copy(bf16[2304,180]{0,1:T(8,128)(2,1)} %collective-permute-done.12) | data formatting | bytes 1658880 | tf_op jit(solution)/shard_map/ppermute | solution.py:206
  98.7 8.7 %mlp.1 = (bf16[64,2304]{1,0:T(8,128)(2,1)}, bf16[64,2304]{1,0:T(8,128)(2,1)}, bf16[64,2304]{1,0:T(8,128)(2,1)}, bf16[64,2304]{1,0:T(8,128)(2,1)}, bf16[64,2304]{...) custom-call(s32[2]{0:T(128)} %pad_add_fusion.refs_0_, ...), custom_call_target="tpu_custom_call" | custom-call | tf_op jit(solution)/shard_map/mlp/pallas_call | solution.py:255
  107.8 3.2 %collective-permute-start.16 = (bf16[64,2304]{1,0:T(8,128)(2,1)}, bf16[64,2304]{1,0:T(8,128)(2,1)S(1)}, u32[]{:S(2)}, u32[]{:S(2)}) collective-permute-start(bf16[64,2304]{1,0:T(8,128)(2,1)} %get-tuple-element.19), channel_id=1, source_target_pairs={{0,16},{8,24},{16,0},{24,8},{1,17},{9,25},{17,1},{25,9},{2,18},{10... | collective-permute-start | bytes 884744 | tf_op jit(solution)/shard_map/ppermute | solution.py:180
  111.0 2.0 %collective-permute-start.17 = (bf16[64,2304]{1,0:T(8,128)(2,1)}, bf16[64,2304]{1,0:T(8,128)(2,1)S(1)}, u32[]{:S(2)}, u32[]{:S(2)}) collective-permute-start(bf16[64,2304]{1,0:T(8,128)(2,1)} %get-tuple-element.20), channel_id=1, source_target_pairs={{0,8},{8,16},{16,24},{24,0},{1,9},{9,17},{17,25},{25,1},{2,10},{10... | collective-permute-start | bytes 884744 | tf_op jit(solution)/shard_map/ppermute | solution.py:180
  113.0 2.6 %collective-permute-start.21 = (bf16[64,2304]{1,0:T(8,128)(2,1)}, bf16[64,2304]{1,0:T(8,128)(2,1)S(1)}, u32[]{:S(2)}, u32[]{:S(2)}) collective-permute-start(bf16[64,2304]{1,0:T(8,128)(2,1)} %get-tuple-element.22), channel_id=1, source_target_pairs={{0,192},{64,0},{128,64},{192,128},{1,193},{65,1},{129,65},{193,129... | collective-permute-start | bytes 884744 | tf_op jit(solution)/shard_map/ppermute | solution.py:180
  115.6 1.4 collective-permute-start.22
  117.0 1.4 collective-permute-start.23
  118.4 1.8 %collective-permute-done.17 = bf16[64,2304]{1,0:T(8,128)(2,1)S(1)} collective-permute-done((bf16[64,2304]{1,0:T(8,128)(2,1)}, bf16[64,2304]{1,0:T(8,128)(2,1)S(1)}, u32[]{:S(2)}, u32[]{:S(2)}) %collective-permute-start.17) | collective-permute-done | bytes 294944 | tf_op jit(solution)/shard_map/ppermute | solution.py:180
  121.3 3.8 %collective-permute-start.18 = (bf16[16,2304]{1,0:T(8,128)(2,1)S(1)}, bf16[16,2304]{1,0:T(8,128)(2,1)S(1)}, u32[]{:S(2)}, u32[]{:S(2)}) collective-permute-start(bf16[16,2304]{1,0:T(8,128)(2,1)S(1)} %get-tuple-element.25), channel_id=1, source_target_pairs={{0,192},{64,0},{128,64},{192,128},{1,193},{65,1},{129,65},{193,129... | collective-permute-start | bytes 221192 | tf_op jit(solution)/shard_map/ppermute | solution.py:180
  125.2 3.4 %collective-permute-start.19 = (bf16[16,2304]{1,0:T(8,128)(2,1)S(1)}, bf16[16,2304]{1,0:T(8,128)(2,1)S(1)}, u32[]{:S(2)}, u32[]{:S(2)}) collective-permute-start(bf16[16,2304]{1,0:T(8,128)(2,1)S(1)} %get-tuple-element.27), channel_id=1, source_target_pairs={{0,128},{64,192},{128,0},{192,64},{1,129},{65,193},{129,1},{193,65... | collective-permute-start | bytes 221192 | tf_op jit(solution)/shard_map/ppermute | solution.py:180
  129.4 1.5 collective-permute-start.26
  130.9 3.2 %collective-permute-start.25 = (bf16[16,2304]{1,0:T(8,128)(2,1)S(1)}, bf16[16,2304]{1,0:T(8,128)(2,1)S(1)}, u32[]{:S(2)}, u32[]{:S(2)}) collective-permute-start(bf16[16,2304]{1,0:T(8,128)(2,1)S(1)} %get-tuple-element.30), channel_id=1, source_target_pairs={{0,16},{8,24},{16,0},{24,8},{1,17},{9,25},{17,1},{25,9},{2,18},{10... | collective-permute-start | bytes 221192 | tf_op jit(solution)/shard_map/ppermute | solution.py:180
  134.9 2.2 %collective-permute-done.25 = bf16[16,2304]{1,0:T(8,128)(2,1)S(1)} collective-permute-done((bf16[16,2304]{1,0:T(8,128)(2,1)S(1)}, bf16[16,2304]{1,0:T(8,128)(2,1)S(1)}, u32[]{:S(2)}, u32[]{:S(2)}) %collective-permute-start.25) | collective-permute-done | bytes 73760 | tf_op jit(solution)/shard_map/ppermute | solution.py:180
  137.3 11.6 %all_to_all.29 = bf16[8,4,2304]{2,1,0:T(4,128)(2,1)S(1)} all-to-all(bf16[8,4,2304]{2,1,0:T(4,128)(2,1)S(1)} %all_to_all.24), channel_id=1, replica_groups=mesh['x'=4,'zh'=2,'yh'=2,'yp'=2,'zl'=4,'c'=2] {'zh','zl'}, dimensions={0} | all-to-all | bytes 294912 | tf_op jit(solution)/shard_map/all_to_all | solution.py:268
  (90 shorter events, 16.9 us)
Async XLA Ops:
  13.1 28.4 %copy-start.1 = (bf16[1,2304,180]{1,2,0:T(8,128)(2,1)S(1)}, bf16[1,2304,180]{1,2,0:T(8,128)(2,1)}, u32[]{:S(2)}) copy-start(bf16[1,2304,180]{1,2,0:T(8,128)(2,1)} %param.24) | copy-start | bytes 2488324
  13.1 28.9 %copy-start = (bf16[1,2304,180]{1,2,0:T(8,128)(2,1)S(1)}, bf16[1,2304,180]{1,2,0:T(8,128)(2,1)}, u32[]{:S(2)}) copy-start(bf16[1,2304,180]{1,2,0:T(8,128)(2,1)} %param.23) | copy-start | bytes 2488324
  13.1 17.7 %all-to-all-start = ((bf16[16,4,2432]{2,1,0:T(4,128)(2,1)}), bf16[16,4,2432]{2,1,0:T(4,128)(2,1)S(1)}, u32[]{:S(2)}, u32[]{:S(2)}) async-start(bf16[16,4,2432]{2,1,0:T(4,128)(2,1)} %all_to_all.19), calls=%async_computation | async-start | bytes 622592 | tf_op jit(solution)/shard_map/all_to_all | solution.py:229
  35.7 15.4 %all-to-all-start.1 = ((bf16[8,4,2432]{2,1,0:T(4,128)(2,1)}), bf16[8,4,2432]{2,1,0:T(4,128)(2,1)S(1)}, u32[]{:S(2)}, u32[]{:S(2)}) async-start(bf16[8,4,2432]{2,1,0:T(4,128)(2,1)} %all_to_all.22), calls=%async_computation.1 | async-start | bytes 311296 | tf_op jit(solution)/shard_map/all_to_all | solution.py:248
  41.5 42.3 %collective-permute-start.14 = (bf16[180,2304]{1,0:T(8,128)(2,1)}, bf16[180,2304]{1,0:T(8,128)(2,1)}, u32[]{:S(2)}, u32[]{:S(2)}) collective-permute-start(bf16[180,2304]{1,0:T(8,128)(2,1)} %bitcast.6.refs_11_), channel_id=1, source_target_pairs={{0,1},{1,0},{2,3},{3,2},{4,5},{5,4},{6,7},{7,6},{8,9},{9,8},{10,11... | collective-permute-start | bytes 2488328 | tf_op jit(solution)/shard_map/ppermute | solution.py:206
  41.5 43.6 %collective-permute-start.13 = (bf16[2304,180]{0,1:T(8,128)(2,1)S(1)}, bf16[2304,180]{0,1:T(8,128)(2,1)S(1)}, u32[]{:S(2)}, u32[]{:S(2)}) collective-permute-start(bf16[2304,180]{0,1:T(8,128)(2,1)S(1)} %bitcast.12), channel_id=1, source_target_pairs={{0,1},{1,0},{2,3},{3,2},{4,5},{5,4},{6,7},{7,6},{8,9},{9,8},{10,11... | collective-permute-start | bytes 2488328 | tf_op jit(solution)/shard_map/ppermute | solution.py:206
  42.0 43.2 %collective-permute-start.12 = (bf16[2304,180]{0,1:T(8,128)(2,1)S(1)}, bf16[2304,180]{0,1:T(8,128)(2,1)}, u32[]{:S(2)}, u32[]{:S(2)}) collective-permute-start(bf16[2304,180]{0,1:T(8,128)(2,1)S(1)} %bitcast.11), channel_id=1, source_target_pairs={{0,1},{1,0},{2,3},{3,2},{4,5},{5,4},{6,7},{7,6},{8,9},{9,8},{10,11... | collective-permute-start | bytes 2488328 | tf_op jit(solution)/shard_map/ppermute | solution.py:206
  51.2 30.8 %collective-permute-start.2 = (bf16[16,2432]{1,0:T(8,128)(2,1)S(1)}, bf16[16,2432]{1,0:T(8,128)(2,1)}, u32[]{:S(2)}, u32[]{:S(2)}) collective-permute-start(bf16[16,2432]{1,0:T(8,128)(2,1)S(1)} %slice.37), channel_id=1, source_target_pairs={{0,192},{64,0},{128,64},{192,128},{1,193},{65,1},{129,65},{193,129... | collective-permute-start | bytes 233480 | tf_op jit(solution)/shard_map/ppermute | solution.py:180
  54.1 5.6 %collective-permute-start = (bf16[16,2432]{1,0:T(8,128)(2,1)S(1)}, bf16[16,2432]{1,0:T(8,128)(2,1)S(1)}, u32[]{:S(2)}, u32[]{:S(2)}) collective-permute-start(bf16[16,2432]{1,0:T(8,128)(2,1)S(1)} %slice.37), channel_id=1, source_target_pairs={{0,64},{64,128},{128,192},{192,0},{1,65},{65,129},{129,193},{193,1... | collective-permute-start | bytes 233480 | tf_op jit(solution)/shard_map/ppermute | solution.py:180
  59.7 5.2 %collective-permute-start.6 = (bf16[16,2432]{1,0:T(8,128)(2,1)S(1)}, bf16[16,2432]{1,0:T(8,128)(2,1)S(1)}, u32[]{:S(2)}, u32[]{:S(2)}) collective-permute-start(bf16[16,2432]{1,0:T(8,128)(2,1)S(1)} %slice.39), channel_id=1, source_target_pairs={{0,8},{8,16},{16,24},{24,0},{1,9},{9,17},{17,25},{25,1},{2,10},{10... | collective-permute-start | bytes 233480 | tf_op jit(solution)/shard_map/ppermute | solution.py:180
  64.9 5.9 %collective-permute-start.7 = (bf16[16,2432]{1,0:T(8,128)(2,1)S(1)}, bf16[16,2432]{1,0:T(8,128)(2,1)S(1)}, u32[]{:S(2)}, u32[]{:S(2)}) collective-permute-start(bf16[16,2432]{1,0:T(8,128)(2,1)S(1)} %slice.39), channel_id=1, source_target_pairs={{0,16},{8,24},{16,0},{24,8},{1,17},{9,25},{17,1},{25,9},{2,18},{10... | collective-permute-start | bytes 233480 | tf_op jit(solution)/shard_map/ppermute | solution.py:180
  70.8 4.4 %collective-permute-start.8 = (bf16[16,2432]{1,0:T(8,128)(2,1)S(1)}, bf16[16,2432]{1,0:T(8,128)(2,1)S(1)}, u32[]{:S(2)}, u32[]{:S(2)}) collective-permute-start(bf16[16,2432]{1,0:T(8,128)(2,1)S(1)} %slice.39), channel_id=1, source_target_pairs={{0,24},{8,0},{16,8},{24,16},{1,25},{9,1},{17,9},{25,17},{2,26},{10... | collective-permute-start | bytes 233480 | tf_op jit(solution)/shard_map/ppermute | solution.py:180
  75.2 6.8 %collective-permute-start.1 = (bf16[16,2432]{1,0:T(8,128)(2,1)S(1)}, bf16[16,2432]{1,0:T(8,128)(2,1)S(1)}, u32[]{:S(2)}, u32[]{:S(2)}) collective-permute-start(bf16[16,2432]{1,0:T(8,128)(2,1)S(1)} %slice.37), channel_id=1, source_target_pairs={{0,128},{64,192},{128,0},{192,64},{1,129},{65,193},{129,1},{193,65... | collective-permute-start | bytes 233480 | tf_op jit(solution)/shard_map/ppermute | solution.py:180
  82.0 7.8 %collective-permute-start.11 = (bf16[64,2432]{1,0:T(8,128)(2,1)S(1)}, bf16[64,2432]{1,0:T(8,128)(2,1)S(1)}, u32[]{:S(2)}, u32[]{:S(2)}) collective-permute-start(bf16[64,2432]{1,0:T(8,128)(2,1)S(1)} %constant_dynamic-update-slice_fusion.4.refs_5_), channel_id=1, source_target_pairs={{0,192},{64,0},{128,64},{192,128},{1,193},{65,1},{129,65},{193,129... | collective-permute-start | bytes 933896 | tf_op jit(solution)/shard_map/ppermute | solution.py:180
  82.0 16.6 %collective-permute-start.10 = (bf16[64,2432]{1,0:T(8,128)(2,1)S(1)}, bf16[64,2432]{1,0:T(8,128)(2,1)}, u32[]{:S(2)}, u32[]{:S(2)}) collective-permute-start(bf16[64,2432]{1,0:T(8,128)(2,1)S(1)} %constant_dynamic-update-slice_fusion.4.refs_5_), channel_id=1, source_target_pairs={{0,128},{64,192},{128,0},{192,64},{1,129},{65,193},{129,1},{193,65... | collective-permute-start | bytes 933896 | tf_op jit(solution)/shard_map/ppermute | solution.py:180
  83.8 14.8 %collective-permute-start.9 = (bf16[64,2432]{1,0:T(8,128)(2,1)S(1)}, bf16[64,2432]{1,0:T(8,128)(2,1)}, u32[]{:S(2)}, u32[]{:S(2)}) collective-permute-start(bf16[64,2432]{1,0:T(8,128)(2,1)S(1)} %constant_dynamic-update-slice_fusion.4.refs_5_), channel_id=1, source_target_pairs={{0,64},{64,128},{128,192},{192,0},{1,65},{65,129},{129,193},{193,1... | collective-permute-start | bytes 933896 | tf_op jit(solution)/shard_map/ppermute | solution.py:180
  85.1 13.5 %collective-permute-start.5 = (bf16[64,2432]{1,0:T(8,128)(2,1)S(1)}, bf16[64,2432]{1,0:T(8,128)(2,1)}, u32[]{:S(2)}, u32[]{:S(2)}) collective-permute-start(bf16[64,2432]{1,0:T(8,128)(2,1)S(1)} %constant_dynamic-update-slice_fusion.refs_1_), channel_id=1, source_target_pairs={{0,24},{8,0},{16,8},{24,16},{1,25},{9,1},{17,9},{25,17},{2,26},{10... | collective-permute-start | bytes 933896 | tf_op jit(solution)/shard_map/ppermute | solution.py:180
  85.2 13.4 %collective-permute-start.4 = (bf16[64,2432]{1,0:T(8,128)(2,1)S(1)}, bf16[64,2432]{1,0:T(8,128)(2,1)}, u32[]{:S(2)}, u32[]{:S(2)}) collective-permute-start(bf16[64,2432]{1,0:T(8,128)(2,1)S(1)} %constant_dynamic-update-slice_fusion.refs_1_), channel_id=1, source_target_pairs={{0,16},{8,24},{16,0},{24,8},{1,17},{9,25},{17,1},{25,9},{2,18},{10... | collective-permute-start | bytes 933896 | tf_op jit(solution)/shard_map/ppermute | solution.py:180
  89.8 8.9 %collective-permute-start.3 = (bf16[64,2432]{1,0:T(8,128)(2,1)S(1)}, bf16[64,2432]{1,0:T(8,128)(2,1)}, u32[]{:S(2)}, u32[]{:S(2)}) collective-permute-start(bf16[64,2432]{1,0:T(8,128)(2,1)S(1)} %constant_dynamic-update-slice_fusion.refs_1_), channel_id=1, source_target_pairs={{0,8},{8,16},{16,24},{24,0},{1,9},{9,17},{17,25},{25,1},{2,10},{10... | collective-permute-start | bytes 933896 | tf_op jit(solution)/shard_map/ppermute | solution.py:180
  107.4 21.2 %copy-start.5 = (bf16[64,2304]{1,0:T(8,128)(2,1)S(1)}, bf16[64,2304]{1,0:T(8,128)(2,1)}, u32[]{:S(2)}) copy-start(bf16[64,2304]{1,0:T(8,128)(2,1)} %get-tuple-element.21) | copy-start | bytes 884740
  107.4 9.6 %collective-permute-start.15 = (bf16[64,2304]{1,0:T(8,128)(2,1)}, bf16[64,2304]{1,0:T(8,128)(2,1)S(1)}, u32[]{:S(2)}, u32[]{:S(2)}) collective-permute-start(bf16[64,2304]{1,0:T(8,128)(2,1)} %get-tuple-element.18), channel_id=1, source_target_pairs={{0,24},{8,0},{16,8},{24,16},{1,25},{9,1},{17,9},{25,17},{2,26},{10... | collective-permute-start | bytes 884744 | tf_op jit(solution)/shard_map/ppermute | solution.py:180
  107.8 10.6 %collective-permute-start.16 = (bf16[64,2304]{1,0:T(8,128)(2,1)}, bf16[64,2304]{1,0:T(8,128)(2,1)S(1)}, u32[]{:S(2)}, u32[]{:S(2)}) collective-permute-start(bf16[64,2304]{1,0:T(8,128)(2,1)} %get-tuple-element.19), channel_id=1, source_target_pairs={{0,16},{8,24},{16,0},{24,8},{1,17},{9,25},{17,1},{25,9},{2,18},{10... | collective-permute-start | bytes 884744 | tf_op jit(solution)/shard_map/ppermute | solution.py:180
  111.0 9.2 %collective-permute-start.17 = (bf16[64,2304]{1,0:T(8,128)(2,1)}, bf16[64,2304]{1,0:T(8,128)(2,1)S(1)}, u32[]{:S(2)}, u32[]{:S(2)}) collective-permute-start(bf16[64,2304]{1,0:T(8,128)(2,1)} %get-tuple-element.20), channel_id=1, source_target_pairs={{0,8},{8,16},{16,24},{24,0},{1,9},{9,17},{17,25},{25,1},{2,10},{10... | collective-permute-start | bytes 884744 | tf_op jit(solution)/shard_map/ppermute | solution.py:180
  113.0 12.1 %collective-permute-start.21 = (bf16[64,2304]{1,0:T(8,128)(2,1)}, bf16[64,2304]{1,0:T(8,128)(2,1)S(1)}, u32[]{:S(2)}, u32[]{:S(2)}) collective-permute-start(bf16[64,2304]{1,0:T(8,128)(2,1)} %get-tuple-element.22), channel_id=1, source_target_pairs={{0,192},{64,0},{128,64},{192,128},{1,193},{65,1},{129,65},{193,129... | collective-permute-start | bytes 884744 | tf_op jit(solution)/shard_map/ppermute | solution.py:180
  115.6 13.0 %collective-permute-start.22 = (bf16[64,2304]{1,0:T(8,128)(2,1)}, bf16[64,2304]{1,0:T(8,128)(2,1)S(1)}, u32[]{:S(2)}, u32[]{:S(2)}) collective-permute-start(bf16[64,2304]{1,0:T(8,128)(2,1)} %get-tuple-element.23), channel_id=1, source_target_pairs={{0,128},{64,192},{128,0},{192,64},{1,129},{65,193},{129,1},{193,65... | collective-permute-start | bytes 884744 | tf_op jit(solution)/shard_map/ppermute | solution.py:180
  117.0 11.6 %collective-permute-start.23 = (bf16[64,2304]{1,0:T(8,128)(2,1)}, bf16[64,2304]{1,0:T(8,128)(2,1)S(1)}, u32[]{:S(2)}, u32[]{:S(2)}) collective-permute-start(bf16[64,2304]{1,0:T(8,128)(2,1)} %get-tuple-element.24), channel_id=1, source_target_pairs={{0,64},{64,128},{128,192},{192,0},{1,65},{65,129},{129,193},{193,1... | collective-permute-start | bytes 884744 | tf_op jit(solution)/shard_map/ppermute | solution.py:180
  121.3 9.5 %collective-permute-start.18 = (bf16[16,2304]{1,0:T(8,128)(2,1)S(1)}, bf16[16,2304]{1,0:T(8,128)(2,1)S(1)}, u32[]{:S(2)}, u32[]{:S(2)}) collective-permute-start(bf16[16,2304]{1,0:T(8,128)(2,1)S(1)} %get-tuple-element.25), channel_id=1, source_target_pairs={{0,192},{64,0},{128,64},{192,128},{1,193},{65,1},{129,65},{193,129... | collective-permute-start | bytes 221192 | tf_op jit(solution)/shard_map/ppermute | solution.py:180
  125.2 8.9 %collective-permute-start.20 = (bf16[16,2304]{1,0:T(8,128)(2,1)S(1)}, bf16[16,2304]{1,0:T(8,128)(2,1)S(1)}, u32[]{:S(2)}, u32[]{:S(2)}) collective-permute-start(bf16[16,2304]{1,0:T(8,128)(2,1)S(1)} %get-tuple-element.26), channel_id=1, source_target_pairs={{0,64},{64,128},{128,192},{192,0},{1,65},{65,129},{129,193},{193,1... | collective-permute-start | bytes 221192 | tf_op jit(solution)/shard_map/ppermute | solution.py:180
  125.2 8.9 %collective-permute-start.19 = (bf16[16,2304]{1,0:T(8,128)(2,1)S(1)}, bf16[16,2304]{1,0:T(8,128)(2,1)S(1)}, u32[]{:S(2)}, u32[]{:S(2)}) collective-permute-start(bf16[16,2304]{1,0:T(8,128)(2,1)S(1)} %get-tuple-element.27), channel_id=1, source_target_pairs={{0,128},{64,192},{128,0},{192,64},{1,129},{65,193},{129,1},{193,65... | collective-permute-start | bytes 221192 | tf_op jit(solution)/shard_map/ppermute | solution.py:180
  128.8 5.4 %collective-permute-start.24 = (bf16[16,2304]{1,0:T(8,128)(2,1)S(1)}, bf16[16,2304]{1,0:T(8,128)(2,1)S(1)}, u32[]{:S(2)}, u32[]{:S(2)}) collective-permute-start(bf16[16,2304]{1,0:T(8,128)(2,1)S(1)} %get-tuple-element.28), channel_id=1, source_target_pairs={{0,24},{8,0},{16,8},{24,16},{1,25},{9,1},{17,9},{25,17},{2,26},{10... | collective-permute-start | bytes 221192 | tf_op jit(solution)/shard_map/ppermute | solution.py:180
  129.4 5.5 %collective-permute-start.26 = (bf16[16,2304]{1,0:T(8,128)(2,1)S(1)}, bf16[16,2304]{1,0:T(8,128)(2,1)S(1)}, u32[]{:S(2)}, u32[]{:S(2)}) collective-permute-start(bf16[16,2304]{1,0:T(8,128)(2,1)S(1)} %get-tuple-element.29), channel_id=1, source_target_pairs={{0,8},{8,16},{16,24},{24,0},{1,9},{9,17},{17,25},{25,1},{2,10},{10... | collective-permute-start | bytes 221192 | tf_op jit(solution)/shard_map/ppermute | solution.py:180
  130.9 6.3 %collective-permute-start.25 = (bf16[16,2304]{1,0:T(8,128)(2,1)S(1)}, bf16[16,2304]{1,0:T(8,128)(2,1)S(1)}, u32[]{:S(2)}, u32[]{:S(2)}) collective-permute-start(bf16[16,2304]{1,0:T(8,128)(2,1)S(1)} %get-tuple-element.30), channel_id=1, source_target_pairs={{0,16},{8,24},{16,0},{24,8},{1,17},{9,25},{17,1},{25,9},{2,18},{10... | collective-permute-start | bytes 221192 | tf_op jit(solution)/shard_map/ppermute | solution.py:180
  (8 other events, 91.4 us)

commit v2 on v1

v2 whole, which is shorter than its diff:
```python
import jax
import jax.numpy as jnp
from jax import lax
from jax.experimental import pallas as pl
from jax.experimental.pallas import tpu as pltpu
from jax.sharding import Mesh, PartitionSpec as P

HEADS = 36
HEAD_DIM = 64
PAGE = 128
D = HEADS * HEAD_DIM
HP = 48
LW = 128
GROUP = 4
W = D + LW
NEG_FILL = -1e30
NORM_EPS = 1e-06
F32 = jnp.float32
BF16 = jnp.bfloat16


def dot(a, b, ca=1, cb=0):
    return lax.dot_general(a, b, (((ca,), (cb,)), ((), ())), preferred_element_type=F32)


def head_mask(rows, cols):
    row = lax.broadcasted_iota(jnp.int32, (rows, cols), 0)
    col = lax.broadcasted_iota(jnp.int32, (rows, cols), 1)
    return (col >= row * HEAD_DIM) & (col < (row + 1) * HEAD_DIM)


def placed(part, shape, axis):
    head = lax.broadcasted_iota(jnp.int32, shape, axis)
    lane = lax.broadcasted_iota(jnp.int32, shape, 1 - axis)
    return ((lane == head + part * HEADS) & (head < HEADS)).astype(BF16)


def halves(value):
    high = value.astype(BF16)
    return high, (value - high.astype(F32)).astype(BF16)


def packed(lse):
    first = lse.astype(BF16)
    second, third = halves(lse - first.astype(F32))
    return (
        dot(first, placed(0, (HP, LW), 0))
        + dot(second, placed(1, (HP, LW), 0))
        + dot(third, placed(2, (HP, LW), 0))
    ).astype(BF16)


def unpacked(lanes):
    return dot(lanes, placed(0, (LW, HP), 1) + placed(1, (LW, HP), 1) + placed(2, (LW, HP), 1))


def spread_heads():
    return head_mask(HP, D).astype(F32).astype(BF16)


def combined(values, lses, spread):
    peak = lses[0]
    for lse in lses[1:]:
        peak = jnp.maximum(peak, lse)
    shares = [jnp.exp(lse - peak) for lse in lses]
    whole = shares[0]
    for share in shares[1:]:
        whole = whole + share
    total = None
    for share, value in zip(shares, values):
        high, low = halves(share / whole)
        term = (dot(high, spread) + dot(low, spread)) * value.astype(F32)
        total = term if total is None else total + term
    return total, peak + jnp.log(whole)


def wanted_rows(tall, rows, core):
    line = lax.broadcasted_iota(jnp.int32, (tall, rows), 0)
    slot = lax.broadcasted_iota(jnp.int32, (tall, rows), 1)
    k = line % (rows // 2)
    here = 8 * (k // 4) + 4 * jnp.where(line < rows // 2, core, 1 - core) + k % 4
    return line, slot == here


def attn_kernel(
    q_ref, table_ref, len_ref, flag_ref, res_ref, routes_ref, gates_ref, k_hbm, v_hbm,
    own_ref, other_ref, split_ref, kbuf, vbuf, obuf, ksem, vsem,
):
    pages = k_hbm.shape[0]
    rows = q_ref.shape[0]
    for p in range(pages):
        pltpu.make_async_copy(k_hbm.at[p], kbuf.at[p], ksem.at[p]).start()
    for p in range(pages):
        pltpu.make_async_copy(v_hbm.at[p], vbuf.at[p], vsem.at[p]).start()
    core = lax.axis_index("c")
    first = (lax.axis_index("zl") * 2 + core) * pages
    table = table_ref[...]
    line = lax.broadcasted_iota(jnp.int32, table.shape, 0)
    step = lax.broadcasted_iota(jnp.int32, table.shape, 1)
    length = jnp.sum(jnp.where(line == step, len_ref[...].astype(F32), 0.0), axis=1, keepdims=True)
    remain = jnp.clip(length - (step * PAGE).astype(F32), 0.0, float(PAGE))
    lane = lax.broadcasted_iota(jnp.int32, (rows, pages), 1)
    owner = jnp.zeros((rows, pages), F32)
    seen = []
    for p in range(pages):
        match = jnp.where(table == first + p, remain, 0.0)
        per_row = jnp.sum(match, axis=1, keepdims=True)
        seen.append(jnp.sum(per_row, axis=0, keepdims=True).astype(jnp.int32))
        owner = jnp.where((lane == p) & (per_row > 0), 1.0, owner)
    own = res_ref.shape[0]
    spot = lax.broadcasted_iota(jnp.int32, (own, LW), 1)
    square = lax.broadcasted_iota(jnp.int32, (own, own), 0) == lax.broadcasted_iota(jnp.int32, (own, own), 1)
    coefs = jnp.zeros((own, LW), F32)
    for k in range(2):
        route, gate = (
            jnp.sum(jnp.where(square, ref[k : k + 1, :].astype(F32), 0.0), axis=1, keepdims=True)
            for ref in (routes_ref, gates_ref)
        )
        coefs = coefs + jnp.where(spot == route.astype(jnp.int32), gate, 0.0)
    own_ref[rows // 2 : rows // 2 + own, :D] = res_ref[...]
    own_ref[rows // 2 : rows // 2 + own, D:] = coefs.astype(BF16)
    own_ref[rows // 2 + own :, :] = jnp.zeros((own_ref.shape[0] - rows // 2 - own, W), BF16)
    owner_b = owner.astype(BF16)
    q_sel = dot(owner_b, q_ref[...], 0, 0)
    mask = head_mask(HP, D)
    spread = mask.astype(F32).astype(BF16)
    token = lax.broadcasted_iota(jnp.int32, (PAGE, HP), 0)
    tops, sums, weights = [], [], []
    for p0 in range(0, pages, GROUP):
        for p in range(p0, p0 + GROUP):
            pltpu.make_async_copy(k_hbm.at[p], kbuf.at[p], ksem.at[p]).wait()
        for p in range(p0, p0 + GROUP):
            q_diag = jnp.where(mask, q_sel[p : p + 1, :], 0.0).astype(BF16)
            scores = dot(kbuf[p], q_diag, 1, 1) * HEAD_DIM**-0.5
            visible = token < seen[p]
            scores = jnp.where(visible, scores, NEG_FILL)
            top = jnp.max(scores, axis=0, keepdims=True)
            terms = jnp.where(visible, jnp.exp(scores - top), 0.0)
            tops.append(top)
            sums.append(jnp.sum(terms, axis=0, keepdims=True))
            weights.append(terms.astype(BF16))
    for p0 in range(0, pages, GROUP):
        for p in range(p0, p0 + GROUP):
            pltpu.make_async_copy(v_hbm.at[p], vbuf.at[p], vsem.at[p]).wait()
        for p in range(p0, p0 + GROUP):
            mixed = dot(weights[p], vbuf[p], 0, 0)
            obuf[p : p + 1, :] = jnp.sum(jnp.where(mask, mixed, 0.0), axis=0, keepdims=True)
    top = jnp.concatenate(tops, axis=0)
    total = jnp.concatenate(sums, axis=0)
    total = jnp.where(total > 0, total, 1.0)
    lse = top + jnp.log(total)
    same = dot(owner_b, owner_b, 0, 0)
    peak = jnp.full(lse.shape, NEG_FILL, F32)
    for p in range(pages):
        peak = jnp.maximum(peak, jnp.where(same[:, p : p + 1] > 0, lse[p : p + 1, :], NEG_FILL))
    share = jnp.exp(lse - peak)
    whole = jnp.zeros(lse.shape, F32)
    for p in range(pages):
        whole = whole + jnp.where(same[:, p : p + 1] > 0, share[p : p + 1, :], 0.0)
    whole = jnp.where(whole > 0, whole, 1.0)
    high, low = halves(share / (whole * total))
    scaled = (dot(high, spread) + dot(low, spread)) * obuf[...]
    joint = peak + jnp.log(whole)
    half = rows // 2
    tall = rows + split_ref.shape[0]
    line, wanted = wanted_rows(tall, rows, core)
    choice = jnp.where(line < rows, wanted.astype(F32), flag_ref[...].astype(F32))
    chosen = dot(choice.astype(BF16), owner_b)
    chosen_b = chosen.astype(BF16)
    high, low = halves(scaled)
    values = (dot(chosen_b, high) + dot(chosen_b, low)).astype(BF16)
    row_lse = jnp.full((tall, HP), NEG_FILL, F32)
    for p in range(pages):
        row_lse = jnp.maximum(row_lse, jnp.where(chosen[:, p : p + 1] > 0, joint[p : p + 1, :], NEG_FILL))
    lanes = packed(row_lse)
    own_ref[:half, :D] = values[:half, :]
    own_ref[:half, D:] = lanes[:half, :]
    other_ref[:, :D] = values[half:rows, :]
    other_ref[:, D:] = lanes[half:rows, :]
    split_ref[:, :D] = values[rows:, :]
    split_ref[:, D:] = lanes[rows:, :]


def chip_kernel(
    own_ref, other_ref, far_0_ref, far_1_ref, flag_ref, out_ref
):
    half = other_ref.shape[0]
    _, wanted = wanted_rows(half, 2 * half, lax.axis_index("c"))
    flag = jnp.sum(jnp.where(wanted, flag_ref[...].astype(F32), 0.0), axis=1, keepdims=True) > 0
    values = [own_ref[:half, :D], other_ref[:, :D]]
    lses = [unpacked(own_ref[:half, D:]), unpacked(other_ref[:, D:])]
    for far in (far_0_ref, far_1_ref):
        values.append(far[0:1, :D])
        lses.append(jnp.where(flag, unpacked(far[:, D:])[0:1, :], NEG_FILL))
    total, lse = combined(values, lses, spread_heads())
    out_ref[:half, :D] = total.astype(BF16)
    out_ref[:half, D:] = packed(lse)
    out_ref[half:, :] = own_ref[half:, :]


def norm_kernel(p0, p1, p2, p3, gain_ref, attn_ref, out_ref):
    parts = (p0, p1, p2, p3)
    rows = out_ref.shape[0]
    own = attn_ref.shape[0]
    total, _ = combined(
        [part[:rows, :D] for part in parts],
        [unpacked(part[:rows, D:]) for part in parts],
        spread_heads(),
    )
    line = lax.broadcasted_iota(jnp.int32, (rows, rows), 0)
    slot = lax.broadcasted_iota(jnp.int32, (rows, rows), 1)
    source = (lax.axis_index("zl") + 4 - line // own) % 4
    turn = (slot == own * source + line % own).astype(F32).astype(BF16)
    attn = dot(turn, total.astype(BF16))
    attn_ref[...] = attn[:own, :].astype(BF16)
    extra = jnp.concatenate([part[rows : rows + own, :].astype(F32) for part in parts], axis=0)
    stream = extra[:, :D] + attn
    normed = stream * lax.rsqrt(jnp.mean(stream * stream, axis=-1, keepdims=True) + NORM_EPS)
    out_ref[:, :D] = (normed * gain_ref[...].astype(F32)).astype(BF16)
    out_ref[:, D:] = extra[:, D:].astype(BF16)


def hold_kernel(*refs):
    count = len(refs) // 2
    for source, target in zip(refs[:count], refs[count:]):
        target[...] = source[...]


def mlp_kernel(x_ref, gate_0, up_0, down_0, gate_1, up_1, down_1, out_ref):
    x = x_ref[:, :D]
    coefs = x_ref[:, D:].astype(F32)
    lane = lax.broadcasted_iota(jnp.int32, coefs.shape, 1)
    mine = lax.axis_index("zl") * 2 + lax.axis_index("c")
    theirs = lax.axis_index("zl") * 2 + 1 - lax.axis_index("c")
    result = None
    for expert, gate, up, down in ((mine, gate_0, up_0, down_0), (theirs, gate_1, up_1, down_1)):
        coef = jnp.sum(jnp.where(lane == expert, coefs, 0.0), axis=1, keepdims=True)
        g = dot(x, gate[...], 1, 1)
        u = dot(x, up[...], 1, 1)
        inner = ((g / (1.0 + jnp.exp(-g))) * u * coef).astype(BF16)
        y = dot(inner, down[...])
        result = y if result is None else result + y
    out_ref[...] = result.astype(BF16)


def join_kernel(*refs):
    out_ref = refs[-1]
    size = refs[0].shape[0]
    for i, ref in enumerate(refs[:-1]):
        out_ref[size * i : size * (i + 1), :] = ref[...]


def vmem(mib):
    return pltpu.CompilerParams(vmem_limit_bytes=mib * 1024 * 1024)


VMEM_SPEC = pl.BlockSpec(memory_space=pltpu.VMEM)
HBM_SPEC = pl.BlockSpec(memory_space=pl.ANY)
PLANE = ("x", "yh", "yp", "c")


def flipped(array, axis, n=2):
    return lax.ppermute(array, axis, [(i, n - 1 - i) for i in range(n)])


def mirrored(array):
    return lax.ppermute(array, ("zh", "zl"), [(i, 7 - i) for i in range(8)])


def along_line(array, shift, n=4):
    return lax.ppermute(array, "zl", [(i, (i + shift) % n) for i in range(n)])


def along_plane(array, shift, wide, n=4):
    pairs = []
    for x in range(n):
        for y in range(n):
            for c in range(2):
                on_y = (c == 0) == wide
                to_x, to_y = (x, (y + shift) % n) if on_y else ((x + shift) % n, y)
                pairs.append(((x * n + y) * 2 + c, (to_x * n + to_y) * 2 + c))
    return lax.ppermute(array, PLANE, pairs)


def joined(*blocks):
    rows = sum(block.shape[0] for block in blocks)
    return pl.pallas_call(
        join_kernel,
        out_shape=jax.ShapeDtypeStruct((rows, W), BF16),
        compiler_params=vmem(8),
        name="join",
    )(*blocks)


def summed(blocks):
    total = blocks[0].astype(F32)
    for block in blocks[1:]:
        total = total + block.astype(F32)
    return total.astype(BF16)


def pieces(array):
    size = array.shape[0] // 4
    return [array[size * i : size * (i + 1)] for i in range(4)]


NEAR = (1, 3, 2)
WIDE = (2, 3, 1)


def on_device(
    queries, residual, gain, key_pages, value_pages, page_table, lengths, split_flag, routes, gates,
    w_gate, w_up, w_down,
):
    own = residual.shape[0]
    rows = queries.shape[0]
    half = rows // 2
    pages = key_pages.shape[0]
    mine = (w_gate[0].T, w_up[0].T, w_down[0])
    theirs = tuple(flipped(w, "c") for w in mine)
    flag_row = split_flag.reshape(1, rows)

    here, there, split = pl.pallas_call(
        attn_kernel,
        out_shape=(
            jax.ShapeDtypeStruct((half + 8, W), BF16),
            jax.ShapeDtypeStruct((half, W), BF16),
            jax.ShapeDtypeStruct((8, W), BF16),
        ),
        in_specs=[VMEM_SPEC] * 7 + [HBM_SPEC] * 2,
        scratch_shapes=[
            pltpu.VMEM((pages, PAGE, D), BF16),
            pltpu.VMEM((pages, PAGE, D), BF16),
            pltpu.VMEM((pages, D), F32),
            pltpu.SemaphoreType.DMA((pages,)),
            pltpu.SemaphoreType.DMA((pages,)),
        ],
        compiler_params=vmem(60),
        cost_estimate=pl.CostEstimate(flops=2 * 10**9, bytes_accessed=10**7, transcendentals=10**6),
        name="attn",
    )(
        queries, page_table, lengths.reshape(1, rows), flag_row, residual, routes.T, gates.T,
        key_pages, value_pages,
    )
    here, there, split, theirs = lax.optimization_barrier((here, there, split, theirs))
    across = flipped(there, "c")
    far_0 = flipped(split, "yp")
    far_1 = lax.ppermute(split, ("yp", "c"), [(i, 3 - i) for i in range(4)])
    chip = pl.pallas_call(
        chip_kernel,
        out_shape=jax.ShapeDtypeStruct((half + 8, W), BF16),
        compiler_params=vmem(8),
        name="chip",
    )(here, across, far_0, far_1, flag_row)
    chip, mine, theirs = lax.optimization_barrier((chip, mine, theirs))
    weights = pl.pallas_call(
        hold_kernel,
        out_shape=[jax.ShapeDtypeStruct(w.shape, BF16) for w in mine + theirs],
        in_specs=[VMEM_SPEC] * 6,
        compiler_params=vmem(16),
        name="hold",
    )(*mine, *theirs)
    attn, normed = pl.pallas_call(
        norm_kernel,
        out_shape=(jax.ShapeDtypeStruct((own, D), BF16), jax.ShapeDtypeStruct((half, W), BF16)),
        compiler_params=vmem(8),
        name="norm",
    )(chip, *[along_line(chip, s) for s in (1, 2, 3)], gain.reshape(1, D))

    def mlp(block):
        return pl.pallas_call(
            mlp_kernel,
            out_shape=jax.ShapeDtypeStruct((block.shape[0], D), BF16),
            compiler_params=vmem(16),
            cost_estimate=pl.CostEstimate(flops=3 * 10**9, bytes_accessed=10**7, transcendentals=10**5),
            name="mlp",
        )(block, *weights)

    group = joined(normed, mirrored(normed))
    line = joined(group, *[along_plane(group, s, False) for s in NEAR])
    blocks = [along_plane(line, s, True) for s in WIDE]
    first = mlp(line)
    results = [mlp(block) for block in blocks]
    back = [along_plane(result, -s, True) for s, result in zip(WIDE, results)]
    parts = pieces(summed([first] + back))
    total = summed(parts[:1] + [along_plane(part, -s, False) for s, part in zip(NEAR, parts[1:])])
    total = summed([total[:half], mirrored(total[half:])])
    parts = pieces(total)
    return summed(parts[:1] + [along_line(part, -s) for s, part in zip((1, 2, 3), parts[1:])] + [attn])


def solution(mesh):
    fine = Mesh(mesh.devices.reshape(4, 2, 2, 2, 4, 2), ("x", "zh", "yh", "yp", "zl", "c"))
    grp = ("x", "zh", "yh", "yp")
    ep = ("zl", "c")
    in_specs = (
        P(grp, None),
        P(grp + ep, None),
        P(),
        P(grp + ep, None, None),
        P(grp + ep, None, None),
        P(grp, None),
        P(grp),
        P(grp),
        P(grp + ep, None),
        P(grp + ep, None),
        P(ep, None, grp),
        P(ep, None, grp),
        P(ep, grp, None),
    )
    return jax.shard_map(
        on_device, mesh=fine, in_specs=in_specs, out_specs=P(grp + ep, None), check_vma=False
    )
```

time: 152 us -> 111 us (0.73)
  starting transfers between devices: 50.3 us -> 35.5 us
  local copies, waits for them, and re-layouts: 13.6 us -> 0.99 us
  blocking collectives: 11.6 us -> 0 us
  waiting for transfers between devices: 48.3 us -> 55.9 us
  Pallas kernels: 21.1 us -> 16.5 us
  other arithmetic: 4.46 us -> 1.05 us
    ppermute x27 -> x26, waiting for transfers between devices: 30.5 us -> 55.9 us  [the longest x12 33.8 us: along_plane(): return lax.ppermute(array, PLANE, pairs)]
    all_to_all x2 -> x0, waiting for transfers between devices: 17.8 us -> none  [the longest x1 9.03 us: on_device(): stacked = lax.all_to_all(normed, Z, 0, 0, tiled=True)]
    all_to_all x2 -> x0, starting transfers between devices: 12.6 us -> none  [the longest x1 6.85 us: on_device(): arrived = lax.all_to_all(both, ('yp', 'zl', 'c'), 0, 0, tiled=True)]
    all_to_all x1 -> x0, blocking collectives: 11.6 us -> none  [on_device(): returned = lax.all_to_all(outgoing, Z, 0, 0, tiled=True).reshape(-1, own, D)]
    pallas_call x3 -> x10, Pallas kernels: 21.1 us -> 16.5 us  [the longest x1 7.84 us: on_device(): pl.pallas_call(attn_kernel, out_shape=(jax.ShapeDtypeStruct((half + 8, W)...]
    ppermute x2 -> x0, local copies, waits for them, and re-layouts: 3.76 us -> none  [on_device(): theirs = tuple((lax.ppermute(w, 'c', swap) for w in mine))]
    all_to_all x4 -> x0, local copies, waits for them, and re-layouts: 3.24 us -> none  [the longest x1 1.61 us: on_device(): stacked = lax.all_to_all(normed, Z, 0, 0, tiled=True)]
    ppermute x27 -> x26, starting transfers between devices: 37.7 us -> 35.5 us  [the longest x12 14 us: along_plane(): return lax.ppermute(array, PLANE, pairs)]
  transfers between devices with their start and end apart: 29 -> 26, of which waited for: 10 -> 19; matrix products, arithmetic and copies ran while one was open for 8% -> 0% of each run, Pallas kernels for 0% -> 14%
where the time goes in v2:
time: 111 us; the launch traced here: 110 us
  waiting for transfers between devices  55.9 us (50%)
  starting transfers between devices  35.5 us (32%)
  Pallas kernels  16.5 us (15%)
    ppermute x12, waiting for transfers between devices, along_plane(): return lax.ppermute(array, PLANE, pairs)  33.8 us
    ppermute x12, starting transfers between devices, along_plane(): return lax.ppermute(array, PLANE, pairs)  14 us
    ppermute x6, waiting for transfers between devices, along_line(): return lax.ppermute(array, 'zl', [(i, (i + shift) % n) for i in range(n)])  10.9 us
    ppermute x6, starting transfers between devices, along_line(): return lax.ppermute(array, 'zl', [(i, (i + shift) % n) for i in range(n)])  10.2 us
    ppermute x2, starting transfers between devices, mirrored(): return lax.ppermute(array, ('zh', 'zl'), [(i, 7 - i) for i in range(8)])  8.83 us
    pallas_call x1, Pallas kernels, on_device(): pl.pallas_call(attn_kernel, out_shape=(jax.ShapeDtypeStruct((half + 8, W)...  7.84 us
    ppermute x2, waiting for transfers between devices, mirrored(): return lax.ppermute(array, ('zh', 'zl'), [(i, 7 - i) for i in range(8)])  7.29 us
    pallas_call x4, Pallas kernels, mlp(): pl.pallas_call(mlp_kernel, out_shape=jax.ShapeDtypeStruct((block.shape[0]...  6.82 us
  transfers between devices with their start and end apart: 26, of which 19 were waited for; matrix products, arithmetic and copies ran while one was open for 0% of the time, Pallas kernels for 14%

profile of v2, /device:TPU:16, one launch (start us, length us, event | category | flops | bytes accessed | tf_op | source)
XLA Modules:
  0.0 110.1 jit_solution(14323881627265572471)
XLA Ops:
  0.5 7.8 %attn.1 = (bf16[24,2432]{1,0:T(8,128)(2,1)}, bf16[16,2432]{1,0:T(8,128)(2,1)}, bf16[8,2432]{1,0:T(8,128)(2,1)}) custom-call(bf16[32,2304]{1,0:T(8,128)(2,1)} %q_ref.1, s32[32,32]{1,0:T(8,128)} %table_ref.1, s32[1,32]{1,0:T(1,128)} %bitcast.20, s32[1,32]{1,0:T(1,128)} %bitcast.17, bf16[4,2304]{1,0:T(4,128)(2,1)} %res_ref.1, s32[2,4]{1,0:T(2,128)} %bitcast.19, ...), custom_call_target="tpu_custom_call" | custom-call | flops 2000000000 | bytes 10000000 | tf_op jit(solution)/shard_map/attn/pallas_call | solution.py:323
  9.0 1.3 %collective-permute-start.4 = (bf16[8,2432]{1,0:T(8,128)(2,1)}, bf16[8,2432]{1,0:T(8,128)(2,1)S(1)}, u32[]{:S(2)}, u32[]{:S(2)}) collective-permute-start(bf16[8,2432]{1,0:T(8,128)(2,1)} %get-tuple-element.34), channel_id=1, source_target_pairs={{0,8},{8,0},{1,9},{9,1},{2,10},{10,2},{3,11},{11,3},{4,12},{12,4},... | collective-permute-start | bytes 116744 | tf_op jit(solution)/shard_map/ppermute | solution.py:263
  10.5 2.7 %collective-permute-done.4.far_0_ref = bf16[8,2432]{1,0:T(8,128)(2,1)S(1)} collective-permute-done((bf16[8,2432]{1,0:T(8,128)(2,1)}, bf16[8,2432]{1,0:T(8,128)(2,1)S(1)}, u32[]{:S(2)}, u32[]{:S(2)}) %collective-permute-start.4) | collective-permute-done | bytes 38944 | tf_op jit(solution)/shard_map/ppermute | solution.py:263
  15.9 2.0 %collective-permute-start.6 = (bf16[24,2432]{1,0:T(8,128)(2,1)S(1)}, bf16[24,2432]{1,0:T(8,128)(2,1)S(1)}, u32[]{:S(2)}, u32[]{:S(2)}) collective-permute-start(bf16[24,2432]{1,0:T(8,128)(2,1)S(1)} %chip.1.p0), channel_id=1, source_target_pairs={{0,2},{2,4},{4,6},{6,0},{1,3},{3,5},{5,7},{7,1},{8,10},{10,12},{12... | collective-permute-start | bytes 350216 | tf_op jit(solution)/shard_map/ppermute | solution.py:271
  17.9 3.3 %collective-permute-start.7 = (bf16[24,2432]{1,0:T(8,128)(2,1)S(1)}, bf16[24,2432]{1,0:T(8,128)(2,1)S(1)}, u32[]{:S(2)}, u32[]{:S(2)}) collective-permute-start(bf16[24,2432]{1,0:T(8,128)(2,1)S(1)} %chip.1.p0), channel_id=1, source_target_pairs={{0,4},{2,6},{4,0},{6,2},{1,5},{3,7},{5,1},{7,3},{8,12},{10,14},{12... | collective-permute-start | bytes 350216 | tf_op jit(solution)/shard_map/ppermute | solution.py:271
  22.1 2.5 %collective-permute-done.6.p1 = bf16[24,2432]{1,0:T(8,128)(2,1)S(1)} collective-permute-done((bf16[24,2432]{1,0:T(8,128)(2,1)S(1)}, bf16[24,2432]{1,0:T(8,128)(2,1)S(1)}, u32[]{:S(2)}, u32[]{:S(2)}) %collective-permute-start.6) | collective-permute-done | bytes 116768 | tf_op jit(solution)/shard_map/ppermute | solution.py:271
  24.6 4.5 %collective-permute-done.7.p2 = bf16[24,2432]{1,0:T(8,128)(2,1)S(1)} collective-permute-done((bf16[24,2432]{1,0:T(8,128)(2,1)S(1)}, bf16[24,2432]{1,0:T(8,128)(2,1)S(1)}, u32[]{:S(2)}, u32[]{:S(2)}) %collective-permute-start.7) | collective-permute-done | bytes 116768 | tf_op jit(solution)/shard_map/ppermute | solution.py:271
  29.9 5.9 %collective-permute-start.9 = (bf16[16,2432]{1,0:T(8,128)(2,1)S(1)}, bf16[16,2432]{1,0:T(8,128)(2,1)S(1)}, u32[]{:S(2)}, u32[]{:S(2)}) collective-permute-start(bf16[16,2432]{1,0:T(8,128)(2,1)S(1)} %get-tuple-element.39.refs_0_), channel_id=1, source_target_pairs={{0,38},{2,36},{4,34},{6,32},{32,6},{34,4},{36,2},{38,0},{1,39},{3,... | collective-permute-start | bytes 233480 | tf_op jit(solution)/shard_map/ppermute | solution.py:267
  35.9 3.9 %collective-permute-done.9.refs_1_ = bf16[16,2432]{1,0:T(8,128)(2,1)S(1)} collective-permute-done((bf16[16,2432]{1,0:T(8,128)(2,1)S(1)}, bf16[16,2432]{1,0:T(8,128)(2,1)S(1)}, u32[]{:S(2)}, u32[]{:S(2)}) %collective-permute-start.9) | collective-permute-done | bytes 77856 | tf_op jit(solution)/shard_map/ppermute | solution.py:267
  39.8 1.6 %collective-permute-start.10 = (bf16[32,2432]{1,0:T(8,128)(2,1)S(1)}, bf16[32,2432]{1,0:T(8,128)(2,1)S(1)}, u32[]{:S(2)}, u32[]{:S(2)}) collective-permute-start(bf16[32,2432]{1,0:T(8,128)(2,1)S(1)} %join.2.refs_0_), channel_id=1, source_target_pairs={{0,64},{1,9},{8,72},{9,17},{16,80},{17,25},{24,88},{25,1},{64,128}... | collective-permute-start | bytes 466952 | tf_op jit(solution)/shard_map/ppermute | solution.py:282
  41.3 1.7 %collective-permute-start.11 = (bf16[32,2432]{1,0:T(8,128)(2,1)S(1)}, bf16[32,2432]{1,0:T(8,128)(2,1)S(1)}, u32[]{:S(2)}, u32[]{:S(2)}) collective-permute-start(bf16[32,2432]{1,0:T(8,128)(2,1)S(1)} %join.2.refs_0_), channel_id=1, source_target_pairs={{0,192},{1,25},{8,200},{9,1},{16,208},{17,9},{24,216},{25,17},{64,... | collective-permute-start | bytes 466952 | tf_op jit(solution)/shard_map/ppermute | solution.py:282
  43.1 1.8 %collective-permute-start.12 = (bf16[32,2432]{1,0:T(8,128)(2,1)S(1)}, bf16[32,2432]{1,0:T(8,128)(2,1)S(1)}, u32[]{:S(2)}, u32[]{:S(2)}) collective-permute-start(bf16[32,2432]{1,0:T(8,128)(2,1)S(1)} %join.2.refs_0_), channel_id=1, source_target_pairs={{0,128},{1,17},{8,136},{9,25},{16,144},{17,1},{24,152},{25,9},{64,... | collective-permute-start | bytes 466952 | tf_op jit(solution)/shard_map/ppermute | solution.py:282
  44.9 1.4 %collective-permute-done.10.refs_1_ = bf16[32,2432]{1,0:T(8,128)(2,1)S(1)} collective-permute-done((bf16[32,2432]{1,0:T(8,128)(2,1)S(1)}, bf16[32,2432]{1,0:T(8,128)(2,1)S(1)}, u32[]{:S(2)}, u32[]{:S(2)}) %collective-permute-start.10) | collective-permute-done | bytes 155680 | tf_op jit(solution)/shard_map/ppermute | solution.py:282
  46.6 4.5 %collective-permute-done.12.refs_3_ = bf16[32,2432]{1,0:T(8,128)(2,1)S(1)} collective-permute-done((bf16[32,2432]{1,0:T(8,128)(2,1)S(1)}, bf16[32,2432]{1,0:T(8,128)(2,1)S(1)}, u32[]{:S(2)}, u32[]{:S(2)}) %collective-permute-start.12) | collective-permute-done | bytes 155680 | tf_op jit(solution)/shard_map/ppermute | solution.py:282
  53.8 9.4 %collective-permute-done.13.x_ref = bf16[128,2432]{1,0:T(8,128)(2,1)S(1)} collective-permute-done((bf16[128,2432]{1,0:T(8,128)(2,1)S(1)}, bf16[128,2432]{1,0:T(8,128)(2,1)S(1)}, u32[]{:S(2)}, u32[]{:S(2)}) %collective-permute-start.13) | collective-permute-done | bytes 622624 | tf_op jit(solution)/shard_map/ppermute | solution.py:282
  63.2 1.7 %mlp.5 = bf16[128,2304]{1,0:T(8,128)(2,1)S(1)} custom-call(bf16[128,2432]{1,0:T(8,128)(2,1)S(1)} %collective-permute-done.13.x_ref, bf16[180,2304]{1,0:T(8,128)(2,1)S(1)} %get-tuple-element.46.gate_0, bf16[180,2304]{1,0:T(8,128)(2,1)S(1)} %get-tuple-element.47.up_0, bf16[180,2304]{1,0:T(8,128)(2,1)S(1)} %get-tuple-element.48.down_0, ...), custom_call_target="tpu_custom_call" | custom-call | flops 3000000000 | bytes 10000000 | tf_op jit(solution)/shard_map/mlp/pallas_call | solution.py:371
  65.0 1.9 %collective-permute-done.15.x_ref = bf16[128,2432]{1,0:T(8,128)(2,1)S(1)} collective-permute-done((bf16[128,2432]{1,0:T(8,128)(2,1)S(1)}, bf16[128,2432]{1,0:T(8,128)(2,1)S(1)}, u32[]{:S(2)}, u32[]{:S(2)}) %collective-permute-start.15) | collective-permute-done | bytes 622624 | tf_op jit(solution)/shard_map/ppermute | solution.py:282
  66.9 1.7 %mlp.6 = bf16[128,2304]{1,0:T(8,128)(2,1)S(1)} custom-call(bf16[128,2432]{1,0:T(8,128)(2,1)S(1)} %collective-permute-done.15.x_ref, bf16[180,2304]{1,0:T(8,128)(2,1)S(1)} %get-tuple-element.46.gate_0, bf16[180,2304]{1,0:T(8,128)(2,1)S(1)} %get-tuple-element.47.up_0, bf16[180,2304]{1,0:T(8,128)(2,1)S(1)} %get-tuple-element.48.down_0, ...), custom_call_target="tpu_custom_call" | custom-call | flops 3000000000 | bytes 10000000 | tf_op jit(solution)/shard_map/mlp/pallas_call | solution.py:371
  68.6 2.6 %collective-permute-start.16 = (bf16[128,2304]{1,0:T(8,128)(2,1)S(1)}, bf16[128,2304]{1,0:T(8,128)(2,1)S(1)}, u32[]{:S(2)}, u32[]{:S(2)}) collective-permute-start(bf16[128,2304]{1,0:T(8,128)(2,1)S(1)} %mlp.6), channel_id=1, source_target_pairs={{0,8},{1,65},{8,16},{9,73},{16,24},{17,81},{24,0},{25,89},{64,72},... | collective-permute-start | bytes 1769480 | tf_op jit(solution)/shard_map/ppermute | solution.py:282
  71.2 1.7 %mlp.7 = bf16[128,2304]{1,0:T(8,128)(2,1)S(1)} custom-call(bf16[128,2432]{1,0:T(8,128)(2,1)S(1)} %collective-permute-done.17.x_ref, bf16[180,2304]{1,0:T(8,128)(2,1)S(1)} %get-tuple-element.46.gate_0, bf16[180,2304]{1,0:T(8,128)(2,1)S(1)} %get-tuple-element.47.up_0, bf16[180,2304]{1,0:T(8,128)(2,1)S(1)} %get-tuple-element.48.down_0, ...), custom_call_target="tpu_custom_call" | custom-call | flops 3000000000 | bytes 10000000 | tf_op jit(solution)/shard_map/mlp/pallas_call | solution.py:371
  73.0 1.7 %mlp.4 = bf16[128,2304]{1,0:T(8,128)(2,1)S(1)} custom-call(bf16[128,2432]{1,0:T(8,128)(2,1)S(1)} %join.3.x_ref, bf16[180,2304]{1,0:T(8,128)(2,1)S(1)} %get-tuple-element.46.gate_0, bf16[180,2304]{1,0:T(8,128)(2,1)S(1)} %get-tuple-element.47.up_0, bf16[180,2304]{1,0:T(8,128)(2,1)S(1)} %get-tuple-element.48.down_0, ...), custom_call_target="tpu_custom_call" | custom-call | flops 3000000000 | bytes 10000000 | tf_op jit(solution)/shard_map/mlp/pallas_call | solution.py:371
  74.7 1.8 %collective-permute-done.14 = bf16[128,2304]{1,0:T(8,128)(2,1)S(1)} collective-permute-done((bf16[128,2304]{1,0:T(8,128)(2,1)S(1)}, bf16[128,2304]{1,0:T(8,128)(2,1)S(1)}, u32[]{:S(2)}, u32[]{:S(2)}) %collective-permute-start.14) | collective-permute-done | bytes 589856 | tf_op jit(solution)/shard_map/ppermute | solution.py:282
  76.5 8.3 %collective-permute-done.16 = bf16[128,2304]{1,0:T(8,128)(2,1)S(1)} collective-permute-done((bf16[128,2304]{1,0:T(8,128)(2,1)S(1)}, bf16[128,2304]{1,0:T(8,128)(2,1)S(1)}, u32[]{:S(2)}, u32[]{:S(2)}) %collective-permute-start.16) | collective-permute-done | bytes 589856 | tf_op jit(solution)/shard_map/ppermute | solution.py:282
  88.5 1.6 %collective-permute-start.21 = (bf16[32,2304]{1,0:T(8,128)(2,1)S(1)}, bf16[32,2304]{1,0:T(8,128)(2,1)S(1)}, u32[]{:S(2)}, u32[]{:S(2)}) collective-permute-start(bf16[32,2304]{1,0:T(8,128)(2,1)S(1)} %get-tuple-element.54), channel_id=1, source_target_pairs={{0,128},{1,17},{8,136},{9,25},{16,144},{17,1},{24,152},{25,9},{64,... | collective-permute-start | bytes 442376 | tf_op jit(solution)/shard_map/ppermute | solution.py:282
  90.1 1.5 %collective-permute-done.19 = bf16[32,2304]{1,0:T(8,128)(2,1)S(1)} collective-permute-done((bf16[32,2304]{1,0:T(8,128)(2,1)S(1)}, bf16[32,2304]{1,0:T(8,128)(2,1)S(1)}, u32[]{:S(2)}, u32[]{:S(2)}) %collective-permute-start.19) | collective-permute-done | bytes 147488 | tf_op jit(solution)/shard_map/ppermute | solution.py:282
  91.6 2.0 %collective-permute-done.20 = bf16[32,2304]{1,0:T(8,128)(2,1)S(1)} collective-permute-done((bf16[32,2304]{1,0:T(8,128)(2,1)S(1)}, bf16[32,2304]{1,0:T(8,128)(2,1)S(1)}, u32[]{:S(2)}, u32[]{:S(2)}) %collective-permute-start.20) | collective-permute-done | bytes 147488 | tf_op jit(solution)/shard_map/ppermute | solution.py:282
  93.6 1.6 %collective-permute-done.21 = bf16[32,2304]{1,0:T(8,128)(2,1)S(1)} collective-permute-done((bf16[32,2304]{1,0:T(8,128)(2,1)S(1)}, bf16[32,2304]{1,0:T(8,128)(2,1)S(1)}, u32[]{:S(2)}, u32[]{:S(2)}) %collective-permute-start.21) | collective-permute-done | bytes 147488 | tf_op jit(solution)/shard_map/ppermute | solution.py:282
  95.3 2.9 %collective-permute-start.22 = (bf16[16,2304]{1,0:T(8,128)(2,1)S(1)}, bf16[16,2304]{1,0:T(8,128)(2,1)S(1)}, u32[]{:S(2)}, u32[]{:S(2)}) collective-permute-start(bf16[16,2304]{1,0:T(8,128)(2,1)S(1)} %slice.45), channel_id=1, source_target_pairs={{0,38},{2,36},{4,34},{6,32},{32,6},{34,4},{36,2},{38,0},{1,39},{3,... | collective-permute-start | bytes 221192 | tf_op jit(solution)/shard_map/ppermute | solution.py:267
  98.2 3.4 %collective-permute-done.22 = bf16[16,2304]{1,0:T(8,128)(2,1)S(1)} collective-permute-done((bf16[16,2304]{1,0:T(8,128)(2,1)S(1)}, bf16[16,2304]{1,0:T(8,128)(2,1)S(1)}, u32[]{:S(2)}, u32[]{:S(2)}) %collective-permute-start.22) | collective-permute-done | bytes 73760 | tf_op jit(solution)/shard_map/ppermute | solution.py:267
  101.7 2.2 %collective-permute-start.24 = (bf16[4,2304]{1,0:T(4,128)(2,1)S(1)}, bf16[4,2304]{1,0:T(4,128)(2,1)S(1)}, u32[]{:S(2)}, u32[]{:S(2)}) collective-permute-start(bf16[4,2304]{1,0:T(4,128)(2,1)S(1)} %get-tuple-element.58), channel_id=1, source_target_pairs={{0,4},{2,6},{4,0},{6,2},{1,5},{3,7},{5,1},{7,3},{8,12},{10,14},{12... | collective-permute-start | bytes 55304 | tf_op jit(solution)/shard_map/ppermute | solution.py:271
  103.9 1.6 %collective-permute-start.25 = (bf16[4,2304]{1,0:T(4,128)(2,1)S(1)}, bf16[4,2304]{1,0:T(4,128)(2,1)S(1)}, u32[]{:S(2)}, u32[]{:S(2)}) collective-permute-start(bf16[4,2304]{1,0:T(4,128)(2,1)S(1)} %get-tuple-element.57), channel_id=1, source_target_pairs={{0,2},{2,4},{4,6},{6,0},{1,3},{3,5},{5,7},{7,1},{8,10},{10,12},{12... | collective-permute-start | bytes 55304 | tf_op jit(solution)/shard_map/ppermute | solution.py:271
  106.5 3.0 %collective-permute-done.25 = bf16[4,2304]{1,0:T(4,128)(2,1)S(1)} collective-permute-done((bf16[4,2304]{1,0:T(4,128)(2,1)S(1)}, bf16[4,2304]{1,0:T(4,128)(2,1)S(1)}, u32[]{:S(2)}, u32[]{:S(2)}) %collective-permute-start.25) | collective-permute-done | bytes 18464 | tf_op jit(solution)/shard_map/ppermute | solution.py:271
  (50 shorter events, 14.4 us)
Async XLA Ops:
  0.0 8.4 %collective-permute-start = (bf16[180,2304]{1,0:T(8,128)(2,1)}, bf16[180,2304]{1,0:T(8,128)(2,1)S(1)}, u32[]{:S(2)}, u32[]{:S(2)}) collective-permute-start(bf16[180,2304]{1,0:T(8,128)(2,1)} %bitcast.11), channel_id=1, source_target_pairs={{0,1},{1,0},{2,3},{3,2},{4,5},{5,4},{6,7},{7,6},{8,9},{9,8},{10,11... | collective-permute-start | bytes 2488328 | tf_op jit(solution)/shard_map/ppermute | solution.py:263
  0.0 8.4 %collective-permute-start.1 = (bf16[180,2304]{1,0:T(8,128)(2,1)}, bf16[180,2304]{1,0:T(8,128)(2,1)S(1)}, u32[]{:S(2)}, u32[]{:S(2)}) collective-permute-start(bf16[180,2304]{1,0:T(8,128)(2,1)} %bitcast.13), channel_id=1, source_target_pairs={{0,1},{1,0},{2,3},{3,2},{4,5},{5,4},{6,7},{7,6},{8,9},{9,8},{10,11... | collective-permute-start | bytes 2488328 | tf_op jit(solution)/shard_map/ppermute | solution.py:263
  0.5 7.9 %collective-permute-start.2 = (bf16[180,2304]{1,0:T(8,128)(2,1)}, bf16[180,2304]{1,0:T(8,128)(2,1)S(1)}, u32[]{:S(2)}, u32[]{:S(2)}) collective-permute-start(bf16[180,2304]{1,0:T(8,128)(2,1)} %bitcast.15), channel_id=1, source_target_pairs={{0,1},{1,0},{2,3},{3,2},{4,5},{5,4},{6,7},{7,6},{8,9},{9,8},{10,11... | collective-permute-start | bytes 2488328 | tf_op jit(solution)/shard_map/ppermute | solution.py:263
  0.5 13.8 %copy-start.4 = (s32[32]{0:T(128)S(1)}, s32[32]{0:T(128)}, u32[]{:S(2)}) copy-start(s32[32]{0:T(128)} %param.20) | copy-start | bytes 388
  0.5 21.6 %copy-start.5 = (bf16[2304]{0:T(1024)(128)(2,1)S(1)}, bf16[2304]{0:T(1024)(128)(2,1)}, u32[]{:S(2)}) copy-start(bf16[2304]{0:T(1024)(128)(2,1)} %param.15) | copy-start | bytes 13828
  0.5 53.0 %copy-start.2 = (bf16[1,180,2304]{2,1,0:T(8,128)(2,1)S(1)}, bf16[1,180,2304]{2,1,0:T(8,128)(2,1)}, u32[]{:S(2)}) copy-start(bf16[1,180,2304]{2,1,0:T(8,128)(2,1)} %param.25) | copy-start | bytes 2488324
  8.4 45.1 %copy-start = (bf16[1,2304,180]{1,2,0:T(8,128)(2,1)S(1)}, bf16[1,2304,180]{1,2,0:T(8,128)(2,1)}, u32[]{:S(2)}) copy-start(bf16[1,2304,180]{1,2,0:T(8,128)(2,1)} %param.23) | copy-start | bytes 2488324
  8.4 45.1 %copy-start.1 = (bf16[1,2304,180]{1,2,0:T(8,128)(2,1)S(1)}, bf16[1,2304,180]{1,2,0:T(8,128)(2,1)}, u32[]{:S(2)}) copy-start(bf16[1,2304,180]{1,2,0:T(8,128)(2,1)} %param.24) | copy-start | bytes 2488324
  8.4 5.9 %collective-permute-start.3 = (bf16[16,2432]{1,0:T(8,128)(2,1)}, bf16[16,2432]{1,0:T(8,128)(2,1)S(1)}, u32[]{:S(2)}, u32[]{:S(2)}) collective-permute-start(bf16[16,2432]{1,0:T(8,128)(2,1)} %get-tuple-element.33), channel_id=1, source_target_pairs={{0,1},{1,0},{2,3},{3,2},{4,5},{5,4},{6,7},{7,6},{8,9},{9,8},{10,11... | collective-permute-start | bytes 233480 | tf_op jit(solution)/shard_map/ppermute | solution.py:263
  9.0 4.2 %collective-permute-start.4 = (bf16[8,2432]{1,0:T(8,128)(2,1)}, bf16[8,2432]{1,0:T(8,128)(2,1)S(1)}, u32[]{:S(2)}, u32[]{:S(2)}) collective-permute-start(bf16[8,2432]{1,0:T(8,128)(2,1)} %get-tuple-element.34), channel_id=1, source_target_pairs={{0,8},{8,0},{1,9},{9,1},{2,10},{10,2},{3,11},{11,3},{4,12},{12,4},... | collective-permute-start | bytes 116744 | tf_op jit(solution)/shard_map/ppermute | solution.py:263
  10.3 4.0 %collective-permute-start.5 = (bf16[8,2432]{1,0:T(8,128)(2,1)}, bf16[8,2432]{1,0:T(8,128)(2,1)S(1)}, u32[]{:S(2)}, u32[]{:S(2)}) collective-permute-start(bf16[8,2432]{1,0:T(8,128)(2,1)} %get-tuple-element.34), channel_id=1, source_target_pairs={{0,9},{1,8},{8,1},{9,0},{2,11},{3,10},{10,3},{11,2},{4,13},{5,12},... | collective-permute-start | bytes 116744 | tf_op jit(solution)/shard_map/ppermute | solution.py:348
  14.3 0.9 copy-start.3
  15.9 8.8 %collective-permute-start.6 = (bf16[24,2432]{1,0:T(8,128)(2,1)S(1)}, bf16[24,2432]{1,0:T(8,128)(2,1)S(1)}, u32[]{:S(2)}, u32[]{:S(2)}) collective-permute-start(bf16[24,2432]{1,0:T(8,128)(2,1)S(1)} %chip.1.p0), channel_id=1, source_target_pairs={{0,2},{2,4},{4,6},{6,0},{1,3},{3,5},{5,7},{7,1},{8,10},{10,12},{12... | collective-permute-start | bytes 350216 | tf_op jit(solution)/shard_map/ppermute | solution.py:271
  17.9 11.2 %collective-permute-start.7 = (bf16[24,2432]{1,0:T(8,128)(2,1)S(1)}, bf16[24,2432]{1,0:T(8,128)(2,1)S(1)}, u32[]{:S(2)}, u32[]{:S(2)}) collective-permute-start(bf16[24,2432]{1,0:T(8,128)(2,1)S(1)} %chip.1.p0), channel_id=1, source_target_pairs={{0,4},{2,6},{4,0},{6,2},{1,5},{3,7},{5,1},{7,3},{8,12},{10,14},{12... | collective-permute-start | bytes 350216 | tf_op jit(solution)/shard_map/ppermute | solution.py:271
  21.1 8.0 %collective-permute-start.8 = (bf16[24,2432]{1,0:T(8,128)(2,1)S(1)}, bf16[24,2432]{1,0:T(8,128)(2,1)S(1)}, u32[]{:S(2)}, u32[]{:S(2)}) collective-permute-start(bf16[24,2432]{1,0:T(8,128)(2,1)S(1)} %chip.1.p0), channel_id=1, source_target_pairs={{0,6},{2,0},{4,2},{6,4},{1,7},{3,1},{5,3},{7,5},{8,14},{10,8},{12,... | collective-permute-start | bytes 350216 | tf_op jit(solution)/shard_map/ppermute | solution.py:271
  29.9 9.8 %collective-permute-start.9 = (bf16[16,2432]{1,0:T(8,128)(2,1)S(1)}, bf16[16,2432]{1,0:T(8,128)(2,1)S(1)}, u32[]{:S(2)}, u32[]{:S(2)}) collective-permute-start(bf16[16,2432]{1,0:T(8,128)(2,1)S(1)} %get-tuple-element.39.refs_0_), channel_id=1, source_target_pairs={{0,38},{2,36},{4,34},{6,32},{32,6},{34,4},{36,2},{38,0},{1,39},{3,... | collective-permute-start | bytes 233480 | tf_op jit(solution)/shard_map/ppermute | solution.py:267
  39.8 6.5 %collective-permute-start.10 = (bf16[32,2432]{1,0:T(8,128)(2,1)S(1)}, bf16[32,2432]{1,0:T(8,128)(2,1)S(1)}, u32[]{:S(2)}, u32[]{:S(2)}) collective-permute-start(bf16[32,2432]{1,0:T(8,128)(2,1)S(1)} %join.2.refs_0_), channel_id=1, source_target_pairs={{0,64},{1,9},{8,72},{9,17},{16,80},{17,25},{24,88},{25,1},{64,128}... | collective-permute-start | bytes 466952 | tf_op jit(solution)/shard_map/ppermute | solution.py:282
  41.3 5.2 %collective-permute-start.11 = (bf16[32,2432]{1,0:T(8,128)(2,1)S(1)}, bf16[32,2432]{1,0:T(8,128)(2,1)S(1)}, u32[]{:S(2)}, u32[]{:S(2)}) collective-permute-start(bf16[32,2432]{1,0:T(8,128)(2,1)S(1)} %join.2.refs_0_), channel_id=1, source_target_pairs={{0,192},{1,25},{8,200},{9,1},{16,208},{17,9},{24,216},{25,17},{64,... | collective-permute-start | bytes 466952 | tf_op jit(solution)/shard_map/ppermute | solution.py:282
  43.1 8.0 %collective-permute-start.12 = (bf16[32,2432]{1,0:T(8,128)(2,1)S(1)}, bf16[32,2432]{1,0:T(8,128)(2,1)S(1)}, u32[]{:S(2)}, u32[]{:S(2)}) collective-permute-start(bf16[32,2432]{1,0:T(8,128)(2,1)S(1)} %join.2.refs_0_), channel_id=1, source_target_pairs={{0,128},{1,17},{8,136},{9,25},{16,144},{17,1},{24,152},{25,9},{64,... | collective-permute-start | bytes 466952 | tf_op jit(solution)/shard_map/ppermute | solution.py:282
  51.1 12.1 %collective-permute-start.13 = (bf16[128,2432]{1,0:T(8,128)(2,1)S(1)}, bf16[128,2432]{1,0:T(8,128)(2,1)S(1)}, u32[]{:S(2)}, u32[]{:S(2)}) collective-permute-start(bf16[128,2432]{1,0:T(8,128)(2,1)S(1)} %join.3.x_ref), channel_id=1, source_target_pairs={{0,16},{1,129},{8,24},{9,137},{16,0},{17,145},{24,8},{25,153},{64,... | collective-permute-start | bytes 1867784 | tf_op jit(solution)/shard_map/ppermute | solution.py:282
  51.4 15.5 %collective-permute-start.15 = (bf16[128,2432]{1,0:T(8,128)(2,1)S(1)}, bf16[128,2432]{1,0:T(8,128)(2,1)S(1)}, u32[]{:S(2)}, u32[]{:S(2)}) collective-permute-start(bf16[128,2432]{1,0:T(8,128)(2,1)S(1)} %join.3.x_ref), channel_id=1, source_target_pairs={{0,24},{1,193},{8,0},{9,201},{16,8},{17,209},{24,16},{25,217},{64,... | collective-permute-start | bytes 1867784 | tf_op jit(solution)/shard_map/ppermute | solution.py:282
  52.5 18.7 %collective-permute-start.17 = (bf16[128,2432]{1,0:T(8,128)(2,1)S(1)}, bf16[128,2432]{1,0:T(8,128)(2,1)S(1)}, u32[]{:S(2)}, u32[]{:S(2)}) collective-permute-start(bf16[128,2432]{1,0:T(8,128)(2,1)S(1)} %join.3.x_ref), channel_id=1, source_target_pairs={{0,8},{1,65},{8,16},{9,73},{16,24},{17,81},{24,0},{25,89},{64,72},... | collective-permute-start | bytes 1867784 | tf_op jit(solution)/shard_map/ppermute | solution.py:282
  64.9 11.6 %collective-permute-start.14 = (bf16[128,2304]{1,0:T(8,128)(2,1)S(1)}, bf16[128,2304]{1,0:T(8,128)(2,1)S(1)}, u32[]{:S(2)}, u32[]{:S(2)}) collective-permute-start(bf16[128,2304]{1,0:T(8,128)(2,1)S(1)} %mlp.5), channel_id=1, source_target_pairs={{0,16},{1,129},{8,24},{9,137},{16,0},{17,145},{24,8},{25,153},{64,... | collective-permute-start | bytes 1769480 | tf_op jit(solution)/shard_map/ppermute | solution.py:282
  68.6 16.3 %collective-permute-start.16 = (bf16[128,2304]{1,0:T(8,128)(2,1)S(1)}, bf16[128,2304]{1,0:T(8,128)(2,1)S(1)}, u32[]{:S(2)}, u32[]{:S(2)}) collective-permute-start(bf16[128,2304]{1,0:T(8,128)(2,1)S(1)} %mlp.6), channel_id=1, source_target_pairs={{0,8},{1,65},{8,16},{9,73},{16,24},{17,81},{24,0},{25,89},{64,72},... | collective-permute-start | bytes 1769480 | tf_op jit(solution)/shard_map/ppermute | solution.py:282
  72.9 13.1 %collective-permute-start.18 = (bf16[128,2304]{1,0:T(8,128)(2,1)S(1)}, bf16[128,2304]{1,0:T(8,128)(2,1)S(1)}, u32[]{:S(2)}, u32[]{:S(2)}) collective-permute-start(bf16[128,2304]{1,0:T(8,128)(2,1)S(1)} %mlp.7), channel_id=1, source_target_pairs={{0,24},{1,193},{8,0},{9,201},{16,8},{17,209},{24,16},{25,217},{64,... | collective-permute-start | bytes 1769480 | tf_op jit(solution)/shard_map/ppermute | solution.py:282
  86.4 5.2 %collective-permute-start.19 = (bf16[32,2304]{1,0:T(8,128)(2,1)S(1)}, bf16[32,2304]{1,0:T(8,128)(2,1)S(1)}, u32[]{:S(2)}, u32[]{:S(2)}) collective-permute-start(bf16[32,2304]{1,0:T(8,128)(2,1)S(1)} %get-tuple-element.53), channel_id=1, source_target_pairs={{0,192},{1,25},{8,200},{9,1},{16,208},{17,9},{24,216},{25,17},{64,... | collective-permute-start | bytes 442376 | tf_op jit(solution)/shard_map/ppermute | solution.py:282
  87.2 6.4 %collective-permute-start.20 = (bf16[32,2304]{1,0:T(8,128)(2,1)S(1)}, bf16[32,2304]{1,0:T(8,128)(2,1)S(1)}, u32[]{:S(2)}, u32[]{:S(2)}) collective-permute-start(bf16[32,2304]{1,0:T(8,128)(2,1)S(1)} %get-tuple-element.55), channel_id=1, source_target_pairs={{0,64},{1,9},{8,72},{9,17},{16,80},{17,25},{24,88},{25,1},{64,128}... | collective-permute-start | bytes 442376 | tf_op jit(solution)/shard_map/ppermute | solution.py:282
  88.5 6.7 %collective-permute-start.21 = (bf16[32,2304]{1,0:T(8,128)(2,1)S(1)}, bf16[32,2304]{1,0:T(8,128)(2,1)S(1)}, u32[]{:S(2)}, u32[]{:S(2)}) collective-permute-start(bf16[32,2304]{1,0:T(8,128)(2,1)S(1)} %get-tuple-element.54), channel_id=1, source_target_pairs={{0,128},{1,17},{8,136},{9,25},{16,144},{17,1},{24,152},{25,9},{64,... | collective-permute-start | bytes 442376 | tf_op jit(solution)/shard_map/ppermute | solution.py:282
  95.3 6.3 %collective-permute-start.22 = (bf16[16,2304]{1,0:T(8,128)(2,1)S(1)}, bf16[16,2304]{1,0:T(8,128)(2,1)S(1)}, u32[]{:S(2)}, u32[]{:S(2)}) collective-permute-start(bf16[16,2304]{1,0:T(8,128)(2,1)S(1)} %slice.45), channel_id=1, source_target_pairs={{0,38},{2,36},{4,34},{6,32},{32,6},{34,4},{36,2},{38,0},{1,39},{3,... | collective-permute-start | bytes 221192 | tf_op jit(solution)/shard_map/ppermute | solution.py:267
  101.6 3.9 %collective-permute-start.23 = (bf16[4,2304]{1,0:T(4,128)(2,1)S(1)}, bf16[4,2304]{1,0:T(4,128)(2,1)S(1)}, u32[]{:S(2)}, u32[]{:S(2)}) collective-permute-start(bf16[4,2304]{1,0:T(4,128)(2,1)S(1)} %get-tuple-element.56), channel_id=1, source_target_pairs={{0,6},{2,0},{4,2},{6,4},{1,7},{3,1},{5,3},{7,5},{8,14},{10,8},{12,... | collective-permute-start | bytes 55304 | tf_op jit(solution)/shard_map/ppermute | solution.py:271
  101.7 4.7 %collective-permute-start.24 = (bf16[4,2304]{1,0:T(4,128)(2,1)S(1)}, bf16[4,2304]{1,0:T(4,128)(2,1)S(1)}, u32[]{:S(2)}, u32[]{:S(2)}) collective-permute-start(bf16[4,2304]{1,0:T(4,128)(2,1)S(1)} %get-tuple-element.58), channel_id=1, source_target_pairs={{0,4},{2,6},{4,0},{6,2},{1,5},{3,7},{5,1},{7,3},{8,12},{10,14},{12... | collective-permute-start | bytes 55304 | tf_op jit(solution)/shard_map/ppermute | solution.py:271
  103.9 5.6 %collective-permute-start.25 = (bf16[4,2304]{1,0:T(4,128)(2,1)S(1)}, bf16[4,2304]{1,0:T(4,128)(2,1)S(1)}, u32[]{:S(2)}, u32[]{:S(2)}) collective-permute-start(bf16[4,2304]{1,0:T(4,128)(2,1)S(1)} %get-tuple-element.57), channel_id=1, source_target_pairs={{0,2},{2,4},{4,6},{6,0},{1,3},{3,5},{5,7},{7,1},{8,10},{10,12},{12... | collective-permute-start | bytes 55304 | tf_op jit(solution)/shard_map/ppermute | solution.py:271

commit v3 on v2

--- a/solution.py
+++ b/solution.py
@@ -13,6 +13,8 @@
 LW = 128
 GROUP = 4
 W = D + LW
+CUT = (0, 640, 1280, 1792, 2304)
+WX = W + 640
 NEG_FILL = -1e30
 NORM_EPS = 1e-06
 F32 = jnp.float32
@@ -117,9 +119,18 @@
             for ref in (routes_ref, gates_ref)
         )
         coefs = coefs + jnp.where(spot == route.astype(jnp.int32), gate, 0.0)
-    own_ref[rows // 2 : rows // 2 + own, :D] = res_ref[...]
-    own_ref[rows // 2 : rows // 2 + own, D:] = coefs.astype(BF16)
-    own_ref[rows // 2 + own :, :] = jnp.zeros((own_ref.shape[0] - rows // 2 - own, W), BF16)
+    extra = None
+    line = lax.broadcasted_iota(jnp.int32, (rows // 2, own), 0)
+    slot = lax.broadcasted_iota(jnp.int32, (rows // 2, own), 1)
+    for q in range(4):
+        piece = res_ref[:, CUT[q] : CUT[q + 1]]
+        if q == 2:
+            piece = jnp.concatenate([piece, coefs.astype(BF16)], axis=1)
+        if q == 3:
+            piece = jnp.concatenate([piece, jnp.zeros((own, LW), BF16)], axis=1)
+        term = dot((line == 4 * slot + q).astype(F32).astype(BF16), piece)
+        extra = term if extra is None else extra + term
+    own_ref[:, W:] = extra.astype(BF16)
     owner_b = owner.astype(BF16)
     q_sel = dot(owner_b, q_ref[...], 0, 0)
     mask = head_mask(HP, D)
@@ -173,8 +184,8 @@
     for p in range(pages):
         row_lse = jnp.maximum(row_lse, jnp.where(chosen[:, p : p + 1] > 0, joint[p : p + 1, :], NEG_FILL))
     lanes = packed(row_lse)
-    own_ref[:half, :D] = values[:half, :]
-    own_ref[:half, D:] = lanes[:half, :]
+    own_ref[:, :D] = values[:half, :]
+    own_ref[:, D:W] = lanes[:half, :]
     other_ref[:, :D] = values[half:rows, :]
     other_ref[:, D:] = lanes[half:rows, :]
     split_ref[:, :D] = values[rows:, :]
@@ -187,15 +198,15 @@
     half = other_ref.shape[0]
     _, wanted = wanted_rows(half, 2 * half, lax.axis_index("c"))
     flag = jnp.sum(jnp.where(wanted, flag_ref[...].astype(F32), 0.0), axis=1, keepdims=True) > 0
-    values = [own_ref[:half, :D], other_ref[:, :D]]
-    lses = [unpacked(own_ref[:half, D:]), unpacked(other_ref[:, D:])]
+    values = [own_ref[:, :D], other_ref[:, :D]]
+    lses = [unpacked(own_ref[:, D:W]), unpacked(other_ref[:, D:])]
     for far in (far_0_ref, far_1_ref):
         values.append(far[0:1, :D])
         lses.append(jnp.where(flag, unpacked(far[:, D:])[0:1, :], NEG_FILL))
     total, lse = combined(values, lses, spread_heads())
-    out_ref[:half, :D] = total.astype(BF16)
-    out_ref[:half, D:] = packed(lse)
-    out_ref[half:, :] = own_ref[half:, :]
+    out_ref[:, :D] = total.astype(BF16)
+    out_ref[:, D:W] = packed(lse)
+    out_ref[:, W:] = own_ref[:, W:]
 
 
 def norm_kernel(p0, p1, p2, p3, gain_ref, attn_ref, out_ref):
@@ -203,8 +214,8 @@
     rows = out_ref.shape[0]
     own = attn_ref.shape[0]
     total, _ = combined(
-        [part[:rows, :D] for part in parts],
-        [unpacked(part[:rows, D:]) for part in parts],
+        [part[:, :D] for part in parts],
+        [unpacked(part[:, D:W]) for part in parts],
         spread_heads(),
     )
     line = lax.broadcasted_iota(jnp.int32, (rows, rows), 0)
@@ -213,11 +224,15 @@
     turn = (slot == own * source + line % own).astype(F32).astype(BF16)
     attn = dot(turn, total.astype(BF16))
     attn_ref[...] = attn[:own, :].astype(BF16)
-    extra = jnp.concatenate([part[rows : rows + own, :].astype(F32) for part in parts], axis=0)
-    stream = extra[:, :D] + attn
+    extras = jnp.concatenate([part[:, W:] for part in parts], axis=0)
+    line = lax.broadcasted_iota(jnp.int32, (rows, 4 * rows), 0)
+    slot = lax.broadcasted_iota(jnp.int32, (rows, 4 * rows), 1)
+    fetched = [dot((slot == 4 * line + q).astype(F32).astype(BF16), extras) for q in range(4)]
+    residual = jnp.concatenate([fetched[q][:, : CUT[q + 1] - CUT[q]] for q in range(4)], axis=1)
+    stream = residual + attn
     normed = stream * lax.rsqrt(jnp.mean(stream * stream, axis=-1, keepdims=True) + NORM_EPS)
     out_ref[:, :D] = (normed * gain_ref[...].astype(F32)).astype(BF16)
-    out_ref[:, D:] = extra[:, D:].astype(BF16)
+    out_ref[:, D:] = fetched[2][:, CUT[3] - CUT[2] :].astype(BF16)
 
 
 def hold_kernel(*refs):
@@ -305,7 +320,7 @@
 
 
 NEAR = (1, 3, 2)
-WIDE = (2, 3, 1)
+WIDE = (2, 1, 3)
 
 
 def on_device(
@@ -323,7 +338,7 @@
     here, there, split = pl.pallas_call(
         attn_kernel,
         out_shape=(
-            jax.ShapeDtypeStruct((half + 8, W), BF16),
+            jax.ShapeDtypeStruct((half, WX), BF16),
             jax.ShapeDtypeStruct((half, W), BF16),
             jax.ShapeDtypeStruct((8, W), BF16),
         ),
@@ -348,7 +363,7 @@
     far_1 = lax.ppermute(split, ("yp", "c"), [(i, 3 - i) for i in range(4)])
     chip = pl.pallas_call(
         chip_kernel,
-        out_shape=jax.ShapeDtypeStruct((half + 8, W), BF16),
+        out_shape=jax.ShapeDtypeStruct((half, WX), BF16),
         compiler_params=vmem(8),
         name="chip",
     )(here, across, far_0, far_1, flag_row)

time: 111 us -> 109 us (0.982)
  waiting for transfers between devices: 55.9 us -> 53 us
  starting transfers between devices: 35.5 us -> 36.8 us
    ppermute x12, waiting for transfers between devices: 33.8 us -> 32.1 us  [along_plane(): return lax.ppermute(array, PLANE, pairs)]
  transfers between devices with their start and end apart: 26 -> 26, of which waited for: 19 -> 18; matrix products, arithmetic and copies ran while one was open for 0% -> 0% of each run, Pallas kernels for 14% -> 14%
where the time goes in v3:
time: 109 us; the launch traced here: 108 us
  waiting for transfers between devices  53 us (49%)
  starting transfers between devices  36.8 us (34%)
  Pallas kernels  16.5 us (15%)
    ppermute x12, waiting for transfers between devices, along_plane(): return lax.ppermute(array, PLANE, pairs)  32.1 us
    ppermute x12, starting transfers between devices, along_plane(): return lax.ppermute(array, PLANE, pairs)  14.6 us
    ppermute x6, starting transfers between devices, along_line(): return lax.ppermute(array, 'zl', [(i, (i + shift) % n) for i in range(n)])  10.1 us
    ppermute x6, waiting for transfers between devices, along_line(): return lax.ppermute(array, 'zl', [(i, (i + shift) % n) for i in range(n)])  9.94 us
    ppermute x2, starting transfers between devices, mirrored(): return lax.ppermute(array, ('zh', 'zl'), [(i, 7 - i) for i in range(8)])  9.55 us
    pallas_call x1, Pallas kernels, on_device(): pl.pallas_call(attn_kernel, out_shape=(jax.ShapeDtypeStruct((half, WX), B...  7.82 us
    ppermute x2, waiting for transfers between devices, mirrored(): return lax.ppermute(array, ('zh', 'zl'), [(i, 7 - i) for i in range(8)])  7.04 us
    pallas_call x4, Pallas kernels, mlp(): pl.pallas_call(mlp_kernel, out_shape=jax.ShapeDtypeStruct((block.shape[0]...  6.82 us
  transfers between devices with their start and end apart: 26, of which 18 were waited for; matrix products, arithmetic and copies ran while one was open for 0% of the time, Pallas kernels for 14%

profile of v3, /device:TPU:16, one launch (start us, length us, event | category | flops | bytes accessed | tf_op | source)
XLA Modules:
  0.0 108.5 jit_solution(10086391202799092645)
XLA Ops:
  0.5 7.8 %attn.1 = (bf16[16,3072]{1,0:T(8,128)(2,1)}, bf16[16,2432]{1,0:T(8,128)(2,1)}, bf16[8,2432]{1,0:T(8,128)(2,1)}) custom-call(bf16[32,2304]{1,0:T(8,128)(2,1)} %q_ref.1, s32[32,32]{1,0:T(8,128)} %table_ref.1, s32[1,32]{1,0:T(1,128)} %bitcast.20, s32[1,32]{1,0:T(1,128)} %bitcast.17, bf16[4,2304]{1,0:T(4,128)(2,1)} %res_ref.1, s32[2,4]{1,0:T(2,128)} %bitcast.19, ...), custom_call_target="tpu_custom_call" | custom-call | flops 2000000000 | bytes 10000000 | tf_op jit(solution)/shard_map/attn/pallas_call | solution.py:338
  9.0 1.3 %collective-permute-start.4 = (bf16[8,2432]{1,0:T(8,128)(2,1)}, bf16[8,2432]{1,0:T(8,128)(2,1)S(1)}, u32[]{:S(2)}, u32[]{:S(2)}) collective-permute-start(bf16[8,2432]{1,0:T(8,128)(2,1)} %get-tuple-element.34), channel_id=1, source_target_pairs={{0,8},{8,0},{1,9},{9,1},{2,10},{10,2},{3,11},{11,3},{4,12},{12,4},... | collective-permute-start | bytes 116744 | tf_op jit(solution)/shard_map/ppermute | solution.py:278
  10.5 2.7 %collective-permute-done.4.far_0_ref = bf16[8,2432]{1,0:T(8,128)(2,1)S(1)} collective-permute-done((bf16[8,2432]{1,0:T(8,128)(2,1)}, bf16[8,2432]{1,0:T(8,128)(2,1)S(1)}, u32[]{:S(2)}, u32[]{:S(2)}) %collective-permute-start.4) | collective-permute-done | bytes 38944 | tf_op jit(solution)/shard_map/ppermute | solution.py:278
  15.8 2.0 %collective-permute-start.6 = (bf16[16,3072]{1,0:T(8,128)(2,1)S(1)}, bf16[16,3072]{1,0:T(8,128)(2,1)S(1)}, u32[]{:S(2)}, u32[]{:S(2)}) collective-permute-start(bf16[16,3072]{1,0:T(8,128)(2,1)S(1)} %chip.1.p0), channel_id=1, source_target_pairs={{0,2},{2,4},{4,6},{6,0},{1,3},{3,5},{5,7},{7,1},{8,10},{10,12},{12... | collective-permute-start | bytes 294920 | tf_op jit(solution)/shard_map/ppermute | solution.py:286
  17.8 3.3 %collective-permute-start.7 = (bf16[16,3072]{1,0:T(8,128)(2,1)S(1)}, bf16[16,3072]{1,0:T(8,128)(2,1)S(1)}, u32[]{:S(2)}, u32[]{:S(2)}) collective-permute-start(bf16[16,3072]{1,0:T(8,128)(2,1)S(1)} %chip.1.p0), channel_id=1, source_target_pairs={{0,4},{2,6},{4,0},{6,2},{1,5},{3,7},{5,1},{7,3},{8,12},{10,14},{12... | collective-permute-start | bytes 294920 | tf_op jit(solution)/shard_map/ppermute | solution.py:286
  22.1 2.1 %collective-permute-done.6.p1 = bf16[16,3072]{1,0:T(8,128)(2,1)S(1)} collective-permute-done((bf16[16,3072]{1,0:T(8,128)(2,1)S(1)}, bf16[16,3072]{1,0:T(8,128)(2,1)S(1)}, u32[]{:S(2)}, u32[]{:S(2)}) %collective-permute-start.6) | collective-permute-done | bytes 98336 | tf_op jit(solution)/shard_map/ppermute | solution.py:286
  24.2 3.7 %collective-permute-done.7.p2 = bf16[16,3072]{1,0:T(8,128)(2,1)S(1)} collective-permute-done((bf16[16,3072]{1,0:T(8,128)(2,1)S(1)}, bf16[16,3072]{1,0:T(8,128)(2,1)S(1)}, u32[]{:S(2)}, u32[]{:S(2)}) %collective-permute-start.7) | collective-permute-done | bytes 98336 | tf_op jit(solution)/shard_map/ppermute | solution.py:286
  28.8 5.5 %collective-permute-start.9 = (bf16[16,2432]{1,0:T(8,128)(2,1)S(1)}, bf16[16,2432]{1,0:T(8,128)(2,1)S(1)}, u32[]{:S(2)}, u32[]{:S(2)}) collective-permute-start(bf16[16,2432]{1,0:T(8,128)(2,1)S(1)} %get-tuple-element.39.refs_0_), channel_id=1, source_target_pairs={{0,38},{2,36},{4,34},{6,32},{32,6},{34,4},{36,2},{38,0},{1,39},{3,... | collective-permute-start | bytes 233480 | tf_op jit(solution)/shard_map/ppermute | solution.py:282
  34.3 3.9 %collective-permute-done.9.refs_1_ = bf16[16,2432]{1,0:T(8,128)(2,1)S(1)} collective-permute-done((bf16[16,2432]{1,0:T(8,128)(2,1)S(1)}, bf16[16,2432]{1,0:T(8,128)(2,1)S(1)}, u32[]{:S(2)}, u32[]{:S(2)}) %collective-permute-start.9) | collective-permute-done | bytes 77856 | tf_op jit(solution)/shard_map/ppermute | solution.py:282
  38.2 1.6 %collective-permute-start.10 = (bf16[32,2432]{1,0:T(8,128)(2,1)S(1)}, bf16[32,2432]{1,0:T(8,128)(2,1)S(1)}, u32[]{:S(2)}, u32[]{:S(2)}) collective-permute-start(bf16[32,2432]{1,0:T(8,128)(2,1)S(1)} %join.2.refs_0_), channel_id=1, source_target_pairs={{0,64},{1,9},{8,72},{9,17},{16,80},{17,25},{24,88},{25,1},{64,128}... | collective-permute-start | bytes 466952 | tf_op jit(solution)/shard_map/ppermute | solution.py:297
  39.8 1.7 %collective-permute-start.11 = (bf16[32,2432]{1,0:T(8,128)(2,1)S(1)}, bf16[32,2432]{1,0:T(8,128)(2,1)S(1)}, u32[]{:S(2)}, u32[]{:S(2)}) collective-permute-start(bf16[32,2432]{1,0:T(8,128)(2,1)S(1)} %join.2.refs_0_), channel_id=1, source_target_pairs={{0,192},{1,25},{8,200},{9,1},{16,208},{17,9},{24,216},{25,17},{64,... | collective-permute-start | bytes 466952 | tf_op jit(solution)/shard_map/ppermute | solution.py:297
  41.5 1.8 %collective-permute-start.12 = (bf16[32,2432]{1,0:T(8,128)(2,1)S(1)}, bf16[32,2432]{1,0:T(8,128)(2,1)S(1)}, u32[]{:S(2)}, u32[]{:S(2)}) collective-permute-start(bf16[32,2432]{1,0:T(8,128)(2,1)S(1)} %join.2.refs_0_), channel_id=1, source_target_pairs={{0,128},{1,17},{8,136},{9,25},{16,144},{17,1},{24,152},{25,9},{64,... | collective-permute-start | bytes 466952 | tf_op jit(solution)/shard_map/ppermute | solution.py:297
  43.4 1.4 %collective-permute-done.10.refs_1_ = bf16[32,2432]{1,0:T(8,128)(2,1)S(1)} collective-permute-done((bf16[32,2432]{1,0:T(8,128)(2,1)S(1)}, bf16[32,2432]{1,0:T(8,128)(2,1)S(1)}, u32[]{:S(2)}, u32[]{:S(2)}) %collective-permute-start.10) | collective-permute-done | bytes 155680 | tf_op jit(solution)/shard_map/ppermute | solution.py:297
  45.0 3.2 %collective-permute-done.12.refs_3_ = bf16[32,2432]{1,0:T(8,128)(2,1)S(1)} collective-permute-done((bf16[32,2432]{1,0:T(8,128)(2,1)S(1)}, bf16[32,2432]{1,0:T(8,128)(2,1)S(1)}, u32[]{:S(2)}, u32[]{:S(2)}) %collective-permute-start.12) | collective-permute-done | bytes 155680 | tf_op jit(solution)/shard_map/ppermute | solution.py:297
  51.6 8.8 %collective-permute-done.13.x_ref = bf16[128,2432]{1,0:T(8,128)(2,1)S(1)} collective-permute-done((bf16[128,2432]{1,0:T(8,128)(2,1)S(1)}, bf16[128,2432]{1,0:T(8,128)(2,1)S(1)}, u32[]{:S(2)}, u32[]{:S(2)}) %collective-permute-start.13) | collective-permute-done | bytes 622624 | tf_op jit(solution)/shard_map/ppermute | solution.py:297
  60.4 1.7 %mlp.5 = bf16[128,2304]{1,0:T(8,128)(2,1)S(1)} custom-call(bf16[128,2432]{1,0:T(8,128)(2,1)S(1)} %collective-permute-done.13.x_ref, bf16[180,2304]{1,0:T(8,128)(2,1)S(1)} %get-tuple-element.46.gate_0, bf16[180,2304]{1,0:T(8,128)(2,1)S(1)} %get-tuple-element.47.up_0, bf16[180,2304]{1,0:T(8,128)(2,1)S(1)} %get-tuple-element.48.down_0, ...), custom_call_target="tpu_custom_call" | custom-call | flops 3000000000 | bytes 10000000 | tf_op jit(solution)/shard_map/mlp/pallas_call | solution.py:386
  62.8 3.3 %collective-permute-done.15.x_ref = bf16[128,2432]{1,0:T(8,128)(2,1)S(1)} collective-permute-done((bf16[128,2432]{1,0:T(8,128)(2,1)S(1)}, bf16[128,2432]{1,0:T(8,128)(2,1)S(1)}, u32[]{:S(2)}, u32[]{:S(2)}) %collective-permute-start.15) | collective-permute-done | bytes 622624 | tf_op jit(solution)/shard_map/ppermute | solution.py:297
  66.1 1.7 %mlp.6 = bf16[128,2304]{1,0:T(8,128)(2,1)S(1)} custom-call(bf16[128,2432]{1,0:T(8,128)(2,1)S(1)} %collective-permute-done.15.x_ref, bf16[180,2304]{1,0:T(8,128)(2,1)S(1)} %get-tuple-element.46.gate_0, bf16[180,2304]{1,0:T(8,128)(2,1)S(1)} %get-tuple-element.47.up_0, bf16[180,2304]{1,0:T(8,128)(2,1)S(1)} %get-tuple-element.48.down_0, ...), custom_call_target="tpu_custom_call" | custom-call | flops 3000000000 | bytes 10000000 | tf_op jit(solution)/shard_map/mlp/pallas_call | solution.py:386
  67.8 1.6 %collective-permute-start.16 = (bf16[128,2304]{1,0:T(8,128)(2,1)S(1)}, bf16[128,2304]{1,0:T(8,128)(2,1)S(1)}, u32[]{:S(2)}, u32[]{:S(2)}) collective-permute-start(bf16[128,2304]{1,0:T(8,128)(2,1)S(1)} %mlp.6), channel_id=1, source_target_pairs={{0,24},{1,193},{8,0},{9,201},{16,8},{17,209},{24,16},{25,217},{64,... | collective-permute-start | bytes 1769480 | tf_op jit(solution)/shard_map/ppermute | solution.py:297
  69.4 1.7 %mlp.7 = bf16[128,2304]{1,0:T(8,128)(2,1)S(1)} custom-call(bf16[128,2432]{1,0:T(8,128)(2,1)S(1)} %collective-permute-done.17.x_ref, bf16[180,2304]{1,0:T(8,128)(2,1)S(1)} %get-tuple-element.46.gate_0, bf16[180,2304]{1,0:T(8,128)(2,1)S(1)} %get-tuple-element.47.up_0, bf16[180,2304]{1,0:T(8,128)(2,1)S(1)} %get-tuple-element.48.down_0, ...), custom_call_target="tpu_custom_call" | custom-call | flops 3000000000 | bytes 10000000 | tf_op jit(solution)/shard_map/mlp/pallas_call | solution.py:386
  71.7 1.7 %mlp.4 = bf16[128,2304]{1,0:T(8,128)(2,1)S(1)} custom-call(bf16[128,2432]{1,0:T(8,128)(2,1)S(1)} %join.3.x_ref, bf16[180,2304]{1,0:T(8,128)(2,1)S(1)} %get-tuple-element.46.gate_0, bf16[180,2304]{1,0:T(8,128)(2,1)S(1)} %get-tuple-element.47.up_0, bf16[180,2304]{1,0:T(8,128)(2,1)S(1)} %get-tuple-element.48.down_0, ...), custom_call_target="tpu_custom_call" | custom-call | flops 3000000000 | bytes 10000000 | tf_op jit(solution)/shard_map/mlp/pallas_call | solution.py:386
  73.6 4.6 %collective-permute-done.16 = bf16[128,2304]{1,0:T(8,128)(2,1)S(1)} collective-permute-done((bf16[128,2304]{1,0:T(8,128)(2,1)S(1)}, bf16[128,2304]{1,0:T(8,128)(2,1)S(1)}, u32[]{:S(2)}, u32[]{:S(2)}) %collective-permute-start.16) | collective-permute-done | bytes 589856 | tf_op jit(solution)/shard_map/ppermute | solution.py:297
  78.2 3.9 %collective-permute-done.18 = bf16[128,2304]{1,0:T(8,128)(2,1)S(1)} collective-permute-done((bf16[128,2304]{1,0:T(8,128)(2,1)S(1)}, bf16[128,2304]{1,0:T(8,128)(2,1)S(1)}, u32[]{:S(2)}, u32[]{:S(2)}) %collective-permute-start.18) | collective-permute-done | bytes 589856 | tf_op jit(solution)/shard_map/ppermute | solution.py:297
  82.5 2.0 %collective-permute-start.19 = (bf16[32,2304]{1,0:T(8,128)(2,1)S(1)}, bf16[32,2304]{1,0:T(8,128)(2,1)S(1)}, u32[]{:S(2)}, u32[]{:S(2)}) collective-permute-start(bf16[32,2304]{1,0:T(8,128)(2,1)S(1)} %get-tuple-element.53), channel_id=1, source_target_pairs={{0,192},{1,25},{8,200},{9,1},{16,208},{17,9},{24,216},{25,17},{64,... | collective-permute-start | bytes 442376 | tf_op jit(solution)/shard_map/ppermute | solution.py:297
  84.6 1.5 %collective-permute-start.21 = (bf16[32,2304]{1,0:T(8,128)(2,1)S(1)}, bf16[32,2304]{1,0:T(8,128)(2,1)S(1)}, u32[]{:S(2)}, u32[]{:S(2)}) collective-permute-start(bf16[32,2304]{1,0:T(8,128)(2,1)S(1)} %get-tuple-element.54), channel_id=1, source_target_pairs={{0,128},{1,17},{8,136},{9,25},{16,144},{17,1},{24,152},{25,9},{64,... | collective-permute-start | bytes 442376 | tf_op jit(solution)/shard_map/ppermute | solution.py:297
  86.1 1.6 %collective-permute-done.19 = bf16[32,2304]{1,0:T(8,128)(2,1)S(1)} collective-permute-done((bf16[32,2304]{1,0:T(8,128)(2,1)S(1)}, bf16[32,2304]{1,0:T(8,128)(2,1)S(1)}, u32[]{:S(2)}, u32[]{:S(2)}) %collective-permute-start.19) | collective-permute-done | bytes 147488 | tf_op jit(solution)/shard_map/ppermute | solution.py:297
  87.8 4.7 %collective-permute-done.20 = bf16[32,2304]{1,0:T(8,128)(2,1)S(1)} collective-permute-done((bf16[32,2304]{1,0:T(8,128)(2,1)S(1)}, bf16[32,2304]{1,0:T(8,128)(2,1)S(1)}, u32[]{:S(2)}, u32[]{:S(2)}) %collective-permute-start.20) | collective-permute-done | bytes 147488 | tf_op jit(solution)/shard_map/ppermute | solution.py:297
  92.6 4.0 %collective-permute-start.22 = (bf16[16,2304]{1,0:T(8,128)(2,1)S(1)}, bf16[16,2304]{1,0:T(8,128)(2,1)S(1)}, u32[]{:S(2)}, u32[]{:S(2)}) collective-permute-start(bf16[16,2304]{1,0:T(8,128)(2,1)S(1)} %slice.45), channel_id=1, source_target_pairs={{0,38},{2,36},{4,34},{6,32},{32,6},{34,4},{36,2},{38,0},{1,39},{3,... | collective-permute-start | bytes 221192 | tf_op jit(solution)/shard_map/ppermute | solution.py:282
  96.6 3.1 %collective-permute-done.22 = bf16[16,2304]{1,0:T(8,128)(2,1)S(1)} collective-permute-done((bf16[16,2304]{1,0:T(8,128)(2,1)S(1)}, bf16[16,2304]{1,0:T(8,128)(2,1)S(1)}, u32[]{:S(2)}, u32[]{:S(2)}) %collective-permute-start.22) | collective-permute-done | bytes 73760 | tf_op jit(solution)/shard_map/ppermute | solution.py:282
  99.9 2.4 %collective-permute-start.24 = (bf16[4,2304]{1,0:T(4,128)(2,1)S(1)}, bf16[4,2304]{1,0:T(4,128)(2,1)S(1)}, u32[]{:S(2)}, u32[]{:S(2)}) collective-permute-start(bf16[4,2304]{1,0:T(4,128)(2,1)S(1)} %get-tuple-element.58), channel_id=1, source_target_pairs={{0,4},{2,6},{4,0},{6,2},{1,5},{3,7},{5,1},{7,3},{8,12},{10,14},{12... | collective-permute-start | bytes 55304 | tf_op jit(solution)/shard_map/ppermute | solution.py:286
  102.3 1.4 %collective-permute-start.25 = (bf16[4,2304]{1,0:T(4,128)(2,1)S(1)}, bf16[4,2304]{1,0:T(4,128)(2,1)S(1)}, u32[]{:S(2)}, u32[]{:S(2)}) collective-permute-start(bf16[4,2304]{1,0:T(4,128)(2,1)S(1)} %get-tuple-element.57), channel_id=1, source_target_pairs={{0,2},{2,4},{4,6},{6,0},{1,3},{3,5},{5,7},{7,1},{8,10},{10,12},{12... | collective-permute-start | bytes 55304 | tf_op jit(solution)/shard_map/ppermute | solution.py:286
  104.7 3.2 %collective-permute-done.25 = bf16[4,2304]{1,0:T(4,128)(2,1)S(1)} collective-permute-done((bf16[4,2304]{1,0:T(4,128)(2,1)S(1)}, bf16[4,2304]{1,0:T(4,128)(2,1)S(1)}, u32[]{:S(2)}, u32[]{:S(2)}) %collective-permute-start.25) | collective-permute-done | bytes 18464 | tf_op jit(solution)/shard_map/ppermute | solution.py:286
  (50 shorter events, 13.2 us)
Async XLA Ops:
  0.0 8.4 %collective-permute-start = (bf16[180,2304]{1,0:T(8,128)(2,1)}, bf16[180,2304]{1,0:T(8,128)(2,1)S(1)}, u32[]{:S(2)}, u32[]{:S(2)}) collective-permute-start(bf16[180,2304]{1,0:T(8,128)(2,1)} %bitcast.11), channel_id=1, source_target_pairs={{0,1},{1,0},{2,3},{3,2},{4,5},{5,4},{6,7},{7,6},{8,9},{9,8},{10,11... | collective-permute-start | bytes 2488328 | tf_op jit(solution)/shard_map/ppermute | solution.py:278
  0.0 8.4 %collective-permute-start.1 = (bf16[180,2304]{1,0:T(8,128)(2,1)}, bf16[180,2304]{1,0:T(8,128)(2,1)S(1)}, u32[]{:S(2)}, u32[]{:S(2)}) collective-permute-start(bf16[180,2304]{1,0:T(8,128)(2,1)} %bitcast.13), channel_id=1, source_target_pairs={{0,1},{1,0},{2,3},{3,2},{4,5},{5,4},{6,7},{7,6},{8,9},{9,8},{10,11... | collective-permute-start | bytes 2488328 | tf_op jit(solution)/shard_map/ppermute | solution.py:278
  0.5 7.9 %collective-permute-start.2 = (bf16[180,2304]{1,0:T(8,128)(2,1)}, bf16[180,2304]{1,0:T(8,128)(2,1)S(1)}, u32[]{:S(2)}, u32[]{:S(2)}) collective-permute-start(bf16[180,2304]{1,0:T(8,128)(2,1)} %bitcast.15), channel_id=1, source_target_pairs={{0,1},{1,0},{2,3},{3,2},{4,5},{5,4},{6,7},{7,6},{8,9},{9,8},{10,11... | collective-permute-start | bytes 2488328 | tf_op jit(solution)/shard_map/ppermute | solution.py:278
  0.5 13.8 %copy-start.4 = (s32[32]{0:T(128)S(1)}, s32[32]{0:T(128)}, u32[]{:S(2)}) copy-start(s32[32]{0:T(128)} %param.20) | copy-start | bytes 388
  0.5 21.6 %copy-start.5 = (bf16[2304]{0:T(1024)(128)(2,1)S(1)}, bf16[2304]{0:T(1024)(128)(2,1)}, u32[]{:S(2)}) copy-start(bf16[2304]{0:T(1024)(128)(2,1)} %param.15) | copy-start | bytes 13828
  0.5 50.7 %copy-start.2 = (bf16[1,180,2304]{2,1,0:T(8,128)(2,1)S(1)}, bf16[1,180,2304]{2,1,0:T(8,128)(2,1)}, u32[]{:S(2)}) copy-start(bf16[1,180,2304]{2,1,0:T(8,128)(2,1)} %param.25) | copy-start | bytes 2488324
  8.4 42.9 %copy-start = (bf16[1,2304,180]{1,2,0:T(8,128)(2,1)S(1)}, bf16[1,2304,180]{1,2,0:T(8,128)(2,1)}, u32[]{:S(2)}) copy-start(bf16[1,2304,180]{1,2,0:T(8,128)(2,1)} %param.23) | copy-start | bytes 2488324
  8.4 42.9 %copy-start.1 = (bf16[1,2304,180]{1,2,0:T(8,128)(2,1)S(1)}, bf16[1,2304,180]{1,2,0:T(8,128)(2,1)}, u32[]{:S(2)}) copy-start(bf16[1,2304,180]{1,2,0:T(8,128)(2,1)} %param.24) | copy-start | bytes 2488324
  8.4 5.9 %collective-permute-start.3 = (bf16[16,2432]{1,0:T(8,128)(2,1)}, bf16[16,2432]{1,0:T(8,128)(2,1)S(1)}, u32[]{:S(2)}, u32[]{:S(2)}) collective-permute-start(bf16[16,2432]{1,0:T(8,128)(2,1)} %get-tuple-element.33), channel_id=1, source_target_pairs={{0,1},{1,0},{2,3},{3,2},{4,5},{5,4},{6,7},{7,6},{8,9},{9,8},{10,11... | collective-permute-start | bytes 233480 | tf_op jit(solution)/shard_map/ppermute | solution.py:278
  9.0 4.2 %collective-permute-start.4 = (bf16[8,2432]{1,0:T(8,128)(2,1)}, bf16[8,2432]{1,0:T(8,128)(2,1)S(1)}, u32[]{:S(2)}, u32[]{:S(2)}) collective-permute-start(bf16[8,2432]{1,0:T(8,128)(2,1)} %get-tuple-element.34), channel_id=1, source_target_pairs={{0,8},{8,0},{1,9},{9,1},{2,10},{10,2},{3,11},{11,3},{4,12},{12,4},... | collective-permute-start | bytes 116744 | tf_op jit(solution)/shard_map/ppermute | solution.py:278
  10.3 4.0 %collective-permute-start.5 = (bf16[8,2432]{1,0:T(8,128)(2,1)}, bf16[8,2432]{1,0:T(8,128)(2,1)S(1)}, u32[]{:S(2)}, u32[]{:S(2)}) collective-permute-start(bf16[8,2432]{1,0:T(8,128)(2,1)} %get-tuple-element.34), channel_id=1, source_target_pairs={{0,9},{1,8},{8,1},{9,0},{2,11},{3,10},{10,3},{11,2},{4,13},{5,12},... | collective-permute-start | bytes 116744 | tf_op jit(solution)/shard_map/ppermute | solution.py:363
  14.3 0.9 copy-start.3
  15.8 8.4 %collective-permute-start.6 = (bf16[16,3072]{1,0:T(8,128)(2,1)S(1)}, bf16[16,3072]{1,0:T(8,128)(2,1)S(1)}, u32[]{:S(2)}, u32[]{:S(2)}) collective-permute-start(bf16[16,3072]{1,0:T(8,128)(2,1)S(1)} %chip.1.p0), channel_id=1, source_target_pairs={{0,2},{2,4},{4,6},{6,0},{1,3},{3,5},{5,7},{7,1},{8,10},{10,12},{12... | collective-permute-start | bytes 294920 | tf_op jit(solution)/shard_map/ppermute | solution.py:286
  17.8 10.1 %collective-permute-start.7 = (bf16[16,3072]{1,0:T(8,128)(2,1)S(1)}, bf16[16,3072]{1,0:T(8,128)(2,1)S(1)}, u32[]{:S(2)}, u32[]{:S(2)}) collective-permute-start(bf16[16,3072]{1,0:T(8,128)(2,1)S(1)} %chip.1.p0), channel_id=1, source_target_pairs={{0,4},{2,6},{4,0},{6,2},{1,5},{3,7},{5,1},{7,3},{8,12},{10,14},{12... | collective-permute-start | bytes 294920 | tf_op jit(solution)/shard_map/ppermute | solution.py:286
  21.1 6.8 %collective-permute-start.8 = (bf16[16,3072]{1,0:T(8,128)(2,1)S(1)}, bf16[16,3072]{1,0:T(8,128)(2,1)S(1)}, u32[]{:S(2)}, u32[]{:S(2)}) collective-permute-start(bf16[16,3072]{1,0:T(8,128)(2,1)S(1)} %chip.1.p0), channel_id=1, source_target_pairs={{0,6},{2,0},{4,2},{6,4},{1,7},{3,1},{5,3},{7,5},{8,14},{10,8},{12,... | collective-permute-start | bytes 294920 | tf_op jit(solution)/shard_map/ppermute | solution.py:286
  28.8 9.4 %collective-permute-start.9 = (bf16[16,2432]{1,0:T(8,128)(2,1)S(1)}, bf16[16,2432]{1,0:T(8,128)(2,1)S(1)}, u32[]{:S(2)}, u32[]{:S(2)}) collective-permute-start(bf16[16,2432]{1,0:T(8,128)(2,1)S(1)} %get-tuple-element.39.refs_0_), channel_id=1, source_target_pairs={{0,38},{2,36},{4,34},{6,32},{32,6},{34,4},{36,2},{38,0},{1,39},{3,... | collective-permute-start | bytes 233480 | tf_op jit(solution)/shard_map/ppermute | solution.py:282
  38.2 6.5 %collective-permute-start.10 = (bf16[32,2432]{1,0:T(8,128)(2,1)S(1)}, bf16[32,2432]{1,0:T(8,128)(2,1)S(1)}, u32[]{:S(2)}, u32[]{:S(2)}) collective-permute-start(bf16[32,2432]{1,0:T(8,128)(2,1)S(1)} %join.2.refs_0_), channel_id=1, source_target_pairs={{0,64},{1,9},{8,72},{9,17},{16,80},{17,25},{24,88},{25,1},{64,128}... | collective-permute-start | bytes 466952 | tf_op jit(solution)/shard_map/ppermute | solution.py:297
  39.8 5.2 %collective-permute-start.11 = (bf16[32,2432]{1,0:T(8,128)(2,1)S(1)}, bf16[32,2432]{1,0:T(8,128)(2,1)S(1)}, u32[]{:S(2)}, u32[]{:S(2)}) collective-permute-start(bf16[32,2432]{1,0:T(8,128)(2,1)S(1)} %join.2.refs_0_), channel_id=1, source_target_pairs={{0,192},{1,25},{8,200},{9,1},{16,208},{17,9},{24,216},{25,17},{64,... | collective-permute-start | bytes 466952 | tf_op jit(solution)/shard_map/ppermute | solution.py:297
  41.5 6.7 %collective-permute-start.12 = (bf16[32,2432]{1,0:T(8,128)(2,1)S(1)}, bf16[32,2432]{1,0:T(8,128)(2,1)S(1)}, u32[]{:S(2)}, u32[]{:S(2)}) collective-permute-start(bf16[32,2432]{1,0:T(8,128)(2,1)S(1)} %join.2.refs_0_), channel_id=1, source_target_pairs={{0,128},{1,17},{8,136},{9,25},{16,144},{17,1},{24,152},{25,9},{64,... | collective-permute-start | bytes 466952 | tf_op jit(solution)/shard_map/ppermute | solution.py:297
  48.3 12.1 %collective-permute-start.13 = (bf16[128,2432]{1,0:T(8,128)(2,1)S(1)}, bf16[128,2432]{1,0:T(8,128)(2,1)S(1)}, u32[]{:S(2)}, u32[]{:S(2)}) collective-permute-start(bf16[128,2432]{1,0:T(8,128)(2,1)S(1)} %join.3.x_ref), channel_id=1, source_target_pairs={{0,16},{1,129},{8,24},{9,137},{16,0},{17,145},{24,8},{25,153},{64,... | collective-permute-start | bytes 1867784 | tf_op jit(solution)/shard_map/ppermute | solution.py:297
  49.2 16.9 %collective-permute-start.15 = (bf16[128,2432]{1,0:T(8,128)(2,1)S(1)}, bf16[128,2432]{1,0:T(8,128)(2,1)S(1)}, u32[]{:S(2)}, u32[]{:S(2)}) collective-permute-start(bf16[128,2432]{1,0:T(8,128)(2,1)S(1)} %join.3.x_ref), channel_id=1, source_target_pairs={{0,8},{1,65},{8,16},{9,73},{16,24},{17,81},{24,0},{25,89},{64,72},... | collective-permute-start | bytes 1867784 | tf_op jit(solution)/shard_map/ppermute | solution.py:297
  50.4 19.0 %collective-permute-start.17 = (bf16[128,2432]{1,0:T(8,128)(2,1)S(1)}, bf16[128,2432]{1,0:T(8,128)(2,1)S(1)}, u32[]{:S(2)}, u32[]{:S(2)}) collective-permute-start(bf16[128,2432]{1,0:T(8,128)(2,1)S(1)} %join.3.x_ref), channel_id=1, source_target_pairs={{0,24},{1,193},{8,0},{9,201},{16,8},{17,209},{24,16},{25,217},{64,... | collective-permute-start | bytes 1867784 | tf_op jit(solution)/shard_map/ppermute | solution.py:297
  62.1 11.5 %collective-permute-start.14 = (bf16[128,2304]{1,0:T(8,128)(2,1)S(1)}, bf16[128,2304]{1,0:T(8,128)(2,1)S(1)}, u32[]{:S(2)}, u32[]{:S(2)}) collective-permute-start(bf16[128,2304]{1,0:T(8,128)(2,1)S(1)} %mlp.5), channel_id=1, source_target_pairs={{0,16},{1,129},{8,24},{9,137},{16,0},{17,145},{24,8},{25,153},{64,... | collective-permute-start | bytes 1769480 | tf_op jit(solution)/shard_map/ppermute | solution.py:297
  67.8 10.4 %collective-permute-start.16 = (bf16[128,2304]{1,0:T(8,128)(2,1)S(1)}, bf16[128,2304]{1,0:T(8,128)(2,1)S(1)}, u32[]{:S(2)}, u32[]{:S(2)}) collective-permute-start(bf16[128,2304]{1,0:T(8,128)(2,1)S(1)} %mlp.6), channel_id=1, source_target_pairs={{0,24},{1,193},{8,0},{9,201},{16,8},{17,209},{24,16},{25,217},{64,... | collective-permute-start | bytes 1769480 | tf_op jit(solution)/shard_map/ppermute | solution.py:297
  71.1 11.1 %collective-permute-start.18 = (bf16[128,2304]{1,0:T(8,128)(2,1)S(1)}, bf16[128,2304]{1,0:T(8,128)(2,1)S(1)}, u32[]{:S(2)}, u32[]{:S(2)}) collective-permute-start(bf16[128,2304]{1,0:T(8,128)(2,1)S(1)} %mlp.7), channel_id=1, source_target_pairs={{0,8},{1,65},{8,16},{9,73},{16,24},{17,81},{24,0},{25,89},{64,72},... | collective-permute-start | bytes 1769480 | tf_op jit(solution)/shard_map/ppermute | solution.py:297
  82.5 5.2 %collective-permute-start.19 = (bf16[32,2304]{1,0:T(8,128)(2,1)S(1)}, bf16[32,2304]{1,0:T(8,128)(2,1)S(1)}, u32[]{:S(2)}, u32[]{:S(2)}) collective-permute-start(bf16[32,2304]{1,0:T(8,128)(2,1)S(1)} %get-tuple-element.53), channel_id=1, source_target_pairs={{0,192},{1,25},{8,200},{9,1},{16,208},{17,9},{24,216},{25,17},{64,... | collective-permute-start | bytes 442376 | tf_op jit(solution)/shard_map/ppermute | solution.py:297
  84.6 7.9 %collective-permute-start.20 = (bf16[32,2304]{1,0:T(8,128)(2,1)S(1)}, bf16[32,2304]{1,0:T(8,128)(2,1)S(1)}, u32[]{:S(2)}, u32[]{:S(2)}) collective-permute-start(bf16[32,2304]{1,0:T(8,128)(2,1)S(1)} %get-tuple-element.55), channel_id=1, source_target_pairs={{0,64},{1,9},{8,72},{9,17},{16,80},{17,25},{24,88},{25,1},{64,128}... | collective-permute-start | bytes 442376 | tf_op jit(solution)/shard_map/ppermute | solution.py:297
  84.6 7.9 %collective-permute-start.21 = (bf16[32,2304]{1,0:T(8,128)(2,1)S(1)}, bf16[32,2304]{1,0:T(8,128)(2,1)S(1)}, u32[]{:S(2)}, u32[]{:S(2)}) collective-permute-start(bf16[32,2304]{1,0:T(8,128)(2,1)S(1)} %get-tuple-element.54), channel_id=1, source_target_pairs={{0,128},{1,17},{8,136},{9,25},{16,144},{17,1},{24,152},{25,9},{64,... | collective-permute-start | bytes 442376 | tf_op jit(solution)/shard_map/ppermute | solution.py:297
  92.6 7.2 %collective-permute-start.22 = (bf16[16,2304]{1,0:T(8,128)(2,1)S(1)}, bf16[16,2304]{1,0:T(8,128)(2,1)S(1)}, u32[]{:S(2)}, u32[]{:S(2)}) collective-permute-start(bf16[16,2304]{1,0:T(8,128)(2,1)S(1)} %slice.45), channel_id=1, source_target_pairs={{0,38},{2,36},{4,34},{6,32},{32,6},{34,4},{36,2},{38,0},{1,39},{3,... | collective-permute-start | bytes 221192 | tf_op jit(solution)/shard_map/ppermute | solution.py:282
  99.8 3.9 %collective-permute-start.23 = (bf16[4,2304]{1,0:T(4,128)(2,1)S(1)}, bf16[4,2304]{1,0:T(4,128)(2,1)S(1)}, u32[]{:S(2)}, u32[]{:S(2)}) collective-permute-start(bf16[4,2304]{1,0:T(4,128)(2,1)S(1)} %get-tuple-element.56), channel_id=1, source_target_pairs={{0,6},{2,0},{4,2},{6,4},{1,7},{3,1},{5,3},{7,5},{8,14},{10,8},{12,... | collective-permute-start | bytes 55304 | tf_op jit(solution)/shard_map/ppermute | solution.py:286
  99.9 4.7 %collective-permute-start.24 = (bf16[4,2304]{1,0:T(4,128)(2,1)S(1)}, bf16[4,2304]{1,0:T(4,128)(2,1)S(1)}, u32[]{:S(2)}, u32[]{:S(2)}) collective-permute-start(bf16[4,2304]{1,0:T(4,128)(2,1)S(1)} %get-tuple-element.58), channel_id=1, source_target_pairs={{0,4},{2,6},{4,0},{6,2},{1,5},{3,7},{5,1},{7,3},{8,12},{10,14},{12... | collective-permute-start | bytes 55304 | tf_op jit(solution)/shard_map/ppermute | solution.py:286
  102.3 5.6 %collective-permute-start.25 = (bf16[4,2304]{1,0:T(4,128)(2,1)S(1)}, bf16[4,2304]{1,0:T(4,128)(2,1)S(1)}, u32[]{:S(2)}, u32[]{:S(2)}) collective-permute-start(bf16[4,2304]{1,0:T(4,128)(2,1)S(1)} %get-tuple-element.57), channel_id=1, source_target_pairs={{0,2},{2,4},{4,6},{6,0},{1,3},{3,5},{5,7},{7,1},{8,10},{10,12},{12... | collective-permute-start | bytes 55304 | tf_op jit(solution)/shard_map/ppermute | solution.py:286

commit v4 on v3

--- a/solution.py
+++ b/solution.py
@@ -375,12 +375,14 @@
         compiler_params=vmem(16),
         name="hold",
     )(*mine, *theirs)
+    across_2, across_1, across_3 = (along_line(chip, s) for s in (2, 1, 3))
+    lines = (across_1, across_2, across_3)
     attn, normed = pl.pallas_call(
         norm_kernel,
         out_shape=(jax.ShapeDtypeStruct((own, D), BF16), jax.ShapeDtypeStruct((half, W), BF16)),
         compiler_params=vmem(8),
         name="norm",
-    )(chip, *[along_line(chip, s) for s in (1, 2, 3)], gain.reshape(1, D))
+    )(chip, *lines, gain.reshape(1, D))
 
     def mlp(block):
         return pl.pallas_call(

time: 109 us -> 109 us (level)
  no operation moved by 1% of the time
where the time goes in v4:
time: 109 us; the launch traced here: 108 us
  waiting for transfers between devices  53 us (49%)
  starting transfers between devices  36.8 us (34%)
  Pallas kernels  16.5 us (15%)
    ppermute x12, waiting for transfers between devices, along_plane(): return lax.ppermute(array, PLANE, pairs)  32.1 us
    ppermute x12, starting transfers between devices, along_plane(): return lax.ppermute(array, PLANE, pairs)  14.6 us
    ppermute x6, starting transfers between devices, along_line(): return lax.ppermute(array, 'zl', [(i, (i + shift) % n) for i in range(n)])  10.1 us
    ppermute x6, waiting for transfers between devices, along_line(): return lax.ppermute(array, 'zl', [(i, (i + shift) % n) for i in range(n)])  9.94 us
    ppermute x2, starting transfers between devices, mirrored(): return lax.ppermute(array, ('zh', 'zl'), [(i, 7 - i) for i in range(8)])  9.55 us
    pallas_call x1, Pallas kernels, on_device(): pl.pallas_call(attn_kernel, out_shape=(jax.ShapeDtypeStruct((half, WX), B...  7.82 us
    ppermute x2, waiting for transfers between devices, mirrored(): return lax.ppermute(array, ('zh', 'zl'), [(i, 7 - i) for i in range(8)])  7.04 us
    pallas_call x4, Pallas kernels, mlp(): pl.pallas_call(mlp_kernel, out_shape=jax.ShapeDtypeStruct((block.shape[0]...  6.82 us
  transfers between devices with their start and end apart: 26, of which 18 were waited for; matrix products, arithmetic and copies ran while one was open for 0% of the time, Pallas kernels for 14%

profile of v4, /device:TPU:16, one launch (start us, length us, event | category | flops | bytes accessed | tf_op | source)
XLA Modules:
  0.0 108.5 jit_solution(10086391202799092645)
XLA Ops:
  0.5 7.8 %attn.1 = (bf16[16,3072]{1,0:T(8,128)(2,1)}, bf16[16,2432]{1,0:T(8,128)(2,1)}, bf16[8,2432]{1,0:T(8,128)(2,1)}) custom-call(bf16[32,2304]{1,0:T(8,128)(2,1)} %q_ref.1, s32[32,32]{1,0:T(8,128)} %table_ref.1, s32[1,32]{1,0:T(1,128)} %bitcast.20, s32[1,32]{1,0:T(1,128)} %bitcast.17, bf16[4,2304]{1,0:T(4,128)(2,1)} %res_ref.1, s32[2,4]{1,0:T(2,128)} %bitcast.19, ...), custom_call_target="tpu_custom_call" | custom-call | flops 2000000000 | bytes 10000000 | tf_op jit(solution)/shard_map/attn/pallas_call | solution.py:338
  9.0 1.3 %collective-permute-start.4 = (bf16[8,2432]{1,0:T(8,128)(2,1)}, bf16[8,2432]{1,0:T(8,128)(2,1)S(1)}, u32[]{:S(2)}, u32[]{:S(2)}) collective-permute-start(bf16[8,2432]{1,0:T(8,128)(2,1)} %get-tuple-element.34), channel_id=1, source_target_pairs={{0,8},{8,0},{1,9},{9,1},{2,10},{10,2},{3,11},{11,3},{4,12},{12,4},... | collective-permute-start | bytes 116744 | tf_op jit(solution)/shard_map/ppermute | solution.py:278
  10.5 2.7 %collective-permute-done.4.far_0_ref = bf16[8,2432]{1,0:T(8,128)(2,1)S(1)} collective-permute-done((bf16[8,2432]{1,0:T(8,128)(2,1)}, bf16[8,2432]{1,0:T(8,128)(2,1)S(1)}, u32[]{:S(2)}, u32[]{:S(2)}) %collective-permute-start.4) | collective-permute-done | bytes 38944 | tf_op jit(solution)/shard_map/ppermute | solution.py:278
  15.8 2.0 %collective-permute-start.6 = (bf16[16,3072]{1,0:T(8,128)(2,1)S(1)}, bf16[16,3072]{1,0:T(8,128)(2,1)S(1)}, u32[]{:S(2)}, u32[]{:S(2)}) collective-permute-start(bf16[16,3072]{1,0:T(8,128)(2,1)S(1)} %chip.1.p0), channel_id=1, source_target_pairs={{0,2},{2,4},{4,6},{6,0},{1,3},{3,5},{5,7},{7,1},{8,10},{10,12},{12... | collective-permute-start | bytes 294920 | tf_op jit(solution)/shard_map/ppermute | solution.py:286
  17.8 3.3 %collective-permute-start.7 = (bf16[16,3072]{1,0:T(8,128)(2,1)S(1)}, bf16[16,3072]{1,0:T(8,128)(2,1)S(1)}, u32[]{:S(2)}, u32[]{:S(2)}) collective-permute-start(bf16[16,3072]{1,0:T(8,128)(2,1)S(1)} %chip.1.p0), channel_id=1, source_target_pairs={{0,4},{2,6},{4,0},{6,2},{1,5},{3,7},{5,1},{7,3},{8,12},{10,14},{12... | collective-permute-start | bytes 294920 | tf_op jit(solution)/shard_map/ppermute | solution.py:286
  22.1 2.1 %collective-permute-done.6.p1 = bf16[16,3072]{1,0:T(8,128)(2,1)S(1)} collective-permute-done((bf16[16,3072]{1,0:T(8,128)(2,1)S(1)}, bf16[16,3072]{1,0:T(8,128)(2,1)S(1)}, u32[]{:S(2)}, u32[]{:S(2)}) %collective-permute-start.6) | collective-permute-done | bytes 98336 | tf_op jit(solution)/shard_map/ppermute | solution.py:286
  24.2 3.7 %collective-permute-done.7.p2 = bf16[16,3072]{1,0:T(8,128)(2,1)S(1)} collective-permute-done((bf16[16,3072]{1,0:T(8,128)(2,1)S(1)}, bf16[16,3072]{1,0:T(8,128)(2,1)S(1)}, u32[]{:S(2)}, u32[]{:S(2)}) %collective-permute-start.7) | collective-permute-done | bytes 98336 | tf_op jit(solution)/shard_map/ppermute | solution.py:286
  28.8 5.5 %collective-permute-start.9 = (bf16[16,2432]{1,0:T(8,128)(2,1)S(1)}, bf16[16,2432]{1,0:T(8,128)(2,1)S(1)}, u32[]{:S(2)}, u32[]{:S(2)}) collective-permute-start(bf16[16,2432]{1,0:T(8,128)(2,1)S(1)} %get-tuple-element.39.refs_0_), channel_id=1, source_target_pairs={{0,38},{2,36},{4,34},{6,32},{32,6},{34,4},{36,2},{38,0},{1,39},{3,... | collective-permute-start | bytes 233480 | tf_op jit(solution)/shard_map/ppermute | solution.py:282
  34.3 3.9 %collective-permute-done.9.refs_1_ = bf16[16,2432]{1,0:T(8,128)(2,1)S(1)} collective-permute-done((bf16[16,2432]{1,0:T(8,128)(2,1)S(1)}, bf16[16,2432]{1,0:T(8,128)(2,1)S(1)}, u32[]{:S(2)}, u32[]{:S(2)}) %collective-permute-start.9) | collective-permute-done | bytes 77856 | tf_op jit(solution)/shard_map/ppermute | solution.py:282
  38.2 1.6 %collective-permute-start.10 = (bf16[32,2432]{1,0:T(8,128)(2,1)S(1)}, bf16[32,2432]{1,0:T(8,128)(2,1)S(1)}, u32[]{:S(2)}, u32[]{:S(2)}) collective-permute-start(bf16[32,2432]{1,0:T(8,128)(2,1)S(1)} %join.2.refs_0_), channel_id=1, source_target_pairs={{0,64},{1,9},{8,72},{9,17},{16,80},{17,25},{24,88},{25,1},{64,128}... | collective-permute-start | bytes 466952 | tf_op jit(solution)/shard_map/ppermute | solution.py:297
  39.8 1.7 %collective-permute-start.11 = (bf16[32,2432]{1,0:T(8,128)(2,1)S(1)}, bf16[32,2432]{1,0:T(8,128)(2,1)S(1)}, u32[]{:S(2)}, u32[]{:S(2)}) collective-permute-start(bf16[32,2432]{1,0:T(8,128)(2,1)S(1)} %join.2.refs_0_), channel_id=1, source_target_pairs={{0,192},{1,25},{8,200},{9,1},{16,208},{17,9},{24,216},{25,17},{64,... | collective-permute-start | bytes 466952 | tf_op jit(solution)/shard_map/ppermute | solution.py:297
  41.5 1.8 %collective-permute-start.12 = (bf16[32,2432]{1,0:T(8,128)(2,1)S(1)}, bf16[32,2432]{1,0:T(8,128)(2,1)S(1)}, u32[]{:S(2)}, u32[]{:S(2)}) collective-permute-start(bf16[32,2432]{1,0:T(8,128)(2,1)S(1)} %join.2.refs_0_), channel_id=1, source_target_pairs={{0,128},{1,17},{8,136},{9,25},{16,144},{17,1},{24,152},{25,9},{64,... | collective-permute-start | bytes 466952 | tf_op jit(solution)/shard_map/ppermute | solution.py:297
  43.4 1.4 %collective-permute-done.10.refs_1_ = bf16[32,2432]{1,0:T(8,128)(2,1)S(1)} collective-permute-done((bf16[32,2432]{1,0:T(8,128)(2,1)S(1)}, bf16[32,2432]{1,0:T(8,128)(2,1)S(1)}, u32[]{:S(2)}, u32[]{:S(2)}) %collective-permute-start.10) | collective-permute-done | bytes 155680 | tf_op jit(solution)/shard_map/ppermute | solution.py:297
  45.0 3.2 %collective-permute-done.12.refs_3_ = bf16[32,2432]{1,0:T(8,128)(2,1)S(1)} collective-permute-done((bf16[32,2432]{1,0:T(8,128)(2,1)S(1)}, bf16[32,2432]{1,0:T(8,128)(2,1)S(1)}, u32[]{:S(2)}, u32[]{:S(2)}) %collective-permute-start.12) | collective-permute-done | bytes 155680 | tf_op jit(solution)/shard_map/ppermute | solution.py:297
  51.6 8.8 %collective-permute-done.13.x_ref = bf16[128,2432]{1,0:T(8,128)(2,1)S(1)} collective-permute-done((bf16[128,2432]{1,0:T(8,128)(2,1)S(1)}, bf16[128,2432]{1,0:T(8,128)(2,1)S(1)}, u32[]{:S(2)}, u32[]{:S(2)}) %collective-permute-start.13) | collective-permute-done | bytes 622624 | tf_op jit(solution)/shard_map/ppermute | solution.py:297
  60.4 1.7 %mlp.5 = bf16[128,2304]{1,0:T(8,128)(2,1)S(1)} custom-call(bf16[128,2432]{1,0:T(8,128)(2,1)S(1)} %collective-permute-done.13.x_ref, bf16[180,2304]{1,0:T(8,128)(2,1)S(1)} %get-tuple-element.46.gate_0, bf16[180,2304]{1,0:T(8,128)(2,1)S(1)} %get-tuple-element.47.up_0, bf16[180,2304]{1,0:T(8,128)(2,1)S(1)} %get-tuple-element.48.down_0, ...), custom_call_target="tpu_custom_call" | custom-call | flops 3000000000 | bytes 10000000 | tf_op jit(solution)/shard_map/mlp/pallas_call | solution.py:388
  62.8 3.3 %collective-permute-done.15.x_ref = bf16[128,2432]{1,0:T(8,128)(2,1)S(1)} collective-permute-done((bf16[128,2432]{1,0:T(8,128)(2,1)S(1)}, bf16[128,2432]{1,0:T(8,128)(2,1)S(1)}, u32[]{:S(2)}, u32[]{:S(2)}) %collective-permute-start.15) | collective-permute-done | bytes 622624 | tf_op jit(solution)/shard_map/ppermute | solution.py:297
  66.1 1.7 %mlp.6 = bf16[128,2304]{1,0:T(8,128)(2,1)S(1)} custom-call(bf16[128,2432]{1,0:T(8,128)(2,1)S(1)} %collective-permute-done.15.x_ref, bf16[180,2304]{1,0:T(8,128)(2,1)S(1)} %get-tuple-element.46.gate_0, bf16[180,2304]{1,0:T(8,128)(2,1)S(1)} %get-tuple-element.47.up_0, bf16[180,2304]{1,0:T(8,128)(2,1)S(1)} %get-tuple-element.48.down_0, ...), custom_call_target="tpu_custom_call" | custom-call | flops 3000000000 | bytes 10000000 | tf_op jit(solution)/shard_map/mlp/pallas_call | solution.py:388
  67.8 1.6 %collective-permute-start.16 = (bf16[128,2304]{1,0:T(8,128)(2,1)S(1)}, bf16[128,2304]{1,0:T(8,128)(2,1)S(1)}, u32[]{:S(2)}, u32[]{:S(2)}) collective-permute-start(bf16[128,2304]{1,0:T(8,128)(2,1)S(1)} %mlp.6), channel_id=1, source_target_pairs={{0,24},{1,193},{8,0},{9,201},{16,8},{17,209},{24,16},{25,217},{64,... | collective-permute-start | bytes 1769480 | tf_op jit(solution)/shard_map/ppermute | solution.py:297
  69.4 1.7 %mlp.7 = bf16[128,2304]{1,0:T(8,128)(2,1)S(1)} custom-call(bf16[128,2432]{1,0:T(8,128)(2,1)S(1)} %collective-permute-done.17.x_ref, bf16[180,2304]{1,0:T(8,128)(2,1)S(1)} %get-tuple-element.46.gate_0, bf16[180,2304]{1,0:T(8,128)(2,1)S(1)} %get-tuple-element.47.up_0, bf16[180,2304]{1,0:T(8,128)(2,1)S(1)} %get-tuple-element.48.down_0, ...), custom_call_target="tpu_custom_call" | custom-call | flops 3000000000 | bytes 10000000 | tf_op jit(solution)/shard_map/mlp/pallas_call | solution.py:388
  71.7 1.7 %mlp.4 = bf16[128,2304]{1,0:T(8,128)(2,1)S(1)} custom-call(bf16[128,2432]{1,0:T(8,128)(2,1)S(1)} %join.3.x_ref, bf16[180,2304]{1,0:T(8,128)(2,1)S(1)} %get-tuple-element.46.gate_0, bf16[180,2304]{1,0:T(8,128)(2,1)S(1)} %get-tuple-element.47.up_0, bf16[180,2304]{1,0:T(8,128)(2,1)S(1)} %get-tuple-element.48.down_0, ...), custom_call_target="tpu_custom_call" | custom-call | flops 3000000000 | bytes 10000000 | tf_op jit(solution)/shard_map/mlp/pallas_call | solution.py:388
  73.6 4.6 %collective-permute-done.16 = bf16[128,2304]{1,0:T(8,128)(2,1)S(1)} collective-permute-done((bf16[128,2304]{1,0:T(8,128)(2,1)S(1)}, bf16[128,2304]{1,0:T(8,128)(2,1)S(1)}, u32[]{:S(2)}, u32[]{:S(2)}) %collective-permute-start.16) | collective-permute-done | bytes 589856 | tf_op jit(solution)/shard_map/ppermute | solution.py:297
  78.2 3.9 %collective-permute-done.18 = bf16[128,2304]{1,0:T(8,128)(2,1)S(1)} collective-permute-done((bf16[128,2304]{1,0:T(8,128)(2,1)S(1)}, bf16[128,2304]{1,0:T(8,128)(2,1)S(1)}, u32[]{:S(2)}, u32[]{:S(2)}) %collective-permute-start.18) | collective-permute-done | bytes 589856 | tf_op jit(solution)/shard_map/ppermute | solution.py:297
  82.5 2.0 %collective-permute-start.19 = (bf16[32,2304]{1,0:T(8,128)(2,1)S(1)}, bf16[32,2304]{1,0:T(8,128)(2,1)S(1)}, u32[]{:S(2)}, u32[]{:S(2)}) collective-permute-start(bf16[32,2304]{1,0:T(8,128)(2,1)S(1)} %get-tuple-element.53), channel_id=1, source_target_pairs={{0,192},{1,25},{8,200},{9,1},{16,208},{17,9},{24,216},{25,17},{64,... | collective-permute-start | bytes 442376 | tf_op jit(solution)/shard_map/ppermute | solution.py:297
  84.6 1.5 %collective-permute-start.21 = (bf16[32,2304]{1,0:T(8,128)(2,1)S(1)}, bf16[32,2304]{1,0:T(8,128)(2,1)S(1)}, u32[]{:S(2)}, u32[]{:S(2)}) collective-permute-start(bf16[32,2304]{1,0:T(8,128)(2,1)S(1)} %get-tuple-element.54), channel_id=1, source_target_pairs={{0,128},{1,17},{8,136},{9,25},{16,144},{17,1},{24,152},{25,9},{64,... | collective-permute-start | bytes 442376 | tf_op jit(solution)/shard_map/ppermute | solution.py:297
  86.1 1.6 %collective-permute-done.19 = bf16[32,2304]{1,0:T(8,128)(2,1)S(1)} collective-permute-done((bf16[32,2304]{1,0:T(8,128)(2,1)S(1)}, bf16[32,2304]{1,0:T(8,128)(2,1)S(1)}, u32[]{:S(2)}, u32[]{:S(2)}) %collective-permute-start.19) | collective-permute-done | bytes 147488 | tf_op jit(solution)/shard_map/ppermute | solution.py:297
  87.8 4.7 %collective-permute-done.20 = bf16[32,2304]{1,0:T(8,128)(2,1)S(1)} collective-permute-done((bf16[32,2304]{1,0:T(8,128)(2,1)S(1)}, bf16[32,2304]{1,0:T(8,128)(2,1)S(1)}, u32[]{:S(2)}, u32[]{:S(2)}) %collective-permute-start.20) | collective-permute-done | bytes 147488 | tf_op jit(solution)/shard_map/ppermute | solution.py:297
  92.6 4.0 %collective-permute-start.22 = (bf16[16,2304]{1,0:T(8,128)(2,1)S(1)}, bf16[16,2304]{1,0:T(8,128)(2,1)S(1)}, u32[]{:S(2)}, u32[]{:S(2)}) collective-permute-start(bf16[16,2304]{1,0:T(8,128)(2,1)S(1)} %slice.45), channel_id=1, source_target_pairs={{0,38},{2,36},{4,34},{6,32},{32,6},{34,4},{36,2},{38,0},{1,39},{3,... | collective-permute-start | bytes 221192 | tf_op jit(solution)/shard_map/ppermute | solution.py:282
  96.6 3.1 %collective-permute-done.22 = bf16[16,2304]{1,0:T(8,128)(2,1)S(1)} collective-permute-done((bf16[16,2304]{1,0:T(8,128)(2,1)S(1)}, bf16[16,2304]{1,0:T(8,128)(2,1)S(1)}, u32[]{:S(2)}, u32[]{:S(2)}) %collective-permute-start.22) | collective-permute-done | bytes 73760 | tf_op jit(solution)/shard_map/ppermute | solution.py:282
  99.9 2.4 %collective-permute-start.24 = (bf16[4,2304]{1,0:T(4,128)(2,1)S(1)}, bf16[4,2304]{1,0:T(4,128)(2,1)S(1)}, u32[]{:S(2)}, u32[]{:S(2)}) collective-permute-start(bf16[4,2304]{1,0:T(4,128)(2,1)S(1)} %get-tuple-element.58), channel_id=1, source_target_pairs={{0,4},{2,6},{4,0},{6,2},{1,5},{3,7},{5,1},{7,3},{8,12},{10,14},{12... | collective-permute-start | bytes 55304 | tf_op jit(solution)/shard_map/ppermute | solution.py:286
  102.3 1.4 %collective-permute-start.25 = (bf16[4,2304]{1,0:T(4,128)(2,1)S(1)}, bf16[4,2304]{1,0:T(4,128)(2,1)S(1)}, u32[]{:S(2)}, u32[]{:S(2)}) collective-permute-start(bf16[4,2304]{1,0:T(4,128)(2,1)S(1)} %get-tuple-element.57), channel_id=1, source_target_pairs={{0,2},{2,4},{4,6},{6,0},{1,3},{3,5},{5,7},{7,1},{8,10},{10,12},{12... | collective-permute-start | bytes 55304 | tf_op jit(solution)/shard_map/ppermute | solution.py:286
  104.7 3.2 %collective-permute-done.25 = bf16[4,2304]{1,0:T(4,128)(2,1)S(1)} collective-permute-done((bf16[4,2304]{1,0:T(4,128)(2,1)S(1)}, bf16[4,2304]{1,0:T(4,128)(2,1)S(1)}, u32[]{:S(2)}, u32[]{:S(2)}) %collective-permute-start.25) | collective-permute-done | bytes 18464 | tf_op jit(solution)/shard_map/ppermute | solution.py:286
  (50 shorter events, 13.2 us)
Async XLA Ops:
  0.0 8.4 %collective-permute-start = (bf16[180,2304]{1,0:T(8,128)(2,1)}, bf16[180,2304]{1,0:T(8,128)(2,1)S(1)}, u32[]{:S(2)}, u32[]{:S(2)}) collective-permute-start(bf16[180,2304]{1,0:T(8,128)(2,1)} %bitcast.11), channel_id=1, source_target_pairs={{0,1},{1,0},{2,3},{3,2},{4,5},{5,4},{6,7},{7,6},{8,9},{9,8},{10,11... | collective-permute-start | bytes 2488328 | tf_op jit(solution)/shard_map/ppermute | solution.py:278
  0.0 8.4 %collective-permute-start.1 = (bf16[180,2304]{1,0:T(8,128)(2,1)}, bf16[180,2304]{1,0:T(8,128)(2,1)S(1)}, u32[]{:S(2)}, u32[]{:S(2)}) collective-permute-start(bf16[180,2304]{1,0:T(8,128)(2,1)} %bitcast.13), channel_id=1, source_target_pairs={{0,1},{1,0},{2,3},{3,2},{4,5},{5,4},{6,7},{7,6},{8,9},{9,8},{10,11... | collective-permute-start | bytes 2488328 | tf_op jit(solution)/shard_map/ppermute | solution.py:278
  0.5 7.9 %collective-permute-start.2 = (bf16[180,2304]{1,0:T(8,128)(2,1)}, bf16[180,2304]{1,0:T(8,128)(2,1)S(1)}, u32[]{:S(2)}, u32[]{:S(2)}) collective-permute-start(bf16[180,2304]{1,0:T(8,128)(2,1)} %bitcast.15), channel_id=1, source_target_pairs={{0,1},{1,0},{2,3},{3,2},{4,5},{5,4},{6,7},{7,6},{8,9},{9,8},{10,11... | collective-permute-start | bytes 2488328 | tf_op jit(solution)/shard_map/ppermute | solution.py:278
  0.5 13.8 %copy-start.4 = (s32[32]{0:T(128)S(1)}, s32[32]{0:T(128)}, u32[]{:S(2)}) copy-start(s32[32]{0:T(128)} %param.20) | copy-start | bytes 388
  0.5 21.6 %copy-start.5 = (bf16[2304]{0:T(1024)(128)(2,1)S(1)}, bf16[2304]{0:T(1024)(128)(2,1)}, u32[]{:S(2)}) copy-start(bf16[2304]{0:T(1024)(128)(2,1)} %param.15) | copy-start | bytes 13828
  0.5 50.7 %copy-start.2 = (bf16[1,180,2304]{2,1,0:T(8,128)(2,1)S(1)}, bf16[1,180,2304]{2,1,0:T(8,128)(2,1)}, u32[]{:S(2)}) copy-start(bf16[1,180,2304]{2,1,0:T(8,128)(2,1)} %param.25) | copy-start | bytes 2488324
  8.4 42.9 %copy-start = (bf16[1,2304,180]{1,2,0:T(8,128)(2,1)S(1)}, bf16[1,2304,180]{1,2,0:T(8,128)(2,1)}, u32[]{:S(2)}) copy-start(bf16[1,2304,180]{1,2,0:T(8,128)(2,1)} %param.23) | copy-start | bytes 2488324
  8.4 42.9 %copy-start.1 = (bf16[1,2304,180]{1,2,0:T(8,128)(2,1)S(1)}, bf16[1,2304,180]{1,2,0:T(8,128)(2,1)}, u32[]{:S(2)}) copy-start(bf16[1,2304,180]{1,2,0:T(8,128)(2,1)} %param.24) | copy-start | bytes 2488324
  8.4 5.9 %collective-permute-start.3 = (bf16[16,2432]{1,0:T(8,128)(2,1)}, bf16[16,2432]{1,0:T(8,128)(2,1)S(1)}, u32[]{:S(2)}, u32[]{:S(2)}) collective-permute-start(bf16[16,2432]{1,0:T(8,128)(2,1)} %get-tuple-element.33), channel_id=1, source_target_pairs={{0,1},{1,0},{2,3},{3,2},{4,5},{5,4},{6,7},{7,6},{8,9},{9,8},{10,11... | collective-permute-start | bytes 233480 | tf_op jit(solution)/shard_map/ppermute | solution.py:278
  9.0 4.2 %collective-permute-start.4 = (bf16[8,2432]{1,0:T(8,128)(2,1)}, bf16[8,2432]{1,0:T(8,128)(2,1)S(1)}, u32[]{:S(2)}, u32[]{:S(2)}) collective-permute-start(bf16[8,2432]{1,0:T(8,128)(2,1)} %get-tuple-element.34), channel_id=1, source_target_pairs={{0,8},{8,0},{1,9},{9,1},{2,10},{10,2},{3,11},{11,3},{4,12},{12,4},... | collective-permute-start | bytes 116744 | tf_op jit(solution)/shard_map/ppermute | solution.py:278
  10.3 4.0 %collective-permute-start.5 = (bf16[8,2432]{1,0:T(8,128)(2,1)}, bf16[8,2432]{1,0:T(8,128)(2,1)S(1)}, u32[]{:S(2)}, u32[]{:S(2)}) collective-permute-start(bf16[8,2432]{1,0:T(8,128)(2,1)} %get-tuple-element.34), channel_id=1, source_target_pairs={{0,9},{1,8},{8,1},{9,0},{2,11},{3,10},{10,3},{11,2},{4,13},{5,12},... | collective-permute-start | bytes 116744 | tf_op jit(solution)/shard_map/ppermute | solution.py:363
  14.3 0.9 copy-start.3
  15.8 8.4 %collective-permute-start.6 = (bf16[16,3072]{1,0:T(8,128)(2,1)S(1)}, bf16[16,3072]{1,0:T(8,128)(2,1)S(1)}, u32[]{:S(2)}, u32[]{:S(2)}) collective-permute-start(bf16[16,3072]{1,0:T(8,128)(2,1)S(1)} %chip.1.p0), channel_id=1, source_target_pairs={{0,2},{2,4},{4,6},{6,0},{1,3},{3,5},{5,7},{7,1},{8,10},{10,12},{12... | collective-permute-start | bytes 294920 | tf_op jit(solution)/shard_map/ppermute | solution.py:286
  17.8 10.1 %collective-permute-start.7 = (bf16[16,3072]{1,0:T(8,128)(2,1)S(1)}, bf16[16,3072]{1,0:T(8,128)(2,1)S(1)}, u32[]{:S(2)}, u32[]{:S(2)}) collective-permute-start(bf16[16,3072]{1,0:T(8,128)(2,1)S(1)} %chip.1.p0), channel_id=1, source_target_pairs={{0,4},{2,6},{4,0},{6,2},{1,5},{3,7},{5,1},{7,3},{8,12},{10,14},{12... | collective-permute-start | bytes 294920 | tf_op jit(solution)/shard_map/ppermute | solution.py:286
  21.1 6.8 %collective-permute-start.8 = (bf16[16,3072]{1,0:T(8,128)(2,1)S(1)}, bf16[16,3072]{1,0:T(8,128)(2,1)S(1)}, u32[]{:S(2)}, u32[]{:S(2)}) collective-permute-start(bf16[16,3072]{1,0:T(8,128)(2,1)S(1)} %chip.1.p0), channel_id=1, source_target_pairs={{0,6},{2,0},{4,2},{6,4},{1,7},{3,1},{5,3},{7,5},{8,14},{10,8},{12,... | collective-permute-start | bytes 294920 | tf_op jit(solution)/shard_map/ppermute | solution.py:286
  28.8 9.4 %collective-permute-start.9 = (bf16[16,2432]{1,0:T(8,128)(2,1)S(1)}, bf16[16,2432]{1,0:T(8,128)(2,1)S(1)}, u32[]{:S(2)}, u32[]{:S(2)}) collective-permute-start(bf16[16,2432]{1,0:T(8,128)(2,1)S(1)} %get-tuple-element.39.refs_0_), channel_id=1, source_target_pairs={{0,38},{2,36},{4,34},{6,32},{32,6},{34,4},{36,2},{38,0},{1,39},{3,... | collective-permute-start | bytes 233480 | tf_op jit(solution)/shard_map/ppermute | solution.py:282
  38.2 6.5 %collective-permute-start.10 = (bf16[32,2432]{1,0:T(8,128)(2,1)S(1)}, bf16[32,2432]{1,0:T(8,128)(2,1)S(1)}, u32[]{:S(2)}, u32[]{:S(2)}) collective-permute-start(bf16[32,2432]{1,0:T(8,128)(2,1)S(1)} %join.2.refs_0_), channel_id=1, source_target_pairs={{0,64},{1,9},{8,72},{9,17},{16,80},{17,25},{24,88},{25,1},{64,128}... | collective-permute-start | bytes 466952 | tf_op jit(solution)/shard_map/ppermute | solution.py:297
  39.8 5.2 %collective-permute-start.11 = (bf16[32,2432]{1,0:T(8,128)(2,1)S(1)}, bf16[32,2432]{1,0:T(8,128)(2,1)S(1)}, u32[]{:S(2)}, u32[]{:S(2)}) collective-permute-start(bf16[32,2432]{1,0:T(8,128)(2,1)S(1)} %join.2.refs_0_), channel_id=1, source_target_pairs={{0,192},{1,25},{8,200},{9,1},{16,208},{17,9},{24,216},{25,17},{64,... | collective-permute-start | bytes 466952 | tf_op jit(solution)/shard_map/ppermute | solution.py:297
  41.5 6.7 %collective-permute-start.12 = (bf16[32,2432]{1,0:T(8,128)(2,1)S(1)}, bf16[32,2432]{1,0:T(8,128)(2,1)S(1)}, u32[]{:S(2)}, u32[]{:S(2)}) collective-permute-start(bf16[32,2432]{1,0:T(8,128)(2,1)S(1)} %join.2.refs_0_), channel_id=1, source_target_pairs={{0,128},{1,17},{8,136},{9,25},{16,144},{17,1},{24,152},{25,9},{64,... | collective-permute-start | bytes 466952 | tf_op jit(solution)/shard_map/ppermute | solution.py:297
  48.3 12.1 %collective-permute-start.13 = (bf16[128,2432]{1,0:T(8,128)(2,1)S(1)}, bf16[128,2432]{1,0:T(8,128)(2,1)S(1)}, u32[]{:S(2)}, u32[]{:S(2)}) collective-permute-start(bf16[128,2432]{1,0:T(8,128)(2,1)S(1)} %join.3.x_ref), channel_id=1, source_target_pairs={{0,16},{1,129},{8,24},{9,137},{16,0},{17,145},{24,8},{25,153},{64,... | collective-permute-start | bytes 1867784 | tf_op jit(solution)/shard_map/ppermute | solution.py:297
  49.2 16.9 %collective-permute-start.15 = (bf16[128,2432]{1,0:T(8,128)(2,1)S(1)}, bf16[128,2432]{1,0:T(8,128)(2,1)S(1)}, u32[]{:S(2)}, u32[]{:S(2)}) collective-permute-start(bf16[128,2432]{1,0:T(8,128)(2,1)S(1)} %join.3.x_ref), channel_id=1, source_target_pairs={{0,8},{1,65},{8,16},{9,73},{16,24},{17,81},{24,0},{25,89},{64,72},... | collective-permute-start | bytes 1867784 | tf_op jit(solution)/shard_map/ppermute | solution.py:297
  50.4 19.0 %collective-permute-start.17 = (bf16[128,2432]{1,0:T(8,128)(2,1)S(1)}, bf16[128,2432]{1,0:T(8,128)(2,1)S(1)}, u32[]{:S(2)}, u32[]{:S(2)}) collective-permute-start(bf16[128,2432]{1,0:T(8,128)(2,1)S(1)} %join.3.x_ref), channel_id=1, source_target_pairs={{0,24},{1,193},{8,0},{9,201},{16,8},{17,209},{24,16},{25,217},{64,... | collective-permute-start | bytes 1867784 | tf_op jit(solution)/shard_map/ppermute | solution.py:297
  62.1 11.5 %collective-permute-start.14 = (bf16[128,2304]{1,0:T(8,128)(2,1)S(1)}, bf16[128,2304]{1,0:T(8,128)(2,1)S(1)}, u32[]{:S(2)}, u32[]{:S(2)}) collective-permute-start(bf16[128,2304]{1,0:T(8,128)(2,1)S(1)} %mlp.5), channel_id=1, source_target_pairs={{0,16},{1,129},{8,24},{9,137},{16,0},{17,145},{24,8},{25,153},{64,... | collective-permute-start | bytes 1769480 | tf_op jit(solution)/shard_map/ppermute | solution.py:297
  67.8 10.4 %collective-permute-start.16 = (bf16[128,2304]{1,0:T(8,128)(2,1)S(1)}, bf16[128,2304]{1,0:T(8,128)(2,1)S(1)}, u32[]{:S(2)}, u32[]{:S(2)}) collective-permute-start(bf16[128,2304]{1,0:T(8,128)(2,1)S(1)} %mlp.6), channel_id=1, source_target_pairs={{0,24},{1,193},{8,0},{9,201},{16,8},{17,209},{24,16},{25,217},{64,... | collective-permute-start | bytes 1769480 | tf_op jit(solution)/shard_map/ppermute | solution.py:297
  71.1 11.1 %collective-permute-start.18 = (bf16[128,2304]{1,0:T(8,128)(2,1)S(1)}, bf16[128,2304]{1,0:T(8,128)(2,1)S(1)}, u32[]{:S(2)}, u32[]{:S(2)}) collective-permute-start(bf16[128,2304]{1,0:T(8,128)(2,1)S(1)} %mlp.7), channel_id=1, source_target_pairs={{0,8},{1,65},{8,16},{9,73},{16,24},{17,81},{24,0},{25,89},{64,72},... | collective-permute-start | bytes 1769480 | tf_op jit(solution)/shard_map/ppermute | solution.py:297
  82.5 5.2 %collective-permute-start.19 = (bf16[32,2304]{1,0:T(8,128)(2,1)S(1)}, bf16[32,2304]{1,0:T(8,128)(2,1)S(1)}, u32[]{:S(2)}, u32[]{:S(2)}) collective-permute-start(bf16[32,2304]{1,0:T(8,128)(2,1)S(1)} %get-tuple-element.53), channel_id=1, source_target_pairs={{0,192},{1,25},{8,200},{9,1},{16,208},{17,9},{24,216},{25,17},{64,... | collective-permute-start | bytes 442376 | tf_op jit(solution)/shard_map/ppermute | solution.py:297
  84.6 7.9 %collective-permute-start.20 = (bf16[32,2304]{1,0:T(8,128)(2,1)S(1)}, bf16[32,2304]{1,0:T(8,128)(2,1)S(1)}, u32[]{:S(2)}, u32[]{:S(2)}) collective-permute-start(bf16[32,2304]{1,0:T(8,128)(2,1)S(1)} %get-tuple-element.55), channel_id=1, source_target_pairs={{0,64},{1,9},{8,72},{9,17},{16,80},{17,25},{24,88},{25,1},{64,128}... | collective-permute-start | bytes 442376 | tf_op jit(solution)/shard_map/ppermute | solution.py:297
  84.6 7.9 %collective-permute-start.21 = (bf16[32,2304]{1,0:T(8,128)(2,1)S(1)}, bf16[32,2304]{1,0:T(8,128)(2,1)S(1)}, u32[]{:S(2)}, u32[]{:S(2)}) collective-permute-start(bf16[32,2304]{1,0:T(8,128)(2,1)S(1)} %get-tuple-element.54), channel_id=1, source_target_pairs={{0,128},{1,17},{8,136},{9,25},{16,144},{17,1},{24,152},{25,9},{64,... | collective-permute-start | bytes 442376 | tf_op jit(solution)/shard_map/ppermute | solution.py:297
  92.6 7.2 %collective-permute-start.22 = (bf16[16,2304]{1,0:T(8,128)(2,1)S(1)}, bf16[16,2304]{1,0:T(8,128)(2,1)S(1)}, u32[]{:S(2)}, u32[]{:S(2)}) collective-permute-start(bf16[16,2304]{1,0:T(8,128)(2,1)S(1)} %slice.45), channel_id=1, source_target_pairs={{0,38},{2,36},{4,34},{6,32},{32,6},{34,4},{36,2},{38,0},{1,39},{3,... | collective-permute-start | bytes 221192 | tf_op jit(solution)/shard_map/ppermute | solution.py:282
  99.8 3.9 %collective-permute-start.23 = (bf16[4,2304]{1,0:T(4,128)(2,1)S(1)}, bf16[4,2304]{1,0:T(4,128)(2,1)S(1)}, u32[]{:S(2)}, u32[]{:S(2)}) collective-permute-start(bf16[4,2304]{1,0:T(4,128)(2,1)S(1)} %get-tuple-element.56), channel_id=1, source_target_pairs={{0,6},{2,0},{4,2},{6,4},{1,7},{3,1},{5,3},{7,5},{8,14},{10,8},{12,... | collective-permute-start | bytes 55304 | tf_op jit(solution)/shard_map/ppermute | solution.py:286
  99.9 4.7 %collective-permute-start.24 = (bf16[4,2304]{1,0:T(4,128)(2,1)S(1)}, bf16[4,2304]{1,0:T(4,128)(2,1)S(1)}, u32[]{:S(2)}, u32[]{:S(2)}) collective-permute-start(bf16[4,2304]{1,0:T(4,128)(2,1)S(1)} %get-tuple-element.58), channel_id=1, source_target_pairs={{0,4},{2,6},{4,0},{6,2},{1,5},{3,7},{5,1},{7,3},{8,12},{10,14},{12... | collective-permute-start | bytes 55304 | tf_op jit(solution)/shard_map/ppermute | solution.py:286
  102.3 5.6 %collective-permute-start.25 = (bf16[4,2304]{1,0:T(4,128)(2,1)S(1)}, bf16[4,2304]{1,0:T(4,128)(2,1)S(1)}, u32[]{:S(2)}, u32[]{:S(2)}) collective-permute-start(bf16[4,2304]{1,0:T(4,128)(2,1)S(1)} %get-tuple-element.57), channel_id=1, source_target_pairs={{0,2},{2,4},{4,6},{6,0},{1,3},{3,5},{5,7},{7,1},{8,10},{10,12},{12... | collective-permute-start | bytes 55304 | tf_op jit(solution)/shard_map/ppermute | solution.py:286
